TPU v7x, 512 devices: a whole 4x8x8 slice. The times are simulated.
512 devices in a mesh: gx: 4 (over z_lo, core), gy: 16 (over z_hi, x), gz: 8 (over y).
Axes of the slice: x: 4, y: 8, z: 8 (z_hi: 4, z_lo: 2; z = z_hi * 2 + z_lo), core: 2. Of those that a mesh axis runs over, the one named last changes fastest.
Arguments:
- body_force: float32 [3, 64, 32, 2048], P(None, 'gz', 'gx', 'gy'), may hold values from -6 to 6
- viscosity: float32 [64, 32, 2048], P('gz', 'gx', 'gy'), may hold values from 0.05 to 0.5
- topography: float32 [256, 16384], P('gx', 'gy'), may hold values from -6 to 6
- kappa: bfloat16 [256, 16384], P('gx', 'gy'), may hold values from 0.019897461 to 0.19921875
Outputs:
- velocity: float32 [3, 64, 32, 2048], P(None, 'gz', 'gx', 'gy')
- surface: float32 [256, 16384], P('gx', ('gy', 'gz'))
All inputs are finite; a program needn't handle non-finite values.
Results may differ from a plain program's by a relative error of at most 0.0008.
Values may be sent and summed in bfloat16 or wider, within the bound.
No kernel may reach another device: no remote copies, remote signals or barrier semaphores. Data moves between devices by JAX's collectives and lax.ppermute only.
A program may use at most 64 MiB of HBM per device.

v0:
```python
import jax
import jax.numpy as jnp
from jax import lax
from jax.sharding import PartitionSpec as P

ITERS = 2
STEPS = 8


drag = 1.0
time_step = 1.0
load_gain = 4.0


def extended_2(cells, sides, width):
    for axis, dim in sides:
        count = lax.axis_size(axis)
        ends = count - 1
        head = lax.slice_in_dim(cells, 0, width, axis=dim)
        tail = lax.slice_in_dim(cells, cells.shape[dim] - width, cells.shape[dim], axis=dim)
        cells = jnp.concatenate(
            [
                lax.ppermute(tail, axis, [(i, (i + 1) % count) for i in range(ends)]),
                cells,
                lax.ppermute(head, axis, [((i + 1) % count, i) for i in range(ends)]),
            ],
            axis=dim,
        )
    return cells


def spread(block, axis, owner):
    block = jnp.where(lax.axis_index(axis) == owner, block, jnp.zeros_like(block))
    return lax.psum(block, axis)


def shifts():
    found = []
    for depth in (-1, 0, 1):
        for across in (-1, 0, 1):
            for along in (-1, 0, 1):
                if depth != 0 or across != 0 or along != 0:
                    found.append((depth, across, along))
    return found


def window(array, depth, across, along):
    inner_depth = array.shape[-3] - 2
    inner_rows = array.shape[-2] - 2
    inner_cols = array.shape[-1] - 2
    return array[
        ...,
        1 + depth : 1 + depth + inner_depth,
        1 + across : 1 + across + inner_rows,
        1 + along : 1 + along + inner_cols,
    ]


def apply_operator(padded, viscous):
    center = window(padded, 0, 0, 0)
    eta_center = window(viscous, 0, 0, 0)
    total = drag * center
    for depth, across, along in shifts():
        weight = 0.5 / (depth * depth + across * across + along * along)
        coupling = weight * (eta_center + window(viscous, depth, across, along))
        total = total + coupling * (center - window(padded, depth, across, along))
    return total


def cell_rim(field):
    return extended_2(field, (("gx", 2), ("gy", 3), ("gz", 1)), 1)


def flux(slope, conduct):
    return conduct * slope / jnp.sqrt(1.0 + slope * slope)


def diffuse_step(extended, conduct):
    along = flux(extended[:, 1:] - extended[:, :-1], 0.5 * (conduct[:, 1:] + conduct[:, :-1]))
    across = flux(extended[1:, :] - extended[:-1, :], 0.5 * (conduct[1:, :] + conduct[:-1, :]))
    change = along[1:-1, 1:] - along[1:-1, :-1] + across[1:, 1:-1] - across[:-1, 1:-1]
    return extended[1:-1, 1:-1] + time_step * change


def squares(residual):
    return lax.psum(jnp.sum(residual * residual), ("gx", "gy", "gz"))


def local(body_force, viscosity, topography, kappa):
    depth_cells = body_force.shape[1]
    row_cells = body_force.shape[2]
    col_cells = body_force.shape[3]
    rows, cols = topography.shape
    row_ratio = rows // row_cells
    col_ratio = cols // col_cells
    is_top = lax.axis_index("gz") == lax.axis_size("gz") - 1
    load = topography.reshape(row_cells, row_ratio, col_cells, col_ratio).mean(axis=(1, 3))
    force = body_force.at[2, depth_cells - 1].add(jnp.where(is_top, -load_gain * load, 0.0))
    viscous = cell_rim(viscosity[None])
    velocity = jnp.zeros_like(force)
    residual = force
    direction = force
    norm_now = squares(residual)
    for step in range(ITERS):
        image = apply_operator(cell_rim(direction), viscous)
        alpha = norm_now / lax.psum(jnp.sum(direction * image), ("gx", "gy", "gz"))
        velocity = velocity + alpha * direction
        if step + 1 < ITERS:
            residual = residual - alpha * image
            norm_next = squares(residual)
            direction = residual + norm_next / norm_now * direction
            norm_now = norm_next
    top = spread(velocity[2, depth_cells - 1], "gz", lax.axis_size("gz") - 1)
    rise = jnp.broadcast_to(
        top[:, None, :, None], (row_cells, row_ratio, col_cells, col_ratio)
    ).reshape(rows, cols)
    reach = 1
    conduct = extended_2(kappa, (("gx", 0), ("gy", 1)), reach).astype(jnp.float32)
    height = topography
    for step in range(STEPS):
        extended = extended_2(height, (("gx", 0), ("gy", 1)), 1)
        height = diffuse_step(extended, conduct)
    surface = height + STEPS * time_step * rise
    share = cols // lax.axis_size("gz")
    surface = lax.dynamic_slice_in_dim(surface, lax.axis_index("gz") * share, share, 1)
    return (velocity, surface)


def solution(mesh):
    in_specs = (P(None, "gz", "gx", "gy"), P("gz", "gx", "gy"), P("gx", "gy"), P("gx", "gy"))
    out_specs = (P(None, "gz", "gx", "gy"), P("gx", ("gy", "gz")))
    return jax.shard_map(local, mesh=mesh, in_specs=in_specs, out_specs=out_specs, check_vma=False)
```

profile of v0, /device:TPU:1, one launch (start us, length us, event | category | flops | bytes accessed | tf_op | source)
XLA Modules:
  0.0 569.1 jit_solution(8678907579575496024)
XLA Ops:
  0.7 4.6 reshape.66
  7.9 8.7 %collective-permute-start.6 = (f32[3,8,1,128]{3,2,1,0:T(1,128)S(1)}, f32[3,8,1,128]{3,2,1,0:T(1,128)S(1)}, u32[]{:S(2)}, u32[]{:S(2)}) collective-permute-start(f32[3,8,1,128]{3,2,1,0:T(1,128)S(1)} %get-tuple-element.106), channel_id=1, source_target_pairs={{128,0},{256,128},{384,256},{129,1},{257,129},{385,257},{130,2},{2... | collective-permute-start | bytes 36872 | tf_op jit(solution)/shard_map/ppermute | solution.py:25
  18.6 3.6 collective-permute-start.22
  24.2 3.6 collective-permute-start.18
  31.3 4.3 collective-permute-start.5
  37.8 4.2 collective-permute-start
  42.1 3.6 collective-permute-start.25
  48.4 4.6 collective-permute-start.2
  55.9 3.6 collective-permute-start.26
  61.1 6.6 %collective-permute-start.29 = (f32[66,1]{1,0:T(8,128)S(1)}, f32[66,1]{1,0:T(8,128)S(1)}, u32[]{:S(2)}, u32[]{:S(2)}) collective-permute-start(f32[66,1]{1,0:T(8,128)S(1)} %get-tuple-element.48), channel_id=1, source_target_pairs={{0,8},{8,16},{16,24},{24,32},{32,40},{40,48},{48,56},{56,64},{64,7... | collective-permute-start | bytes 800 | tf_op jit(solution)/shard_map/ppermute | solution.py:23
  69.2 3.5 collective-permute-done.28
  80.7 6.4 %collective-permute-start.33 = (f32[66,1]{1,0:T(8,128)S(1)}, f32[66,1]{1,0:T(8,128)S(1)}, u32[]{:S(2)}, u32[]{:S(2)}) collective-permute-start(f32[66,1]{1,0:T(8,128)S(1)} %get-tuple-element.46), channel_id=1, source_target_pairs={{0,8},{8,16},{16,24},{24,32},{32,40},{40,48},{48,56},{56,64},{64,7... | collective-permute-start | bytes 800 | tf_op jit(solution)/shard_map/ppermute | solution.py:23
  88.6 3.9 collective-permute-done.32
  95.3 4.6 collective-permute-start.34
  100.7 6.6 %collective-permute-start.37 = (f32[66,1]{1,0:T(8,128)S(1)}, f32[66,1]{1,0:T(8,128)S(1)}, u32[]{:S(2)}, u32[]{:S(2)}) collective-permute-start(f32[66,1]{1,0:T(8,128)S(1)} %get-tuple-element.44), channel_id=1, source_target_pairs={{0,8},{8,16},{16,24},{24,32},{32,40},{40,48},{48,56},{56,64},{64,7... | collective-permute-start | bytes 800 | tf_op jit(solution)/shard_map/ppermute | solution.py:23
  108.7 3.6 collective-permute-done.36
  115.1 5.3 collective-permute-start.38
  121.3 4.6 collective-permute-start.41
  128.5 5.7 %collective-permute-start.7 = (f32[3,8,10,1]{3,2,1,0:T(8,128)S(1)}, f32[3,8,10,1]{3,2,1,0:T(8,128)S(1)}, u32[]{:S(2)}, u32[]{:S(2)}) collective-permute-start(f32[3,8,10,1]{3,2,1,0:T(8,128)S(1)} %get-tuple-element.69), channel_id=1, source_target_pairs={{0,8},{8,16},{16,24},{24,32},{32,40},{40,48},{48,56},{56,64},{64,7... | collective-permute-start | bytes 2888 | tf_op jit(solution)/shard_map/ppermute | solution.py:23
  137.0 4.7 collective-permute-start.42
  142.6 7.8 %collective-permute-start.45 = (f32[66,1]{1,0:T(8,128)S(1)}, f32[66,1]{1,0:T(8,128)S(1)}, u32[]{:S(2)}, u32[]{:S(2)}) collective-permute-start(f32[66,1]{1,0:T(8,128)S(1)} %get-tuple-element.40), channel_id=1, source_target_pairs={{0,8},{8,16},{16,24},{24,32},{32,40},{40,48},{48,56},{56,64},{64,7... | collective-permute-start | bytes 800 | tf_op jit(solution)/shard_map/ppermute | solution.py:23
  159.1 4.7 collective-permute-start.46
  165.9 119.2 %all-reduce = (f32[]{:T(128)}, f32[]{:T(128)}) all-reduce(f32[]{:T(128)} %get-tuple-element.15, f32[]{:T(128)} %get-tuple-element.14), channel_id=1, replica_groups=mesh['gx'=4,'gy'=16,'gz'=8] {'gx','gy','gz'}, use_global_device_ids=true, to_apply=%region_2.3 | all-reduce | flops 2 | bytes 16 | tf_op jit(solution)/shard_map/psum | solution.py:86
  287.1 95.5 %psum.37 = f32[]{:T(128)} all-reduce(f32[]{:T(128)} %multiply_reduce_fusion), channel_id=1, replica_groups=mesh['gx'=4,'gy'=16,'gz'=8] {'gx','gy','gz'}, use_global_device_ids=true, to_apply=%region_6.7 | all-reduce | flops 1 | bytes 8 | tf_op jit(solution)/shard_map/psum | solution.py:86
  392.3 4.0 collective-permute-start.51
  400.9 3.6 collective-permute-start.12
  407.7 4.9 collective-permute-done.52
  414.3 7.3 %collective-permute-start.14 = (f32[3,8,10,1]{3,2,1,0:T(8,128)S(1)}, f32[3,8,10,1]{3,2,1,0:T(8,128)S(1)}, u32[]{:S(2)}, u32[]{:S(2)}) collective-permute-start(f32[3,8,10,1]{3,2,1,0:T(8,128)S(1)} %get-tuple-element.67), channel_id=1, source_target_pairs={{0,8},{8,16},{16,24},{24,32},{32,40},{40,48},{48,56},{56,64},{64,7... | collective-permute-start | bytes 2888 | tf_op jit(solution)/shard_map/ppermute | solution.py:23
  429.2 3.5 collective-permute-done.17
  435.1 113.4 %psum.38 = f32[]{:T(128)} all-reduce(f32[]{:T(128)} %fusion.12), channel_id=1, replica_groups=mesh['gx'=4,'gy'=16,'gz'=8] {'gx','gy','gz'}, use_global_device_ids=true, to_apply=%region_8.9 | all-reduce | flops 1 | bytes 8 | tf_op jit(solution)/shard_map/psum | solution.py:106
  549.9 12.0 %psum.39 = f32[8,128]{1,0:T(8,128)S(1)} all-reduce(f32[8,128]{1,0:T(8,128)S(1)} %fusion.179), channel_id=1, replica_groups=mesh['gx'=4,'gy'=16,'gz'=8] {'gz'}, use_global_device_ids=true, to_apply=%region_9.10 | all-reduce | flops 1024 | bytes 8192 | tf_op jit(solution)/shard_map/psum | solution.py:34
  564.5 4.0 mul.874
  (182 shorter events, 86.4 us)
Async XLA Ops:
  7.9 100.8 %collective-permute-start.6 = (f32[3,8,1,128]{3,2,1,0:T(1,128)S(1)}, f32[3,8,1,128]{3,2,1,0:T(1,128)S(1)}, u32[]{:S(2)}, u32[]{:S(2)}) collective-permute-start(f32[3,8,1,128]{3,2,1,0:T(1,128)S(1)} %get-tuple-element.106), channel_id=1, source_target_pairs={{128,0},{256,128},{384,256},{129,1},{257,129},{385,257},{130,2},{2... | collective-permute-start | bytes 36872 | tf_op jit(solution)/shard_map/ppermute | solution.py:25
  16.6 21.1 %collective-permute-start.23 = (f32[1,1024]{1,0:T(1,128)S(1)}, f32[1,1024]{1,0:T(1,128)S(1)}, u32[]{:S(2)}, u32[]{:S(2)}) collective-permute-start(f32[1,1024]{1,0:T(1,128)S(1)} %get-tuple-element.66), channel_id=1, source_target_pairs={{128,0},{256,128},{384,256},{129,1},{257,129},{385,257},{130,2},{2... | collective-permute-start | bytes 12296 | tf_op jit(solution)/shard_map/ppermute | solution.py:25
  18.6 23.4 %collective-permute-start.22 = (f32[1,1024]{1,0:T(1,128)S(1)}, f32[1,1024]{1,0:T(1,128)S(1)}, u32[]{:S(2)}, u32[]{:S(2)}) collective-permute-start(f32[1,1024]{1,0:T(1,128)S(1)} %get-tuple-element.65), channel_id=1, source_target_pairs={{0,128},{128,256},{256,384},{1,129},{129,257},{257,385},{2,130},{1... | collective-permute-start | bytes 12296 | tf_op jit(solution)/shard_map/ppermute | solution.py:23
  31.3 77.4 %collective-permute-start.5 = (f32[3,8,1,128]{3,2,1,0:T(1,128)S(1)}, f32[3,8,1,128]{3,2,1,0:T(1,128)S(1)}, u32[]{:S(2)}, u32[]{:S(2)}) collective-permute-start(f32[3,8,1,128]{3,2,1,0:T(1,128)S(1)} %get-tuple-element.105), channel_id=1, source_target_pairs={{0,128},{128,256},{256,384},{1,129},{129,257},{257,385},{2,130},{1... | collective-permute-start | bytes 36872 | tf_op jit(solution)/shard_map/ppermute | solution.py:23
  35.6 10.1 %collective-permute-start.1 = (f32[1,8,1,128]{3,2,1,0:T(1,128)S(1)}, f32[1,8,1,128]{3,2,1,0:T(1,128)S(1)}, u32[]{:S(2)}, u32[]{:S(2)}) collective-permute-start(f32[1,8,1,128]{3,2,1,0:T(1,128)S(1)} %get-tuple-element.121), channel_id=1, source_target_pairs={{128,0},{256,128},{384,256},{129,1},{257,129},{385,257},{130,2},{2... | collective-permute-start | bytes 12296 | tf_op jit(solution)/shard_map/ppermute | solution.py:25
  37.8 7.9 %collective-permute-start = (f32[1,8,1,128]{3,2,1,0:T(1,128)S(1)}, f32[1,8,1,128]{3,2,1,0:T(1,128)S(1)}, u32[]{:S(2)}, u32[]{:S(2)}) collective-permute-start(f32[1,8,1,128]{3,2,1,0:T(1,128)S(1)} %get-tuple-element.120), channel_id=1, source_target_pairs={{0,128},{128,256},{256,384},{1,129},{129,257},{257,385},{2,130},{1... | collective-permute-start | bytes 12296 | tf_op jit(solution)/shard_map/ppermute | solution.py:23
  45.8 7.2 %collective-permute-start.24 = (f32[66,1]{1,0:T(8,128)S(1)}, f32[66,1]{1,0:T(8,128)S(1)}, u32[]{:S(2)}, u32[]{:S(2)}) collective-permute-start(f32[66,1]{1,0:T(8,128)S(1)} %get-tuple-element.49), channel_id=1, source_target_pairs={{8,0},{16,8},{24,16},{32,24},{40,32},{48,40},{56,48},{64,56},{72,6... | collective-permute-start | bytes 800 | tf_op jit(solution)/shard_map/ppermute | solution.py:25
  47.1 8.8 %collective-permute-start.3 = (f32[1,8,10,1]{3,2,1,0:T(8,128)S(1)}, f32[1,8,10,1]{3,2,1,0:T(8,128)S(1)}, u32[]{:S(2)}, u32[]{:S(2)}) collective-permute-start(f32[1,8,10,1]{3,2,1,0:T(8,128)S(1)} %get-tuple-element.108), channel_id=1, source_target_pairs={{8,0},{16,8},{24,16},{32,24},{40,32},{48,40},{56,48},{64,56},{72,6... | collective-permute-start | bytes 968 | tf_op jit(solution)/shard_map/ppermute | solution.py:25
  48.4 11.1 %collective-permute-start.2 = (f32[1,8,10,1]{3,2,1,0:T(8,128)S(1)}, f32[1,8,10,1]{3,2,1,0:T(8,128)S(1)}, u32[]{:S(2)}, u32[]{:S(2)}) collective-permute-start(f32[1,8,10,1]{3,2,1,0:T(8,128)S(1)} %get-tuple-element.107), channel_id=1, source_target_pairs={{0,8},{8,16},{16,24},{24,32},{32,40},{40,48},{48,56},{56,64},{64,7... | collective-permute-start | bytes 968 | tf_op jit(solution)/shard_map/ppermute | solution.py:23
  54.0 7.0 %collective-permute-start.27 = (f32[1,1024]{1,0:T(1,128)S(1)}, f32[1,1024]{1,0:T(1,128)S(1)}, u32[]{:S(2)}, u32[]{:S(2)}) collective-permute-start(f32[1,1024]{1,0:T(1,128)S(1)} %get-tuple-element.64), channel_id=1, source_target_pairs={{128,0},{256,128},{384,256},{129,1},{257,129},{385,257},{130,2},{2... | collective-permute-start | bytes 12296 | tf_op jit(solution)/shard_map/ppermute | solution.py:25
  59.7 27.4 %collective-permute-start.4 = (f32[1,1,10,130]{3,2,1,0:T(8,128)S(1)}, f32[1,1,10,130]{3,2,1,0:T(8,128)S(1)}, u32[]{:S(2)}, u32[]{:S(2)}) collective-permute-start(f32[1,1,10,130]{3,2,1,0:T(8,128)S(1)} %get-tuple-element.91), channel_id=1, source_target_pairs={{0,1},{1,2},{2,3},{3,4},{4,5},{5,6},{6,7},{8,9},{9,10},{10,11},{11... | collective-permute-start | bytes 15608 | tf_op jit(solution)/shard_map/ppermute | solution.py:23
  61.1 8.1 %collective-permute-start.29 = (f32[66,1]{1,0:T(8,128)S(1)}, f32[66,1]{1,0:T(8,128)S(1)}, u32[]{:S(2)}, u32[]{:S(2)}) collective-permute-start(f32[66,1]{1,0:T(8,128)S(1)} %get-tuple-element.48), channel_id=1, source_target_pairs={{0,8},{8,16},{16,24},{24,32},{32,40},{40,48},{48,56},{56,64},{64,7... | collective-permute-start | bytes 800 | tf_op jit(solution)/shard_map/ppermute | solution.py:23
  79.2 9.1 %collective-permute-start.10 = (f32[1,1,10,130]{3,2,1,0:T(8,128)S(1)}, f32[1,1,10,130]{3,2,1,0:T(8,128)S(1)}, u32[]{:S(2)}, u32[]{:S(2)}) collective-permute-start(f32[1,1,10,130]{3,2,1,0:T(8,128)S(1)} %get-tuple-element.92), channel_id=1, source_target_pairs={{1,0},{2,1},{3,2},{4,3},{5,4},{6,5},{7,6},{9,8},{10,9},{11,10},{12... | collective-permute-start | bytes 15608 | tf_op jit(solution)/shard_map/ppermute | solution.py:25
  80.7 7.9 %collective-permute-start.33 = (f32[66,1]{1,0:T(8,128)S(1)}, f32[66,1]{1,0:T(8,128)S(1)}, u32[]{:S(2)}, u32[]{:S(2)}) collective-permute-start(f32[66,1]{1,0:T(8,128)S(1)} %get-tuple-element.46), channel_id=1, source_target_pairs={{0,8},{8,16},{16,24},{24,32},{32,40},{40,48},{48,56},{56,64},{64,7... | collective-permute-start | bytes 800 | tf_op jit(solution)/shard_map/ppermute | solution.py:23
  100.7 8.0 %collective-permute-start.37 = (f32[66,1]{1,0:T(8,128)S(1)}, f32[66,1]{1,0:T(8,128)S(1)}, u32[]{:S(2)}, u32[]{:S(2)}) collective-permute-start(f32[66,1]{1,0:T(8,128)S(1)} %get-tuple-element.44), channel_id=1, source_target_pairs={{0,8},{8,16},{16,24},{24,32},{32,40},{40,48},{48,56},{56,64},{64,7... | collective-permute-start | bytes 800 | tf_op jit(solution)/shard_map/ppermute | solution.py:23
  113.1 8.0 %collective-permute-start.39 = (f32[1,1024]{1,0:T(1,128)S(1)}, f32[1,1024]{1,0:T(1,128)S(1)}, u32[]{:S(2)}, u32[]{:S(2)}) collective-permute-start(f32[1,1024]{1,0:T(1,128)S(1)} %get-tuple-element.58), channel_id=1, source_target_pairs={{128,0},{256,128},{384,256},{129,1},{257,129},{385,257},{130,2},{2... | collective-permute-start | bytes 12296 | tf_op jit(solution)/shard_map/ppermute | solution.py:25
  121.3 13.0 %collective-permute-start.41 = (f32[66,1]{1,0:T(8,128)S(1)}, f32[66,1]{1,0:T(8,128)S(1)}, u32[]{:S(2)}, u32[]{:S(2)}) collective-permute-start(f32[66,1]{1,0:T(8,128)S(1)} %get-tuple-element.42), channel_id=1, source_target_pairs={{0,8},{8,16},{16,24},{24,32},{32,40},{40,48},{48,56},{56,64},{64,7... | collective-permute-start | bytes 800 | tf_op jit(solution)/shard_map/ppermute | solution.py:23
  125.9 8.3 %collective-permute-start.40 = (f32[66,1]{1,0:T(8,128)S(1)}, f32[66,1]{1,0:T(8,128)S(1)}, u32[]{:S(2)}, u32[]{:S(2)}) collective-permute-start(f32[66,1]{1,0:T(8,128)S(1)} %get-tuple-element.41), channel_id=1, source_target_pairs={{8,0},{16,8},{24,16},{32,24},{40,32},{48,40},{56,48},{64,56},{72,6... | collective-permute-start | bytes 800 | tf_op jit(solution)/shard_map/ppermute | solution.py:25
  127.2 14.5 %collective-permute-start.8 = (f32[3,8,10,1]{3,2,1,0:T(8,128)}, f32[3,8,10,1]{3,2,1,0:T(8,128)S(1)}, u32[]{:S(2)}, u32[]{:S(2)}) collective-permute-start(f32[3,8,10,1]{3,2,1,0:T(8,128)} %get-tuple-element.70), channel_id=1, source_target_pairs={{8,0},{16,8},{24,16},{32,24},{40,32},{48,40},{56,48},{64,56},{72,6... | collective-permute-start | bytes 2888 | tf_op jit(solution)/shard_map/ppermute | solution.py:25
  128.5 13.2 %collective-permute-start.7 = (f32[3,8,10,1]{3,2,1,0:T(8,128)S(1)}, f32[3,8,10,1]{3,2,1,0:T(8,128)S(1)}, u32[]{:S(2)}, u32[]{:S(2)}) collective-permute-start(f32[3,8,10,1]{3,2,1,0:T(8,128)S(1)} %get-tuple-element.69), channel_id=1, source_target_pairs={{0,8},{8,16},{16,24},{24,32},{32,40},{40,48},{48,56},{56,64},{64,7... | collective-permute-start | bytes 2888 | tf_op jit(solution)/shard_map/ppermute | solution.py:23
  135.1 6.8 %collective-permute-start.43 = (f32[1,1024]{1,0:T(1,128)S(1)}, f32[1,1024]{1,0:T(1,128)S(1)}, u32[]{:S(2)}, u32[]{:S(2)}) collective-permute-start(f32[1,1024]{1,0:T(1,128)S(1)} %get-tuple-element.56), channel_id=1, source_target_pairs={{128,0},{256,128},{384,256},{129,1},{257,129},{385,257},{130,2},{2... | collective-permute-start | bytes 12296 | tf_op jit(solution)/shard_map/ppermute | solution.py:25
  142.6 13.7 %collective-permute-start.45 = (f32[66,1]{1,0:T(8,128)S(1)}, f32[66,1]{1,0:T(8,128)S(1)}, u32[]{:S(2)}, u32[]{:S(2)}) collective-permute-start(f32[66,1]{1,0:T(8,128)S(1)} %get-tuple-element.40), channel_id=1, source_target_pairs={{0,8},{8,16},{16,24},{24,32},{32,40},{40,48},{48,56},{56,64},{64,7... | collective-permute-start | bytes 800 | tf_op jit(solution)/shard_map/ppermute | solution.py:23
  151.7 12.1 %collective-permute-start.9 = (f32[3,1,10,130]{3,2,1,0:T(8,128)S(1)}, f32[3,1,10,130]{3,2,1,0:T(8,128)S(1)}, u32[]{:S(2)}, u32[]{:S(2)}) collective-permute-start(f32[3,1,10,130]{3,2,1,0:T(8,128)S(1)} %get-tuple-element.29), channel_id=1, source_target_pairs={{0,1},{1,2},{2,3},{3,4},{4,5},{5,6},{6,7},{8,9},{9,10},{10,11},{11... | collective-permute-start | bytes 46808 | tf_op jit(solution)/shard_map/ppermute | solution.py:23
  155.0 8.8 %collective-permute-start.11 = (f32[3,1,10,130]{3,2,1,0:T(8,128)S(1)}, f32[3,1,10,130]{3,2,1,0:T(8,128)S(1)}, u32[]{:S(2)}, u32[]{:S(2)}) collective-permute-start(f32[3,1,10,130]{3,2,1,0:T(8,128)S(1)} %get-tuple-element.30), channel_id=1, source_target_pairs={{1,0},{2,1},{3,2},{4,3},{5,4},{6,5},{7,6},{9,8},{10,9},{11,10},{12... | collective-permute-start | bytes 46808 | tf_op jit(solution)/shard_map/ppermute | solution.py:25
  157.1 226.7 %collective-permute-start.47 = (f32[1,1024]{1,0:T(1,128)S(1)}, f32[1,1024]{1,0:T(1,128)S(1)}, u32[]{:S(2)}, u32[]{:S(2)}) collective-permute-start(f32[1,1024]{1,0:T(1,128)S(1)} %get-tuple-element.54), channel_id=1, source_target_pairs={{128,0},{256,128},{384,256},{129,1},{257,129},{385,257},{130,2},{2... | collective-permute-start | bytes 12296 | tf_op jit(solution)/shard_map/ppermute | solution.py:25
  159.1 224.8 %collective-permute-start.46 = (f32[1,1024]{1,0:T(1,128)S(1)}, f32[1,1024]{1,0:T(1,128)S(1)}, u32[]{:S(2)}, u32[]{:S(2)}) collective-permute-start(f32[1,1024]{1,0:T(1,128)S(1)} %get-tuple-element.53), channel_id=1, source_target_pairs={{0,128},{128,256},{256,384},{1,129},{129,257},{257,385},{2,130},{1... | collective-permute-start | bytes 12296 | tf_op jit(solution)/shard_map/ppermute | solution.py:23
  392.3 12.3 %collective-permute-start.51 = (f32[1,1024]{1,0:T(1,128)S(1)}, f32[1,1024]{1,0:T(1,128)S(1)}, u32[]{:S(2)}, u32[]{:S(2)}) collective-permute-start(f32[1,1024]{1,0:T(1,128)S(1)} %get-tuple-element.52), channel_id=1, source_target_pairs={{128,0},{256,128},{384,256},{129,1},{257,129},{385,257},{130,2},{2... | collective-permute-start | bytes 12296 | tf_op jit(solution)/shard_map/ppermute | solution.py:25
  396.3 8.3 %collective-permute-start.50 = (f32[1,1024]{1,0:T(1,128)S(1)}, f32[1,1024]{1,0:T(1,128)S(1)}, u32[]{:S(2)}, u32[]{:S(2)}) collective-permute-start(f32[1,1024]{1,0:T(1,128)S(1)} %get-tuple-element.51), channel_id=1, source_target_pairs={{0,128},{128,256},{256,384},{1,129},{129,257},{257,385},{2,130},{1... | collective-permute-start | bytes 12296 | tf_op jit(solution)/shard_map/ppermute | solution.py:23
  399.0 13.8 %collective-permute-start.13 = (f32[3,8,1,128]{3,2,1,0:T(1,128)S(1)}, f32[3,8,1,128]{3,2,1,0:T(1,128)S(1)}, u32[]{:S(2)}, u32[]{:S(2)}) collective-permute-start(f32[3,8,1,128]{3,2,1,0:T(1,128)S(1)} %get-tuple-element.104), channel_id=1, source_target_pairs={{128,0},{256,128},{384,256},{129,1},{257,129},{385,257},{130,2},{2... | collective-permute-start | bytes 36872 | tf_op jit(solution)/shard_map/ppermute | solution.py:25
  400.9 11.9 %collective-permute-start.12 = (f32[3,8,1,128]{3,2,1,0:T(1,128)S(1)}, f32[3,8,1,128]{3,2,1,0:T(1,128)S(1)}, u32[]{:S(2)}, u32[]{:S(2)}) collective-permute-start(f32[3,8,1,128]{3,2,1,0:T(1,128)S(1)} %get-tuple-element.103), channel_id=1, source_target_pairs={{0,128},{128,256},{256,384},{1,129},{129,257},{257,385},{2,130},{1... | collective-permute-start | bytes 36872 | tf_op jit(solution)/shard_map/ppermute | solution.py:23
  413.0 12.0 %collective-permute-start.15 = (f32[3,8,10,1]{3,2,1,0:T(8,128)S(1)}, f32[3,8,10,1]{3,2,1,0:T(8,128)S(1)}, u32[]{:S(2)}, u32[]{:S(2)}) collective-permute-start(f32[3,8,10,1]{3,2,1,0:T(8,128)S(1)} %get-tuple-element.68), channel_id=1, source_target_pairs={{8,0},{16,8},{24,16},{32,24},{40,32},{48,40},{56,48},{64,56},{72,6... | collective-permute-start | bytes 2888 | tf_op jit(solution)/shard_map/ppermute | solution.py:25
  414.3 11.6 %collective-permute-start.14 = (f32[3,8,10,1]{3,2,1,0:T(8,128)S(1)}, f32[3,8,10,1]{3,2,1,0:T(8,128)S(1)}, u32[]{:S(2)}, u32[]{:S(2)}) collective-permute-start(f32[3,8,10,1]{3,2,1,0:T(8,128)S(1)} %get-tuple-element.67), channel_id=1, source_target_pairs={{0,8},{8,16},{16,24},{24,32},{32,40},{40,48},{48,56},{56,64},{64,7... | collective-permute-start | bytes 2888 | tf_op jit(solution)/shard_map/ppermute | solution.py:23
  (27 other events, 201.8 us)
where the time goes:
time: 574 us; the launch traced here: 569 us
  blocking collectives  340 us (59%)
  starting transfers between devices  165 us (29%)
  waiting for transfers between devices  29 us (5%)
  local copies, waits for them, and re-layouts  14.9 us (3%)
  other arithmetic  13.8 us (2%)
  between operations  5.99 us (1%)
    psum x2, blocking collectives, squares(): return lax.psum(jnp.sum(residual * residual), ('gx', 'gy', 'gz'))  215 us
    ppermute x27, starting transfers between devices, extended_2(): lax.ppermute(tail, axis, [(i, (i + 1) % count) for i in range(ends)])  114 us
    psum x1, blocking collectives, local(): alpha = norm_now / lax.psum(jnp.sum(direction * image), ('gx', 'gy', 'gz'))  113 us
    ppermute x27, starting transfers between devices, extended_2(): lax.ppermute(head, axis, [((i + 1) % count, i) for i in range(ends)])  51.6 us
    ppermute x27, waiting for transfers between devices, extended_2(): lax.ppermute(head, axis, [((i + 1) % count, i) for i in range(ends)])  26.2 us
    psum x1, blocking collectives, spread(): return lax.psum(block, axis)  12 us
  transfers between devices with their start and end apart: 54, of which 11 were waited for; matrix products, arithmetic and copies ran while one was open for 2% of the time, Pallas kernels for 0%

commit v1 on v0

v1 whole, which is shorter than its diff:
```python
import jax
import jax.numpy as jnp
from jax import lax
from jax.experimental import pallas as pl
from jax.experimental.pallas import tpu as pltpu
from jax.sharding import PartitionSpec as P

STEPS = 8
DRAG = 1.0
TIME_STEP = 1.0
LOAD_GAIN = 4.0
FACE, EDGE, CORNER = 0.5, 0.25, 0.5 / 3.0
TOTAL = 6 * FACE + 12 * EDGE + 8 * CORNER

DEPTHS = 12
PLANES = 4 * DEPTHS
PAIRS_ROW = 2 * PLANES
SURFACE_ROW = PAIRS_ROW + 8
GX_ROWS = SURFACE_ROW + 32

f32 = jnp.float32


def vmem():
    return pl.BlockSpec(memory_space=pltpu.VMEM)


def call(body, outs, ins, scratch=(), cost=20000):
    return pl.pallas_call(
        body,
        out_shape=[jax.ShapeDtypeStruct(s, f32) for s in outs],
        in_specs=[vmem() for _ in ins],
        out_specs=[vmem() for _ in outs],
        scratch_shapes=list(scratch),
        cost_estimate=pl.CostEstimate(flops=cost * 1024, bytes_accessed=1 << 18, transcendentals=0),
    )(*ins)


def lanes(shape):
    return lax.broadcasted_iota(jnp.int32, shape, len(shape) - 1)


def rolled(x, amount, axis=1):
    amount = amount % x.shape[axis]
    return x if amount == 0 else pltpu.roll(x, amount, axis)


def surface_own(topo_ref, kappa_ref, load_ref, height_ref, conduct_ref, left_ref, right_ref):
    g = lax.axis_index("gz")
    last = lax.axis_size("gz") - 1
    lane = lanes((8, 128))
    pieces = []
    for v in range(8):
        piece = topo_ref[:, 128 * v : 128 * v + 128].reshape(8, 8, 128)
        pieces.append(jnp.sum(piece, axis=1))
    stacked = jnp.concatenate(pieces, axis=0)
    pick = (
        lax.broadcasted_iota(jnp.int32, (128, 128), 0) // 8 == lax.broadcasted_iota(jnp.int32, (128, 128), 1)
    ).astype(f32)
    sums = jnp.dot(stacked, pick, precision=lax.Precision.HIGHEST, preferred_element_type=f32)
    load = jnp.zeros((8, 128), f32)
    for v in range(8):
        load = load + rolled(sums[8 * v : 8 * v + 8], 16 * v)
    load_ref[...] = jnp.where(g == last, load * (-LOAD_GAIN / 64.0), 0.0)
    wide = lanes((64, 128))
    own = pl.ds(pl.multiple_of(g * 128, 128), 128)
    before = pl.ds(pl.multiple_of(jnp.maximum(g - 1, 0) * 128, 128), 128)
    after = pl.ds(pl.multiple_of(jnp.minimum(g + 1, last) * 128, 128), 128)
    for source, target in ((topo_ref, height_ref), (kappa_ref, conduct_ref)):
        target[:, 0:128] = source[:, own].astype(f32)
        side = jnp.where((wide < 8) & (g < last), source[:, after].astype(f32), 0.0)
        side = jnp.where((wide >= 120) & (g > 0), source[:, before].astype(f32), side)
        target[:, 128:256] = side
    width = topo_ref.shape[1]
    left = jnp.zeros((8, 128), f32)
    right = jnp.zeros((8, 128), f32)
    slot = 0
    for source in (topo_ref, kappa_ref):
        head = source[:, 0:128].astype(f32)
        tail = source[:, width - 128 : width].astype(f32)
        for r in range(8):
            mask = lane // 8 == slot
            left = jnp.where(mask, rolled(head[8 * r : 8 * r + 8], 8 * slot), left)
            right = jnp.where(mask, rolled(tail[8 * r : 8 * r + 8], 8 * slot - 120), right)
            slot += 1
    left_ref[...] = left
    right_ref[...] = right


def assemble(force_ref, visc_ref, load_ref, low_ref, high_ref, sl_ref, sr_ref, planes_ref, left_ref, right_ref):
    lane = lanes((8, 128))
    left = jnp.zeros((8, 128), f32)
    right = jnp.zeros((8, 128), f32)
    for field in range(4):
        for depth in range(DEPTHS):
            if depth < 2:
                plane = low_ref[2 * field + depth]
            elif depth >= DEPTHS - 2:
                plane = high_ref[2 * field + depth - (DEPTHS - 2)]
            elif field == 3:
                plane = visc_ref[depth - 2]
            else:
                plane = force_ref[field, depth - 2]
                if field == 2 and depth == DEPTHS - 3:
                    plane = plane + load_ref[...]
            p = field * DEPTHS + depth
            planes_ref[p] = plane
            mask = lane // 2 == p
            left = jnp.where(mask, rolled(plane, 2 * p), left)
            right = jnp.where(mask, rolled(plane, 2 * p - 126), right)
    left_ref[0] = left
    right_ref[0] = right
    left_ref[1] = sl_ref[...]
    right_ref[1] = sr_ref[...]


def prepare_rows(planes_ref, rl_ref, rr_ref, height_ref, conduct_ref, down_ref, up_ref, height_out, conduct_out):
    g = lax.axis_index("gz")
    last = lax.axis_size("gz") - 1
    lane = lanes((8, 128))
    for p in range(PLANES):
        down_ref[2 * p : 2 * p + 2, :] = planes_ref[p, 6:8, :]
        up_ref[2 * p : 2 * p + 2, :] = planes_ref[p, 0:2, :]
    down_ref[PAIRS_ROW : PAIRS_ROW + 4, :] = jnp.concatenate([rl_ref[0, 6:8, :], rr_ref[0, 6:8, :]], axis=0)
    up_ref[PAIRS_ROW : PAIRS_ROW + 4, :] = jnp.concatenate([rl_ref[0, 0:2, :], rr_ref[0, 0:2, :]], axis=0)
    down_ref[PAIRS_ROW + 4 : SURFACE_ROW, :] = jnp.zeros((4, 128), f32)
    up_ref[PAIRS_ROW + 4 : SURFACE_ROW, :] = jnp.zeros((4, 128), f32)
    slot = 0
    for index, (source, target) in enumerate(((height_ref, height_out), (conduct_ref, conduct_out))):
        base = SURFACE_ROW + 16 * index
        for r in range(8):
            rows = slice(8 * r, 8 * r + 8)
            main = source[rows, 0:128]
            side = source[rows, 128:256]
            side = jnp.where((g == 0) & (lane >= 120), rolled(rl_ref[1], 120 - 8 * slot), side)
            side = jnp.where((g == last) & (lane < 8), rolled(rr_ref[1], -8 * slot), side)
            target[rows, 0:128] = main
            target[rows, 128:256] = side
            if r == 0:
                up_ref[base : base + 8, :] = main
                up_ref[base + 8 : base + 16, :] = side
            if r == 7:
                down_ref[base : base + 8, :] = main
                down_ref[base + 8 : base + 16, :] = side
            slot += 1


def stencil(before, here, after):
    outer = before + after
    a = FACE * here + EDGE * outer
    b = EDGE * here + CORNER * outer
    both = a + rolled(b, 1, 0) + rolled(b, 15, 0)
    rows = rolled(a, 1, 0) + rolled(a, 15, 0)
    return FACE * outer + rows + rolled(both, 1, 1) + rolled(both, 255, 1)


def operate(planes_ref, rl_ref, rr_ref, before_ref, after_ref, image_ref, sums_ref, top_ref, x, w, diag):
    lane = lanes((8, 128))
    row = lax.broadcasted_iota(jnp.int32, (8, 128), 0)
    pad = jnp.zeros((4, 128), f32)
    lower_l = jnp.concatenate([after_ref[PAIRS_ROW : PAIRS_ROW + 2, :], pad, before_ref[PAIRS_ROW : PAIRS_ROW + 2, :]], 0)
    lower_r = jnp.concatenate(
        [after_ref[PAIRS_ROW + 2 : PAIRS_ROW + 4, :], pad, before_ref[PAIRS_ROW + 2 : PAIRS_ROW + 4, :]], 0
    )
    for p in range(PLANES):
        x[p, 0:8, 0:128] = planes_ref[p]
        x[p, 8:16, 0:128] = jnp.concatenate(
            [after_ref[2 * p : 2 * p + 2, :], pad, before_ref[2 * p : 2 * p + 2, :]], 0
        )
        for start, l, r in ((0, rl_ref[0], rr_ref[0]), (8, lower_l, lower_r)):
            side = jnp.where(lane < 2, rolled(r, -2 * p), 0.0)
            side = jnp.where(lane >= 126, rolled(l, 126 - 2 * p), side)
            x[p, start : start + 8, 128:256] = side
    for depth in range(1, DEPTHS - 1):
        e = [x[3 * DEPTHS + depth + i] for i in (-1, 0, 1)]
        d = (DRAG + TOTAL * e[1]) + stencil(*e)
        diag[depth] = d[0:8, 0:128]
        inside = e[1] > 0.0
        for c in range(3):
            v = [x[c * DEPTHS + depth + i] for i in (-1, 0, 1)]
            ev = [e[i] * v[i] for i in range(3)]
            out = v[1] * d - e[1] * stencil(*v) - stencil(*ev)
            w[c * DEPTHS + depth] = jnp.where(inside, out, 0.0)
    m = [jnp.zeros((8, 128), f32) for _ in range(4)]
    for depth in range(2, DEPTHS - 2):
        e = x[3 * DEPTHS + depth, 0:8, 0:128]
        d = diag[depth]
        for c in range(3):
            p = c * DEPTHS + depth
            s = stencil(w[p - 1], w[p], w[p + 1])[0:8, 0:128]
            v = x[p, 0:8, 0:128]
            q = w[p, 0:8, 0:128]
            image_ref[c, depth - 2] = q
            m[0] = m[0] + v * v
            m[1] = m[1] + v * q
            m[2] = m[2] + q * q
            m[3] = m[3] + q * (q * d - 2.0 * (e * s))
    total = jnp.zeros((8, 128), f32)
    for k in range(4):
        total = jnp.where(lane == k, jnp.sum(m[k]), total)
    for i in range(sums_ref.shape[0] // 8):
        sums_ref[8 * i : 8 * i + 8, :] = total
    p = 2 * DEPTHS + DEPTHS - 3
    top_ref[0] = x[p, 0:8, 0:128]
    top_ref[1] = w[p, 0:8, 0:128]


def diffuse(height_ref, conduct_ref, before_ref, after_ref, out_ref):
    def extended(source, base):
        def joined(ref):
            return jnp.concatenate([ref[base : base + 8, :], ref[base + 8 : base + 16, :]], axis=1)

        return jnp.concatenate([source[...], joined(after_ref), joined(before_ref)], axis=0)

    h = extended(height_ref, SURFACE_ROW)
    k = extended(conduct_ref, SURFACE_ROW + 16)
    inside = k > 0.0
    along = 0.5 * (k + rolled(k, 255, 1))
    across = 0.5 * (k + rolled(k, 79, 0))
    for step in range(STEPS):
        s = rolled(h, 255, 1) - h
        q = along * s * lax.rsqrt(1.0 + s * s)
        t = rolled(h, 79, 0) - h
        r = across * t * lax.rsqrt(1.0 + t * t)
        change = (q - rolled(q, 1, 1)) + (r - rolled(r, 1, 0))
        h = jnp.where(inside, h + TIME_STEP * change, 0.0)
    out_ref[...] = h[0:64, 0:128]


def middle(sums_ref, top_ref, out_ref):
    lane = lanes((8, 128))
    part = jnp.sum(sums_ref[...], axis=0, keepdims=True)
    base = jnp.broadcast_to(rolled(part, 32), (8, 128))
    base = jnp.where((lane >= 32) & (lane < 36), base, 0.0)
    for j in range(out_ref.shape[0]):
        piece = jnp.where(lane < 16, rolled(top_ref[0], -16 * j), base)
        out_ref[j] = jnp.where(lane // 16 == 1, rolled(top_ref[1], 16 - 16 * j), piece)


def finish(parts_ref, planes_ref, image_ref, height_ref, velocity_ref, surface_ref):
    count = parts_ref.shape[0]
    lane = lanes((1, 128))
    total = parts_ref[0, 0:1, :]
    for j in range(1, count):
        total = total + parts_ref[j, 0:1, :]

    def moment(k):
        return jnp.sum(jnp.where(lane == 32 + k, total, 0.0), axis=1, keepdims=True)

    m0, m1, m2, m3 = (moment(k) for k in range(4))
    first = m0 / m1
    later = first * first * m2 - m0
    gain = 1.0 + later / m0
    second = later / (gain * gain * m1 - 2.0 * first * gain * m2 + first * first * m3)
    on_force = first + second * gain
    on_image = -(second * first)
    for c in range(3):
        for depth in range(8):
            velocity_ref[c, depth] = on_force * planes_ref[c * DEPTHS + depth + 2] + on_image * image_ref[c, depth]
    top = parts_ref[count - 1]
    rise = on_force * top + on_image * rolled(top, -16)
    spread = (
        lax.broadcasted_iota(jnp.int32, (128, 128), 1) // 8 == lax.broadcasted_iota(jnp.int32, (128, 128), 0)
    ).astype(f32)
    rise = jnp.where(lanes((8, 128)) < 16, rise, 0.0)
    wide = (STEPS * TIME_STEP) * jnp.dot(rise, spread, precision=lax.Precision.HIGHEST, preferred_element_type=f32)
    for r in range(8):
        rows = slice(8 * r, 8 * r + 8)
        surface_ref[rows, :] = height_ref[rows, :] + jnp.broadcast_to(wide[r : r + 1, :], (8, 128))


def shift(value, axis):
    ends = lax.axis_size(axis) - 1
    return value, [(i, i + 1) for i in range(ends)], [(i + 1, i) for i in range(ends)]


def exchange(to_next, to_before, axis):
    ends = lax.axis_size(axis) - 1
    from_before = lax.ppermute(to_next, axis, [(i, i + 1) for i in range(ends)])
    from_after = lax.ppermute(to_before, axis, [(i + 1, i) for i in range(ends)])
    return from_before, from_after


def local(body_force, viscosity, topography, kappa):
    depth = viscosity.shape[0]

    def layers(start):
        fields = [body_force[c, start : start + 2] for c in range(3)] + [viscosity[start : start + 2]]
        return jnp.concatenate(fields, axis=0)

    low, high = exchange(layers(depth - 2), layers(0), "gz")
    load, height, conduct, left, right = call(
        surface_own,
        [(8, 128), (64, 256), (64, 256), (8, 128), (8, 128)],
        (topography, kappa),
    )
    planes, left, right = call(
        assemble,
        [(PLANES, 8, 128), (2, 8, 128), (2, 8, 128)],
        (body_force, viscosity, load, low, high, left, right),
    )
    from_left, from_right = exchange(right, left, "gy")
    down, up, height, conduct = call(
        prepare_rows,
        [(GX_ROWS, 128), (GX_ROWS, 128), (64, 256), (64, 256)],
        (planes, from_left, from_right, height, conduct),
    )
    before, after = exchange(down, up, "gx")
    group = lax.axis_size("gx") * lax.axis_size("gy")
    image, sums, top = call(
        operate,
        [(3, 8, 8, 128), (group, 128), (2, 8, 128)],
        (planes, from_left, from_right, before, after),
        [
            pltpu.VMEM((PLANES, 16, 256), f32),
            pltpu.VMEM((3 * DEPTHS, 16, 256), f32),
            pltpu.VMEM((DEPTHS, 8, 128), f32),
        ],
    )
    sums = lax.all_to_all(sums.reshape(group, 1, 128), ("gx", "gy"), 0, 0)
    (height,) = call(diffuse, [(64, 128)], (height, conduct, before, after))
    (parts,) = call(middle, [(lax.axis_size("gz"), 8, 128)], (sums.reshape(group, 128), top))
    parts = lax.all_to_all(parts, "gz", 0, 0)
    velocity, surface = call(
        finish, [(3, 8, 8, 128), (64, 128)], (parts, planes, image, height)
    )
    return velocity, surface


def solution(mesh):
    in_specs = (P(None, "gz", "gx", "gy"), P("gz", "gx", "gy"), P("gx", "gy"), P("gx", "gy"))
    out_specs = (P(None, "gz", "gx", "gy"), P("gx", ("gy", "gz")))
    return jax.shard_map(local, mesh=mesh, in_specs=in_specs, out_specs=out_specs, check_vma=False)
```

time: 574 us -> 84.6 us (0.15)
  blocking collectives: 340 us -> 25.6 us
  starting transfers between devices: 165 us -> 26.1 us
  waiting for transfers between devices: 29 us -> 12.6 us
  Pallas kernels: 0 us -> 14.9 us
  other arithmetic: 13.8 us -> 0.01 us
  local copies, waits for them, and re-layouts: 14.9 us -> 3.96 us
    psum x4 -> x0, blocking collectives: 340 us -> none  [the longest x2 215 us: squares(): return lax.psum(jnp.sum(residual * residual), ('gx', 'gy', 'gz'))]
    ppermute x54 -> x6, starting transfers between devices: 165 us -> 19 us  [the longest x3 14.5 us: exchange(): from_before = lax.ppermute(to_next, axis, [(i, i + 1) for i in range(ends)])]
    all_to_all x0 -> x1, blocking collectives: none -> 25.6 us  [local(): sums = lax.all_to_all(sums.reshape(group, 1, 128), ('gx', 'gy'), 0, 0)]
    ppermute x54 -> x6, waiting for transfers between devices: 29 us -> 8.63 us  [the longest x3 8.62 us: exchange(): lax.ppermute(to_before, axis, [(i + 1, i) for i in range(ends)])]
    pallas_call x0 -> x7, Pallas kernels: none -> 14.9 us  [call(): pl.pallas_call(body, out_shape=[jax.ShapeDtypeStruct(s, f32) for s in out...]
    all_to_all x0 -> x1, starting transfers between devices: none -> 7.02 us  [local(): parts = lax.all_to_all(parts, 'gz', 0, 0)]
    reduce_sum x4 -> x0, other arithmetic: 6.06 us -> none  [the longest x2 2.89 us: local(): alpha = norm_now / lax.psum(jnp.sum(direction * image), ('gx', 'gy', 'gz'))]
  transfers between devices with their start and end apart: 54 -> 7, of which waited for: 11 -> 4; matrix products, arithmetic and copies ran while one was open for 2% -> 0% of each run, Pallas kernels for 0% -> 6%
where the time goes in v1:
time: 84.6 us; the launch traced here: 83.9 us
  starting transfers between devices  26.1 us (31%)
  blocking collectives  25.6 us (30%)
  Pallas kernels  14.9 us (18%)
  waiting for transfers between devices  12.6 us (15%)
  local copies, waits for them, and re-layouts  3.96 us (5%)
    all_to_all x1, blocking collectives, local(): sums = lax.all_to_all(sums.reshape(group, 1, 128), ('gx', 'gy'), 0, 0)  25.6 us
    pallas_call x7, Pallas kernels, call(): pl.pallas_call(body, out_shape=[jax.ShapeDtypeStruct(s, f32) for s in out...  14.9 us
    ppermute x3, starting transfers between devices, exchange(): from_before = lax.ppermute(to_next, axis, [(i, i + 1) for i in range(ends)])  14.5 us
    ppermute x3, waiting for transfers between devices, exchange(): lax.ppermute(to_before, axis, [(i + 1, i) for i in range(ends)])  8.62 us
    all_to_all x1, starting transfers between devices, local(): parts = lax.all_to_all(parts, 'gz', 0, 0)  7.02 us
    ppermute x3, starting transfers between devices, exchange(): lax.ppermute(to_before, axis, [(i + 1, i) for i in range(ends)])  4.5 us
    all_to_all x1, waiting for transfers between devices, local(): parts = lax.all_to_all(parts, 'gz', 0, 0)  3.98 us
    unnamed x14, local copies, waits for them, and re-layouts  2.45 us
  transfers between devices with their start and end apart: 7, of which 4 were waited for; matrix products, arithmetic and copies ran while one was open for 0% of the time, Pallas kernels for 6%

profile of v1, /device:TPU:1, one launch (start us, length us, event | category | flops | bytes accessed | tf_op | source)
XLA Modules:
  0.0 83.9 jit_solution(16554480397082359960)
XLA Ops:
  0.6 0.7 fusion
  1.3 0.8 slice_bitcast_fusion.2
  2.1 4.0 %collective-permute-start = (f32[8,8,128]{2,1,0:T(8,128)S(1)}, f32[8,8,128]{2,1,0:T(8,128)S(1)}, u32[]{:S(2)}, u32[]{:S(2)}) collective-permute-start(f32[8,8,128]{2,1,0:T(8,128)S(1)} %pad_maximum_fusion), channel_id=1, source_target_pairs={{0,1},{1,2},{2,3},{3,4},{4,5},{5,6},{6,7},{8,9},{9,10},{10,11},{11... | collective-permute-start | bytes 98312 | tf_op jit(solution)/shard_map/ppermute | solution.py:279
  6.2 1.3 %collective-permute-start.1 = (f32[8,8,128]{2,1,0:T(8,128)S(1)}, f32[8,8,128]{2,1,0:T(8,128)S(1)}, u32[]{:S(2)}, u32[]{:S(2)}) collective-permute-start(f32[8,8,128]{2,1,0:T(8,128)S(1)} %pad_maximum_fusion.1), channel_id=1, source_target_pairs={{1,0},{2,1},{3,2},{4,3},{5,4},{6,5},{7,6},{9,8},{10,9},{11,10},{12... | collective-permute-start | bytes 98312 | tf_op jit(solution)/shard_map/ppermute | solution.py:280
  7.5 1.9 %shard_map.59 = (f32[8,128]{1,0:T(8,128)}, f32[64,256]{1,0:T(8,128)}, f32[64,256]{1,0:T(8,128)}, f32[8,128]{1,0:T(8,128)}, f32[8,128]{1,0:T(8,128)}) custom-call(f32[64,1024]{1,0:T(8,128)} %topo_ref.1, bf16[64,1024]{1,0:T(8,128)(2,1)} %kappa_ref.1), custom_call_target="tpu_custom_call" | custom-call | flops 20480000 | bytes 262144 | tf_op jit(solution)/shard_map/pallas_call | solution.py:29
  9.4 0.0 collective-permute-done.low_ref
  9.4 1.4 %collective-permute-done.1.high_ref = f32[8,8,128]{2,1,0:T(8,128)S(1)} collective-permute-done((f32[8,8,128]{2,1,0:T(8,128)S(1)}, f32[8,8,128]{2,1,0:T(8,128)S(1)}, u32[]{:S(2)}, u32[]{:S(2)}) %collective-permute-start.1) | collective-permute-done | bytes 32800 | tf_op jit(solution)/shard_map/ppermute | solution.py:280
  10.8 0.0 copy-done.3
  10.8 0.6 copy-done.4
  11.5 1.7 %shard_map.60 = (f32[48,8,128]{2,1,0:T(8,128)}, f32[2,8,128]{2,1,0:T(8,128)}, f32[2,8,128]{2,1,0:T(8,128)}) custom-call(f32[3,8,8,128]{3,2,1,0:T(8,128)} %force_ref.1, f32[8,8,128]{2,1,0:T(8,128)} %visc_ref.1, f32[8,128]{1,0:T(8,128)} %get-tuple-element.17.load_ref, f32[8,8,128]{2,1,0:T(8,128)} %copy-done.3, f32[8,8,128]{2,1,0:T(8,128)} %copy-done.4, ...), custom_call_target="tpu_custom_call" | custom-call | flops 20480000 | bytes 262144 | tf_op jit(solution)/shard_map/pallas_call | solution.py:29
  13.2 3.1 %collective-permute-start.2 = (f32[2,8,128]{2,1,0:T(8,128)}, f32[2,8,128]{2,1,0:T(8,128)S(1)}, u32[]{:S(2)}, u32[]{:S(2)}) collective-permute-start(f32[2,8,128]{2,1,0:T(8,128)} %get-tuple-element.21), channel_id=1, source_target_pairs={{0,8},{8,16},{16,24},{24,32},{32,40},{40,48},{48,56},{56,64},{64,7... | collective-permute-start | bytes 24584 | tf_op jit(solution)/shard_map/ppermute | solution.py:279
  16.3 1.3 %collective-permute-start.3 = (f32[2,8,128]{2,1,0:T(8,128)}, f32[2,8,128]{2,1,0:T(8,128)S(1)}, u32[]{:S(2)}, u32[]{:S(2)}) collective-permute-start(f32[2,8,128]{2,1,0:T(8,128)} %get-tuple-element.22), channel_id=1, source_target_pairs={{8,0},{16,8},{24,16},{32,24},{40,32},{48,40},{56,48},{64,56},{72,6... | collective-permute-start | bytes 24584 | tf_op jit(solution)/shard_map/ppermute | solution.py:280
  17.6 0.0 collective-permute-done.2.rl_ref
  17.6 3.3 %collective-permute-done.3.rr_ref = f32[2,8,128]{2,1,0:T(8,128)S(1)} collective-permute-done((f32[2,8,128]{2,1,0:T(8,128)}, f32[2,8,128]{2,1,0:T(8,128)S(1)}, u32[]{:S(2)}, u32[]{:S(2)}) %collective-permute-start.3) | collective-permute-done | bytes 8224 | tf_op jit(solution)/shard_map/ppermute | solution.py:280
  20.9 0.0 copy-done.5
  20.9 0.6 copy-done.6
  21.5 1.8 %shard_map.61 = (f32[136,128]{1,0:T(8,128)}, f32[136,128]{1,0:T(8,128)}, f32[64,256]{1,0:T(8,128)}, f32[64,256]{1,0:T(8,128)}) custom-call(f32[48,8,128]{2,1,0:T(8,128)} %get-tuple-element.20.planes_ref, f32[2,8,128]{2,1,0:T(8,128)} %copy-done.5, f32[2,8,128]{2,1,0:T(8,128)} %copy-done.6, f32[64,256]{1,0:T(8,128)} %get-tuple-element.23.height_ref, ...), custom_call_target="tpu_custom_call" | custom-call | flops 20480000 | bytes 262144 | tf_op jit(solution)/shard_map/pallas_call | solution.py:29
  23.2 7.4 %collective-permute-start.4 = (f32[136,128]{1,0:T(8,128)}, f32[136,128]{1,0:T(8,128)S(1)}, u32[]{:S(2)}, u32[]{:S(2)}) collective-permute-start(f32[136,128]{1,0:T(8,128)} %get-tuple-element.25), channel_id=1, source_target_pairs={{0,128},{128,256},{256,384},{1,129},{129,257},{257,385},{2,130},{1... | collective-permute-start | bytes 208904 | tf_op jit(solution)/shard_map/ppermute | solution.py:279
  30.6 1.9 %collective-permute-start.5 = (f32[136,128]{1,0:T(8,128)}, f32[136,128]{1,0:T(8,128)S(1)}, u32[]{:S(2)}, u32[]{:S(2)}) collective-permute-start(f32[136,128]{1,0:T(8,128)} %get-tuple-element.26), channel_id=1, source_target_pairs={{128,0},{256,128},{384,256},{129,1},{257,129},{385,257},{130,2},{2... | collective-permute-start | bytes 208904 | tf_op jit(solution)/shard_map/ppermute | solution.py:280
  32.6 0.0 collective-permute-done.4.before_ref
  32.6 0.0 copy-start
  32.6 3.9 %collective-permute-done.5.after_ref = f32[136,128]{1,0:T(8,128)S(1)} collective-permute-done((f32[136,128]{1,0:T(8,128)}, f32[136,128]{1,0:T(8,128)S(1)}, u32[]{:S(2)}, u32[]{:S(2)}) %collective-permute-start.5) | collective-permute-done | bytes 69664 | tf_op jit(solution)/shard_map/ppermute | solution.py:280
  36.5 0.0 copy-done
  36.5 0.6 copy-done.1
  37.1 3.2 %shard_map.62 = (f32[3,8,8,128]{3,2,1,0:T(8,128)}, f32[64,128]{1,0:T(8,128)}, f32[2,8,128]{2,1,0:T(8,128)}) custom-call(f32[48,8,128]{2,1,0:T(8,128)} %get-tuple-element.20.planes_ref, f32[2,8,128]{2,1,0:T(8,128)} %copy-done.5, f32[2,8,128]{2,1,0:T(8,128)} %copy-done.6, f32[136,128]{1,0:T(8,128)} %copy-done, f32[136,128]{1,0:T(8,128)} %copy-done.1), custom_call_target="tpu_custom_call" | custom-call | flops 20480000 | bytes 262144 | tf_op jit(solution)/shard_map/pallas_call | solution.py:29
  40.3 25.6 %all_to_all.10 = f32[64,1,128]{2,1,0:T(1,128)} all-to-all(f32[64,1,128]{2,1,0:T(1,128)} %bitcast.16), channel_id=1, replica_groups=mesh['gx'=4,'gy'=16,'gz'=8] {'gx','gy'}, dimensions={0} | all-to-all | bytes 65536 | tf_op jit(solution)/shard_map/all_to_all | solution.py:320
  65.9 1.5 %shard_map.63 = f32[8,8,128]{2,1,0:T(8,128)} custom-call(f32[64,128]{1,0:T(8,128)} %bitcast.17, f32[2,8,128]{2,1,0:T(8,128)} %get-tuple-element.28.top_ref), custom_call_target="tpu_custom_call" | custom-call | flops 20480000 | bytes 262144 | tf_op jit(solution)/shard_map/pallas_call | solution.py:29
  67.4 7.0 %all-to-all-start.1 = ((f32[8,8,128]{2,1,0:T(8,128)}), f32[8,8,128]{2,1,0:T(8,128)S(1)}, u32[]{:S(2)}, u32[]{:S(2)}) async-start(f32[8,8,128]{2,1,0:T(8,128)} %shard_map.63), calls=%async_computation.1 | async-start | bytes 65536 | tf_op jit(solution)/shard_map/all_to_all | solution.py:323
  74.4 3.0 %shard_map.64.height_ref = f32[64,128]{1,0:T(8,128)} custom-call(f32[64,256]{1,0:T(8,128)} %get-tuple-element.30.height_ref, f32[64,256]{1,0:T(8,128)} %get-tuple-element.31.conduct_ref, f32[136,128]{1,0:T(8,128)} %copy-done, f32[136,128]{1,0:T(8,128)} %copy-done.1), custom_call_target="tpu_custom_call" | custom-call | flops 20480000 | bytes 262144 | tf_op jit(solution)/shard_map/pallas_call | solution.py:29
  77.4 4.0 %all-to-all-done.1.parts_ref = f32[8,8,128]{2,1,0:T(8,128)S(1)} async-done(((f32[8,8,128]{2,1,0:T(8,128)}), f32[8,8,128]{2,1,0:T(8,128)S(1)}, u32[]{:S(2)}, u32[]{:S(2)}) %all-to-all-start.1) | async-done | bytes 32800 | tf_op jit(solution)/shard_map/all_to_all | solution.py:323
  81.4 0.6 copy-done.2
  82.0 1.9 %shard_map.65 = (f32[3,8,8,128]{3,2,1,0:T(8,128)}, f32[64,128]{1,0:T(8,128)}) custom-call(f32[8,8,128]{2,1,0:T(8,128)} %copy-done.2, f32[48,8,128]{2,1,0:T(8,128)} %get-tuple-element.20.planes_ref, f32[3,8,8,128]{3,2,1,0:T(8,128)} %get-tuple-element.29.image_ref, f32[64,128]{1,0:T(8,128)} %shard_map.64.height_ref), custom_call_target="tpu_custom_call" | custom-call | flops 20480000 | bytes 262144 | tf_op jit(solution)/shard_map/pallas_call | solution.py:29
  (8 shorter events, 0.0 us)
Async XLA Ops:
  2.1 7.3 %collective-permute-start = (f32[8,8,128]{2,1,0:T(8,128)S(1)}, f32[8,8,128]{2,1,0:T(8,128)S(1)}, u32[]{:S(2)}, u32[]{:S(2)}) collective-permute-start(f32[8,8,128]{2,1,0:T(8,128)S(1)} %pad_maximum_fusion), channel_id=1, source_target_pairs={{0,1},{1,2},{2,3},{3,4},{4,5},{5,6},{6,7},{8,9},{9,10},{10,11},{11... | collective-permute-start | bytes 98312 | tf_op jit(solution)/shard_map/ppermute | solution.py:279
  6.2 4.7 %collective-permute-start.1 = (f32[8,8,128]{2,1,0:T(8,128)S(1)}, f32[8,8,128]{2,1,0:T(8,128)S(1)}, u32[]{:S(2)}, u32[]{:S(2)}) collective-permute-start(f32[8,8,128]{2,1,0:T(8,128)S(1)} %pad_maximum_fusion.1), channel_id=1, source_target_pairs={{1,0},{2,1},{3,2},{4,3},{5,4},{6,5},{7,6},{9,8},{10,9},{11,10},{12... | collective-permute-start | bytes 98312 | tf_op jit(solution)/shard_map/ppermute | solution.py:280
  9.4 1.5 %copy-start.3 = (f32[8,8,128]{2,1,0:T(8,128)}, f32[8,8,128]{2,1,0:T(8,128)S(1)}, u32[]{:S(2)}) copy-start(f32[8,8,128]{2,1,0:T(8,128)S(1)} %collective-permute-done.low_ref) | copy-start | bytes 98308
  10.8 0.6 copy-start.4
  13.2 4.4 %collective-permute-start.2 = (f32[2,8,128]{2,1,0:T(8,128)}, f32[2,8,128]{2,1,0:T(8,128)S(1)}, u32[]{:S(2)}, u32[]{:S(2)}) collective-permute-start(f32[2,8,128]{2,1,0:T(8,128)} %get-tuple-element.21), channel_id=1, source_target_pairs={{0,8},{8,16},{16,24},{24,32},{32,40},{40,48},{48,56},{56,64},{64,7... | collective-permute-start | bytes 24584 | tf_op jit(solution)/shard_map/ppermute | solution.py:279
  16.3 4.6 %collective-permute-start.3 = (f32[2,8,128]{2,1,0:T(8,128)}, f32[2,8,128]{2,1,0:T(8,128)S(1)}, u32[]{:S(2)}, u32[]{:S(2)}) collective-permute-start(f32[2,8,128]{2,1,0:T(8,128)} %get-tuple-element.22), channel_id=1, source_target_pairs={{8,0},{16,8},{24,16},{32,24},{40,32},{48,40},{56,48},{64,56},{72,6... | collective-permute-start | bytes 24584 | tf_op jit(solution)/shard_map/ppermute | solution.py:280
  17.6 3.3 %copy-start.5 = (f32[2,8,128]{2,1,0:T(8,128)}, f32[2,8,128]{2,1,0:T(8,128)S(1)}, u32[]{:S(2)}) copy-start(f32[2,8,128]{2,1,0:T(8,128)S(1)} %collective-permute-done.2.rl_ref) | copy-start | bytes 24580
  20.9 0.6 copy-start.6
  23.2 9.3 %collective-permute-start.4 = (f32[136,128]{1,0:T(8,128)}, f32[136,128]{1,0:T(8,128)S(1)}, u32[]{:S(2)}, u32[]{:S(2)}) collective-permute-start(f32[136,128]{1,0:T(8,128)} %get-tuple-element.25), channel_id=1, source_target_pairs={{0,128},{128,256},{256,384},{1,129},{129,257},{257,385},{2,130},{1... | collective-permute-start | bytes 208904 | tf_op jit(solution)/shard_map/ppermute | solution.py:279
  30.6 5.8 %collective-permute-start.5 = (f32[136,128]{1,0:T(8,128)}, f32[136,128]{1,0:T(8,128)S(1)}, u32[]{:S(2)}, u32[]{:S(2)}) collective-permute-start(f32[136,128]{1,0:T(8,128)} %get-tuple-element.26), channel_id=1, source_target_pairs={{128,0},{256,128},{384,256},{129,1},{257,129},{385,257},{130,2},{2... | collective-permute-start | bytes 208904 | tf_op jit(solution)/shard_map/ppermute | solution.py:280
  32.6 3.9 %copy-start = (f32[136,128]{1,0:T(8,128)}, f32[136,128]{1,0:T(8,128)S(1)}, u32[]{:S(2)}) copy-start(f32[136,128]{1,0:T(8,128)S(1)} %collective-permute-done.4.before_ref) | copy-start | bytes 208900
  36.5 0.6 copy-start.1
  67.4 14.0 %all-to-all-start.1 = ((f32[8,8,128]{2,1,0:T(8,128)}), f32[8,8,128]{2,1,0:T(8,128)S(1)}, u32[]{:S(2)}, u32[]{:S(2)}) async-start(f32[8,8,128]{2,1,0:T(8,128)} %shard_map.63), calls=%async_computation.1 | async-start | bytes 65536 | tf_op jit(solution)/shard_map/all_to_all | solution.py:323
  81.4 0.6 copy-start.2

commit v2 on v1

--- a/solution.py
+++ b/solution.py
@@ -25,13 +25,14 @@
     return pl.BlockSpec(memory_space=pltpu.VMEM)
 
 
-def call(body, outs, ins, scratch=(), cost=20000):
+def call(body, outs, ins, scratch=(), cost=20000, limit=8 << 20):
     return pl.pallas_call(
         body,
         out_shape=[jax.ShapeDtypeStruct(s, f32) for s in outs],
         in_specs=[vmem() for _ in ins],
         out_specs=[vmem() for _ in outs],
         scratch_shapes=list(scratch),
+        compiler_params=pltpu.CompilerParams(vmem_limit_bytes=limit),
         cost_estimate=pl.CostEstimate(flops=cost * 1024, bytes_accessed=1 << 18, transcendentals=0),
     )(*ins)
 

time: 84.6 us -> 74.7 us (0.88)
  Pallas kernels: 14.9 us -> 5.14 us
  waiting for transfers between devices: 12.6 us -> 14.4 us
  local copies, waits for them, and re-layouts: 3.96 us -> 2.46 us
    pallas_call x7, Pallas kernels: 14.9 us -> 5.14 us  [call(): pl.pallas_call(body, out_shape=[jax.ShapeDtypeStruct(s, f32) for s in out...]
    unnamed x14 -> x8, local copies, waits for them, and re-layouts: 2.45 us -> 0.91 us
    all_to_all x1, waiting for transfers between devices: 3.98 us -> 5.47 us  [local(): parts = lax.all_to_all(parts, 'gz', 0, 0)]
  transfers between devices with their start and end apart: 7 -> 7, of which waited for: 4 -> 4; matrix products, arithmetic and copies ran while one was open for 0% -> 0% of each run, Pallas kernels for 6% -> 2%
where the time goes in v2:
time: 74.7 us; the launch traced here: 74.2 us
  starting transfers between devices  26.2 us (35%)
  blocking collectives  25.2 us (34%)
  waiting for transfers between devices  14.4 us (19%)
  Pallas kernels  5.14 us (7%)
  local copies, waits for them, and re-layouts  2.46 us (3%)
  between operations  0.78 us (1%)
    all_to_all x1, blocking collectives, local(): sums = lax.all_to_all(sums.reshape(group, 1, 128), ('gx', 'gy'), 0, 0)  25.2 us
    ppermute x3, starting transfers between devices, exchange(): from_before = lax.ppermute(to_next, axis, [(i, i + 1) for i in range(ends)])  14.6 us
    ppermute x3, waiting for transfers between devices, exchange(): lax.ppermute(to_before, axis, [(i + 1, i) for i in range(ends)])  8.88 us
    all_to_all x1, starting transfers between devices, local(): parts = lax.all_to_all(parts, 'gz', 0, 0)  7.02 us
    all_to_all x1, waiting for transfers between devices, local(): parts = lax.all_to_all(parts, 'gz', 0, 0)  5.47 us
    pallas_call x7, Pallas kernels, call(): pl.pallas_call(body, out_shape=[jax.ShapeDtypeStruct(s, f32) for s in out...  5.14 us
    ppermute x3, starting transfers between devices, exchange(): lax.ppermute(to_before, axis, [(i + 1, i) for i in range(ends)])  4.64 us
  transfers between devices with their start and end apart: 7, of which 4 were waited for; matrix products, arithmetic and copies ran while one was open for 0% of the time, Pallas kernels for 2%

profile of v2, /device:TPU:1, one launch (start us, length us, event | category | flops | bytes accessed | tf_op | source)
XLA Modules:
  0.0 74.2 jit_solution(12710422903795492522)
XLA Ops:
  0.6 0.0 copy-start
  0.6 0.8 %fusion = (f32[2,8,128]{2,1,0:T(8,128)S(1)}, f32[2,8,128]{2,1,0:T(8,128)S(1)}) fusion(f32[8,8,128]{2,1,0:T(8,128)} %visc_ref.1), kind=kLoop, calls=%fused_computation.8 | loop fusion | bytes 32768 | tf_op jit(solution)/shard_map/slice | solution.py:289
  1.4 0.8 %slice_bitcast_fusion.2 = (f32[2,8,128]{2,1,0:T(8,128)S(1)}, f32[2,8,128]{2,1,0:T(8,128)S(1)}, f32[2,8,128]{2,1,0:T(8,128)S(1)}, f32[2,8,128]{2,1,0:T(8,128)S(1)...) fusion(f32[3,8,8,128]{3,2,1,0:T(8,128)} %force_ref.1), kind=kLoop, calls=%fused_computation.4 | loop fusion | bytes 98304 | tf_op jit(solution)/shard_map/squeeze | solution.py:289
  2.2 4.0 %collective-permute-start = (f32[8,8,128]{2,1,0:T(8,128)S(1)}, f32[8,8,128]{2,1,0:T(8,128)S(1)}, u32[]{:S(2)}, u32[]{:S(2)}) collective-permute-start(f32[8,8,128]{2,1,0:T(8,128)S(1)} %pad_maximum_fusion), channel_id=1, source_target_pairs={{0,1},{1,2},{2,3},{3,4},{4,5},{5,6},{6,7},{8,9},{9,10},{10,11},{11... | collective-permute-start | bytes 98312 | tf_op jit(solution)/shard_map/ppermute | solution.py:280
  6.2 0.0 copy-start.1
  6.2 1.4 %collective-permute-start.1 = (f32[8,8,128]{2,1,0:T(8,128)S(1)}, f32[8,8,128]{2,1,0:T(8,128)S(1)}, u32[]{:S(2)}, u32[]{:S(2)}) collective-permute-start(f32[8,8,128]{2,1,0:T(8,128)S(1)} %pad_maximum_fusion.1), channel_id=1, source_target_pairs={{1,0},{2,1},{3,2},{4,3},{5,4},{6,5},{7,6},{9,8},{10,9},{11,10},{12... | collective-permute-start | bytes 98312 | tf_op jit(solution)/shard_map/ppermute | solution.py:281
  7.7 0.0 copy-done
  7.7 0.0 copy-start.2
  7.7 0.9 %copy-done.2 = bf16[64,1024]{1,0:T(8,128)(2,1)S(1)} copy-done((bf16[64,1024]{1,0:T(8,128)(2,1)S(1)}, bf16[64,1024]{1,0:T(8,128)(2,1)}, u32[]{:S(2)}) %copy-start.2) | copy-done | bytes 131096
  8.6 0.0 copy-start.3
  8.6 0.3 shard_map.59
  8.9 0.0 collective-permute-done.low_ref
  8.9 2.1 %collective-permute-done.1.high_ref = f32[8,8,128]{2,1,0:T(8,128)S(1)} collective-permute-done((f32[8,8,128]{2,1,0:T(8,128)S(1)}, f32[8,8,128]{2,1,0:T(8,128)S(1)}, u32[]{:S(2)}, u32[]{:S(2)}) %collective-permute-start.1) | collective-permute-done | bytes 32800 | tf_op jit(solution)/shard_map/ppermute | solution.py:281
  11.0 0.0 copy-done.1
  11.0 0.0 copy-done.3
  11.0 0.2 shard_map.60
  11.2 3.1 %collective-permute-start.2 = (f32[2,8,128]{2,1,0:T(8,128)S(1)}, f32[2,8,128]{2,1,0:T(8,128)S(1)}, u32[]{:S(2)}, u32[]{:S(2)}) collective-permute-start(f32[2,8,128]{2,1,0:T(8,128)S(1)} %get-tuple-element.21), channel_id=1, source_target_pairs={{0,8},{8,16},{16,24},{24,32},{32,40},{40,48},{48,56},{56,64},{64,7... | collective-permute-start | bytes 24584 | tf_op jit(solution)/shard_map/ppermute | solution.py:280
  14.3 1.3 %collective-permute-start.3 = (f32[2,8,128]{2,1,0:T(8,128)S(1)}, f32[2,8,128]{2,1,0:T(8,128)S(1)}, u32[]{:S(2)}, u32[]{:S(2)}) collective-permute-start(f32[2,8,128]{2,1,0:T(8,128)S(1)} %get-tuple-element.22), channel_id=1, source_target_pairs={{8,0},{16,8},{24,16},{32,24},{40,32},{48,40},{56,48},{64,56},{72,6... | collective-permute-start | bytes 24584 | tf_op jit(solution)/shard_map/ppermute | solution.py:281
  15.6 0.0 collective-permute-done.2.rl_ref
  15.6 3.1 %collective-permute-done.3.rr_ref = f32[2,8,128]{2,1,0:T(8,128)S(1)} collective-permute-done((f32[2,8,128]{2,1,0:T(8,128)S(1)}, f32[2,8,128]{2,1,0:T(8,128)S(1)}, u32[]{:S(2)}, u32[]{:S(2)}) %collective-permute-start.3) | collective-permute-done | bytes 8224 | tf_op jit(solution)/shard_map/ppermute | solution.py:281
  18.7 0.1 shard_map.61
  18.8 7.4 %collective-permute-start.4 = (f32[136,128]{1,0:T(8,128)S(1)}, f32[136,128]{1,0:T(8,128)S(1)}, u32[]{:S(2)}, u32[]{:S(2)}) collective-permute-start(f32[136,128]{1,0:T(8,128)S(1)} %get-tuple-element.25), channel_id=1, source_target_pairs={{0,128},{128,256},{256,384},{1,129},{129,257},{257,385},{2,130},{1... | collective-permute-start | bytes 208904 | tf_op jit(solution)/shard_map/ppermute | solution.py:280
  26.3 1.9 %collective-permute-start.5 = (f32[136,128]{1,0:T(8,128)S(1)}, f32[136,128]{1,0:T(8,128)S(1)}, u32[]{:S(2)}, u32[]{:S(2)}) collective-permute-start(f32[136,128]{1,0:T(8,128)S(1)} %get-tuple-element.26), channel_id=1, source_target_pairs={{128,0},{256,128},{384,256},{129,1},{257,129},{385,257},{130,2},{2... | collective-permute-start | bytes 208904 | tf_op jit(solution)/shard_map/ppermute | solution.py:281
  28.2 0.0 collective-permute-done.4.before_ref
  28.2 3.7 %collective-permute-done.5.after_ref = f32[136,128]{1,0:T(8,128)S(1)} collective-permute-done((f32[136,128]{1,0:T(8,128)S(1)}, f32[136,128]{1,0:T(8,128)S(1)}, u32[]{:S(2)}, u32[]{:S(2)}) %collective-permute-start.5) | collective-permute-done | bytes 69664 | tf_op jit(solution)/shard_map/ppermute | solution.py:281
  31.9 1.5 %shard_map.62 = (f32[3,8,8,128]{3,2,1,0:T(8,128)S(1)}, f32[64,128]{1,0:T(8,128)S(1)}, f32[2,8,128]{2,1,0:T(8,128)S(1)}) custom-call(f32[48,8,128]{2,1,0:T(8,128)S(1)} %get-tuple-element.20.planes_ref, f32[2,8,128]{2,1,0:T(8,128)S(1)} %collective-permute-done.2.rl_ref, f32[2,8,128]{2,1,0:T(8,128)S(1)} %collective-permute-done.3.rr_ref, ...), custom_call_target="tpu_custom_call" | custom-call | flops 20480000 | bytes 262144 | tf_op jit(solution)/shard_map/pallas_call | solution.py:29
  33.5 25.2 %all_to_all.10 = f32[64,1,128]{2,1,0:T(1,128)S(1)} all-to-all(f32[64,1,128]{2,1,0:T(1,128)S(1)} %bitcast.16), channel_id=1, replica_groups=mesh['gx'=4,'gy'=16,'gz'=8] {'gx','gy'}, dimensions={0} | all-to-all | bytes 65536 | tf_op jit(solution)/shard_map/all_to_all | solution.py:321
  58.7 0.7 shard_map.63
  59.4 7.0 %all-to-all-start.1 = ((f32[8,8,128]{2,1,0:T(8,128)}), f32[8,8,128]{2,1,0:T(8,128)S(1)}, u32[]{:S(2)}, u32[]{:S(2)}) async-start(f32[8,8,128]{2,1,0:T(8,128)} %shard_map.63), calls=%async_computation.1 | async-start | bytes 65536 | tf_op jit(solution)/shard_map/all_to_all | solution.py:324
  66.4 1.4 %shard_map.64.height_ref = f32[64,128]{1,0:T(8,128)S(1)} custom-call(f32[64,256]{1,0:T(8,128)S(1)} %get-tuple-element.30.height_ref, f32[64,256]{1,0:T(8,128)S(1)} %get-tuple-element.31.conduct_ref, f32[136,128]{1,0:T(8,128)S(1)} %collective-permute-done.4.before_ref, f32[136,128]{1,0:T(8,128)S(1)} %collective-permute-done.5.after_ref), custom_call_target="tpu_custom_call" | custom-call | flops 20480000 | bytes 262144 | tf_op jit(solution)/shard_map/pallas_call | solution.py:29
  67.8 5.5 %all-to-all-done.1.parts_ref = f32[8,8,128]{2,1,0:T(8,128)S(1)} async-done(((f32[8,8,128]{2,1,0:T(8,128)}), f32[8,8,128]{2,1,0:T(8,128)S(1)}, u32[]{:S(2)}, u32[]{:S(2)}) %all-to-all-start.1) | async-done | bytes 32800 | tf_op jit(solution)/shard_map/all_to_all | solution.py:324
  73.3 0.9 %shard_map.65 = (f32[3,8,8,128]{3,2,1,0:T(8,128)}, f32[64,128]{1,0:T(8,128)}) custom-call(f32[8,8,128]{2,1,0:T(8,128)S(1)} %all-to-all-done.1.parts_ref, f32[48,8,128]{2,1,0:T(8,128)S(1)} %get-tuple-element.20.planes_ref, f32[3,8,8,128]{3,2,1,0:T(8,128)S(1)} %get-tuple-element.29.image_ref, f32[64,128]{1,0:T(8,128)S(1)} %shard_map.64.height_ref), custom_call_target="tpu_custom_call" | custom-call | flops 20480000 | bytes 262144 | tf_op jit(solution)/shard_map/pallas_call | solution.py:29
  (2 shorter events, 0.0 us)
Async XLA Ops:
  0.6 7.0 %copy-start = (f32[64,1024]{1,0:T(8,128)S(1)}, f32[64,1024]{1,0:T(8,128)}, u32[]{:S(2)}) copy-start(f32[64,1024]{1,0:T(8,128)} %topo_ref.1) | copy-start | bytes 786436
  2.2 6.7 %collective-permute-start = (f32[8,8,128]{2,1,0:T(8,128)S(1)}, f32[8,8,128]{2,1,0:T(8,128)S(1)}, u32[]{:S(2)}, u32[]{:S(2)}) collective-permute-start(f32[8,8,128]{2,1,0:T(8,128)S(1)} %pad_maximum_fusion), channel_id=1, source_target_pairs={{0,1},{1,2},{2,3},{3,4},{4,5},{5,6},{6,7},{8,9},{9,10},{10,11},{11... | collective-permute-start | bytes 98312 | tf_op jit(solution)/shard_map/ppermute | solution.py:280
  6.2 4.8 %copy-start.1 = (f32[3,8,8,128]{3,2,1,0:T(8,128)S(1)}, f32[3,8,8,128]{3,2,1,0:T(8,128)}, u32[]{:S(2)}) copy-start(f32[3,8,8,128]{3,2,1,0:T(8,128)} %force_ref.1) | copy-start | bytes 294916
  6.2 4.8 %collective-permute-start.1 = (f32[8,8,128]{2,1,0:T(8,128)S(1)}, f32[8,8,128]{2,1,0:T(8,128)S(1)}, u32[]{:S(2)}, u32[]{:S(2)}) collective-permute-start(f32[8,8,128]{2,1,0:T(8,128)S(1)} %pad_maximum_fusion.1), channel_id=1, source_target_pairs={{1,0},{2,1},{3,2},{4,3},{5,4},{6,5},{7,6},{9,8},{10,9},{11,10},{12... | collective-permute-start | bytes 98312 | tf_op jit(solution)/shard_map/ppermute | solution.py:281
  7.7 0.9 %copy-start.2 = (bf16[64,1024]{1,0:T(8,128)(2,1)S(1)}, bf16[64,1024]{1,0:T(8,128)(2,1)}, u32[]{:S(2)}) copy-start(bf16[64,1024]{1,0:T(8,128)(2,1)} %kappa_ref.1) | copy-start | bytes 393220
  8.6 2.4 %copy-start.3 = (f32[8,8,128]{2,1,0:T(8,128)S(1)}, f32[8,8,128]{2,1,0:T(8,128)}, u32[]{:S(2)}) copy-start(f32[8,8,128]{2,1,0:T(8,128)} %visc_ref.1) | copy-start | bytes 98308
  11.2 4.4 %collective-permute-start.2 = (f32[2,8,128]{2,1,0:T(8,128)S(1)}, f32[2,8,128]{2,1,0:T(8,128)S(1)}, u32[]{:S(2)}, u32[]{:S(2)}) collective-permute-start(f32[2,8,128]{2,1,0:T(8,128)S(1)} %get-tuple-element.21), channel_id=1, source_target_pairs={{0,8},{8,16},{16,24},{24,32},{32,40},{40,48},{48,56},{56,64},{64,7... | collective-permute-start | bytes 24584 | tf_op jit(solution)/shard_map/ppermute | solution.py:280
  14.3 4.4 %collective-permute-start.3 = (f32[2,8,128]{2,1,0:T(8,128)S(1)}, f32[2,8,128]{2,1,0:T(8,128)S(1)}, u32[]{:S(2)}, u32[]{:S(2)}) collective-permute-start(f32[2,8,128]{2,1,0:T(8,128)S(1)} %get-tuple-element.22), channel_id=1, source_target_pairs={{8,0},{16,8},{24,16},{32,24},{40,32},{48,40},{56,48},{64,56},{72,6... | collective-permute-start | bytes 24584 | tf_op jit(solution)/shard_map/ppermute | solution.py:281
  18.8 9.4 %collective-permute-start.4 = (f32[136,128]{1,0:T(8,128)S(1)}, f32[136,128]{1,0:T(8,128)S(1)}, u32[]{:S(2)}, u32[]{:S(2)}) collective-permute-start(f32[136,128]{1,0:T(8,128)S(1)} %get-tuple-element.25), channel_id=1, source_target_pairs={{0,128},{128,256},{256,384},{1,129},{129,257},{257,385},{2,130},{1... | collective-permute-start | bytes 208904 | tf_op jit(solution)/shard_map/ppermute | solution.py:280
  26.3 5.6 %collective-permute-start.5 = (f32[136,128]{1,0:T(8,128)S(1)}, f32[136,128]{1,0:T(8,128)S(1)}, u32[]{:S(2)}, u32[]{:S(2)}) collective-permute-start(f32[136,128]{1,0:T(8,128)S(1)} %get-tuple-element.26), channel_id=1, source_target_pairs={{128,0},{256,128},{384,256},{129,1},{257,129},{385,257},{130,2},{2... | collective-permute-start | bytes 208904 | tf_op jit(solution)/shard_map/ppermute | solution.py:281
  59.4 13.9 %all-to-all-start.1 = ((f32[8,8,128]{2,1,0:T(8,128)}), f32[8,8,128]{2,1,0:T(8,128)S(1)}, u32[]{:S(2)}, u32[]{:S(2)}) async-start(f32[8,8,128]{2,1,0:T(8,128)} %shard_map.63), calls=%async_computation.1 | async-start | bytes 65536 | tf_op jit(solution)/shard_map/all_to_all | solution.py:324

commit v3 on v2

--- a/solution.py
+++ b/solution.py
@@ -88,16 +88,37 @@
     right_ref[...] = right
 
 
-def assemble(force_ref, visc_ref, load_ref, low_ref, high_ref, sl_ref, sr_ref, planes_ref, left_ref, right_ref):
+def is_even(axis):
+    return lax.rem(lax.axis_index(axis), 2) == 0
+
+
+def fetch(force_ref, visc_ref, topo_ref, kappa_ref, odd_ref, even_ref, force_out, visc_out, topo_out, kappa_out, sems):
+    depth = visc_ref.shape[0]
+    start = jnp.where(is_even("gz"), 0, depth - 2)
+    moves = []
+    for target, first in ((odd_ref, start), (even_ref, depth - 2 - start)):
+        moves.append((force_ref.at[:, pl.ds(first, 2)], target.at[0:3]))
+        moves.append((visc_ref.at[pl.ds(first, 2)], target.at[3]))
+    moves += [(force_ref, force_out), (visc_ref, visc_out), (topo_ref, topo_out), (kappa_ref, kappa_out)]
+    copies = [pltpu.make_async_copy(source, target, sems.at[i]) for i, (source, target) in enumerate(moves)]
+    for copy in copies:
+        copy.start()
+    for copy in copies:
+        copy.wait()
+
+
+def assemble(force_ref, visc_ref, load_ref, odd_ref, even_ref, sl_ref, sr_ref, planes_ref, odd_out, even_out):
+    upward = is_even("gz")
     lane = lanes((8, 128))
     left = jnp.zeros((8, 128), f32)
     right = jnp.zeros((8, 128), f32)
     for field in range(4):
         for depth in range(DEPTHS):
             if depth < 2:
-                plane = low_ref[2 * field + depth]
+                plane = jnp.where(upward, odd_ref[field, depth], even_ref[field, depth])
             elif depth >= DEPTHS - 2:
-                plane = high_ref[2 * field + depth - (DEPTHS - 2)]
+                i = depth - (DEPTHS - 2)
+                plane = jnp.where(upward, even_ref[field, i], odd_ref[field, i])
             elif field == 3:
                 plane = visc_ref[depth - 2]
             else:
@@ -109,23 +130,35 @@
             mask = lane // 2 == p
             left = jnp.where(mask, rolled(plane, 2 * p), left)
             right = jnp.where(mask, rolled(plane, 2 * p - 126), right)
-    left_ref[0] = left
-    right_ref[0] = right
-    left_ref[1] = sl_ref[...]
-    right_ref[1] = sr_ref[...]
-
-
-def prepare_rows(planes_ref, rl_ref, rr_ref, height_ref, conduct_ref, down_ref, up_ref, height_out, conduct_out):
+    rightward = is_even("gy")
+    odd_out[0] = jnp.where(rightward, left, right)
+    even_out[0] = jnp.where(rightward, right, left)
+    odd_out[1] = jnp.where(rightward, sl_ref[...], sr_ref[...])
+    even_out[1] = jnp.where(rightward, sr_ref[...], sl_ref[...])
+
+
+def prepare_rows(planes_ref, odd_ref, even_ref, height_ref, conduct_ref, odd_out, even_out, rl_ref, rr_ref, height_out, conduct_out):
+    rightward = is_even("gy")
+    for i in range(2):
+        rl_ref[i] = jnp.where(rightward, odd_ref[i], even_ref[i])
+        rr_ref[i] = jnp.where(rightward, even_ref[i], odd_ref[i])
+    downward = is_even("gx")
+
+    def send(rows, low, high):
+        odd_out[rows, :] = jnp.where(downward, low, high)
+        even_out[rows, :] = jnp.where(downward, high, low)
+
     g = lax.axis_index("gz")
     last = lax.axis_size("gz") - 1
     lane = lanes((8, 128))
     for p in range(PLANES):
-        down_ref[2 * p : 2 * p + 2, :] = planes_ref[p, 6:8, :]
-        up_ref[2 * p : 2 * p + 2, :] = planes_ref[p, 0:2, :]
-    down_ref[PAIRS_ROW : PAIRS_ROW + 4, :] = jnp.concatenate([rl_ref[0, 6:8, :], rr_ref[0, 6:8, :]], axis=0)
-    up_ref[PAIRS_ROW : PAIRS_ROW + 4, :] = jnp.concatenate([rl_ref[0, 0:2, :], rr_ref[0, 0:2, :]], axis=0)
-    down_ref[PAIRS_ROW + 4 : SURFACE_ROW, :] = jnp.zeros((4, 128), f32)
-    up_ref[PAIRS_ROW + 4 : SURFACE_ROW, :] = jnp.zeros((4, 128), f32)
+        send(slice(2 * p, 2 * p + 2), planes_ref[p, 0:2, :], planes_ref[p, 6:8, :])
+    pad = jnp.zeros((4, 128), f32)
+    send(
+        slice(PAIRS_ROW, SURFACE_ROW),
+        jnp.concatenate([rl_ref[0, 0:2, :], rr_ref[0, 0:2, :], pad], axis=0),
+        jnp.concatenate([rl_ref[0, 6:8, :], rr_ref[0, 6:8, :], pad], axis=0),
+    )
     slot = 0
     for index, (source, target) in enumerate(((height_ref, height_out), (conduct_ref, conduct_out))):
         base = SURFACE_ROW + 16 * index
@@ -138,11 +171,10 @@
             target[rows, 0:128] = main
             target[rows, 128:256] = side
             if r == 0:
-                up_ref[base : base + 8, :] = main
-                up_ref[base + 8 : base + 16, :] = side
+                first = (main, side)
             if r == 7:
-                down_ref[base : base + 8, :] = main
-                down_ref[base + 8 : base + 16, :] = side
+                send(slice(base, base + 8), first[0], main)
+                send(slice(base + 8, base + 16), first[1], side)
             slot += 1
 
 
@@ -155,19 +187,33 @@
     return FACE * outer + rows + rolled(both, 1, 1) + rolled(both, 255, 1)
 
 
-def operate(planes_ref, rl_ref, rr_ref, before_ref, after_ref, image_ref, sums_ref, top_ref, x, w, diag):
+def sided(odd_ref, even_ref, axis):
+    first = is_even(axis)
+
+    def before(rows):
+        return jnp.where(first, odd_ref[rows, :], even_ref[rows, :])
+
+    def after(rows):
+        return jnp.where(first, even_ref[rows, :], odd_ref[rows, :])
+
+    return before, after
+
+
+def operate(planes_ref, rl_ref, rr_ref, odd_ref, even_ref, image_ref, sums_ref, top_ref, x, w, diag):
     lane = lanes((8, 128))
     row = lax.broadcasted_iota(jnp.int32, (8, 128), 0)
     pad = jnp.zeros((4, 128), f32)
-    lower_l = jnp.concatenate([after_ref[PAIRS_ROW : PAIRS_ROW + 2, :], pad, before_ref[PAIRS_ROW : PAIRS_ROW + 2, :]], 0)
-    lower_r = jnp.concatenate(
-        [after_ref[PAIRS_ROW + 2 : PAIRS_ROW + 4, :], pad, before_ref[PAIRS_ROW + 2 : PAIRS_ROW + 4, :]], 0
-    )
+    before, after = sided(odd_ref, even_ref, "gx")
+
+    def around(start):
+        rows = slice(start, start + 2)
+        return jnp.concatenate([after(rows), pad, before(rows)], axis=0)
+
+    lower_l = around(PAIRS_ROW)
+    lower_r = around(PAIRS_ROW + 2)
     for p in range(PLANES):
         x[p, 0:8, 0:128] = planes_ref[p]
-        x[p, 8:16, 0:128] = jnp.concatenate(
-            [after_ref[2 * p : 2 * p + 2, :], pad, before_ref[2 * p : 2 * p + 2, :]], 0
-        )
+        x[p, 8:16, 0:128] = around(2 * p)
         for start, l, r in ((0, rl_ref[0], rr_ref[0]), (8, lower_l, lower_r)):
             side = jnp.where(lane < 2, rolled(r, -2 * p), 0.0)
             side = jnp.where(lane >= 126, rolled(l, 126 - 2 * p), side)
@@ -206,12 +252,14 @@
     top_ref[1] = w[p, 0:8, 0:128]
 
 
-def diffuse(height_ref, conduct_ref, before_ref, after_ref, out_ref):
+def diffuse(height_ref, conduct_ref, odd_ref, even_ref, out_ref):
+    before, after = sided(odd_ref, even_ref, "gx")
+
     def extended(source, base):
-        def joined(ref):
-            return jnp.concatenate([ref[base : base + 8, :], ref[base + 8 : base + 16, :]], axis=1)
-
-        return jnp.concatenate([source[...], joined(after_ref), joined(before_ref)], axis=0)
+        def joined(side):
+            return jnp.concatenate([side(slice(base, base + 8)), side(slice(base + 8, base + 16))], axis=1)
+
+        return jnp.concatenate([source[...], joined(after), joined(before)], axis=0)
 
     h = extended(height_ref, SURFACE_ROW)
     k = extended(conduct_ref, SURFACE_ROW + 16)
@@ -270,56 +318,61 @@
         surface_ref[rows, :] = height_ref[rows, :] + jnp.broadcast_to(wide[r : r + 1, :], (8, 128))
 
 
-def shift(value, axis):
-    ends = lax.axis_size(axis) - 1
-    return value, [(i, i + 1) for i in range(ends)], [(i + 1, i) for i in range(ends)]
-
-
-def exchange(to_next, to_before, axis):
-    ends = lax.axis_size(axis) - 1
-    from_before = lax.ppermute(to_next, axis, [(i, i + 1) for i in range(ends)])
-    from_after = lax.ppermute(to_before, axis, [(i + 1, i) for i in range(ends)])
-    return from_before, from_after
+def swap(odd, even, axis):
+    count = lax.axis_size(axis)
+
+    def pairs(start):
+        found = []
+        for i in range(start, count - 1, 2):
+            found += [(i, i + 1), (i + 1, i)]
+        return found
+
+    return lax.ppermute(odd, axis, pairs(1)), lax.ppermute(even, axis, pairs(0))
 
 
 def local(body_force, viscosity, topography, kappa):
-    depth = viscosity.shape[0]
-
-    def layers(start):
-        fields = [body_force[c, start : start + 2] for c in range(3)] + [viscosity[start : start + 2]]
-        return jnp.concatenate(fields, axis=0)
-
-    low, high = exchange(layers(depth - 2), layers(0), "gz")
+    inputs = (body_force, viscosity, topography, kappa)
+    odd, even, body_force, viscosity, topography, kappa = pl.pallas_call(
+        fetch,
+        out_shape=[jax.ShapeDtypeStruct((4, 2, 8, 128), f32)] * 2
+        + [jax.ShapeDtypeStruct(x.shape, x.dtype) for x in inputs],
+        in_specs=[pl.BlockSpec(memory_space=pltpu.HBM)] * 4,
+        out_specs=[vmem()] * 6,
+        scratch_shapes=[pltpu.SemaphoreType.DMA((8,))],
+        compiler_params=pltpu.CompilerParams(vmem_limit_bytes=4 << 20),
+    )(*[pltpu.with_memory_space_constraint(x, pltpu.HBM) for x in inputs])
+    odd, even = swap(odd, even, "gz")
     load, height, conduct, left, right = call(
         surface_own,
         [(8, 128), (64, 256), (64, 256), (8, 128), (8, 128)],
         (topography, kappa),
     )
-    planes, left, right = call(
+    planes, odd, even = call(
         assemble,
         [(PLANES, 8, 128), (2, 8, 128), (2, 8, 128)],
-        (body_force, viscosity, load, low, high, left, right),
-    )
-    from_left, from_right = exchange(right, left, "gy")
-    down, up, height, conduct = call(
+        (body_force, viscosity, load, odd, even, left, right),
+    )
+    odd, even = swap(odd, even, "gy")
+    odd, even, from_left, from_right, height, conduct = call(
         prepare_rows,
-        [(GX_ROWS, 128), (GX_ROWS, 128), (64, 256), (64, 256)],
-        (planes, from_left, from_right, height, conduct),
-    )
-    before, after = exchange(down, up, "gx")
+        [(GX_ROWS, 128), (GX_ROWS, 128), (2, 8, 128), (2, 8, 128), (64, 256), (64, 256)],
+        (planes, odd, even, height, conduct),
+    )
+    odd, even = swap(odd, even, "gx")
     group = lax.axis_size("gx") * lax.axis_size("gy")
     image, sums, top = call(
         operate,
         [(3, 8, 8, 128), (group, 128), (2, 8, 128)],
-        (planes, from_left, from_right, before, after),
+        (planes, from_left, from_right, odd, even),
         [
             pltpu.VMEM((PLANES, 16, 256), f32),
             pltpu.VMEM((3 * DEPTHS, 16, 256), f32),
             pltpu.VMEM((DEPTHS, 8, 128), f32),
         ],
     )
+    (height,) = call(diffuse, [(64, 128)], (height, conduct, odd, even))
     sums = lax.all_to_all(sums.reshape(group, 1, 128), ("gx", "gy"), 0, 0)
-    (height,) = call(diffuse, [(64, 128)], (height, conduct, before, after))
+    sums, height = lax.optimization_barrier((sums, height))
     (parts,) = call(middle, [(lax.axis_size("gz"), 8, 128)], (sums.reshape(group, 128), top))
     parts = lax.all_to_all(parts, "gz", 0, 0)
     velocity, surface = call(

time: 74.7 us -> 67.3 us (0.901)
  blocking collectives: 25.2 us -> 12.9 us
  starting transfers between devices: 26.2 us -> 35.9 us
  waiting for transfers between devices: 14.4 us -> 11.1 us
  local copies, waits for them, and re-layouts: 2.46 us -> 0 us
  Pallas kernels: 5.14 us -> 6.33 us
    all_to_all x1, blocking collectives: 25.2 us -> 12.9 us  [local(): parts = lax.all_to_all(parts, 'gz', 0, 0)]
    all_to_all x1, starting transfers between devices: 7.02 us -> 13.6 us  [local(): sums = lax.all_to_all(sums.reshape(group, 1, 128), ('gx', 'gy'), 0, 0)]
    ppermute x6, waiting for transfers between devices: 8.89 us -> 3.2 us  [the longest x3 3.15 us: swap(): lax.ppermute(even, axis, pairs(0))]
    ppermute x6, starting transfers between devices: 19.2 us -> 22.2 us  [the longest x3 14.1 us: swap(): lax.ppermute(even, axis, pairs(0))]
    all_to_all x1, waiting for transfers between devices: 5.47 us -> 7.88 us  [local(): sums = lax.all_to_all(sums.reshape(group, 1, 128), ('gx', 'gy'), 0, 0)]
    pallas_call x0 -> x1, Pallas kernels: none -> 1.2 us  [local(): pl.pallas_call(fetch, out_shape=[jax.ShapeDtypeStruct((4, 2, 8, 128), f32...]
    unnamed x8 -> x0, local copies, waits for them, and re-layouts: 0.91 us -> none
    squeeze x1 -> x0, local copies, waits for them, and re-layouts: 0.78 us -> none  [layers(): body_force[c, start:start + 2]]
  transfers between devices with their start and end apart: 7 -> 7, of which waited for: 4 -> 4; matrix products, arithmetic and copies ran while one was open for 0% -> 0% of each run, Pallas kernels for 2% -> 3%
where the time goes in v3:
time: 67.3 us; the launch traced here: 66.9 us
  starting transfers between devices  35.9 us (53%)
  blocking collectives  12.9 us (19%)
  waiting for transfers between devices  11.1 us (16%)
  Pallas kernels  6.33 us (9%)
  between operations  0.73 us (1%)
    ppermute x3, starting transfers between devices, swap(): lax.ppermute(even, axis, pairs(0))  14.1 us
    all_to_all x1, starting transfers between devices, local(): sums = lax.all_to_all(sums.reshape(group, 1, 128), ('gx', 'gy'), 0, 0)  13.6 us
    all_to_all x1, blocking collectives, local(): parts = lax.all_to_all(parts, 'gz', 0, 0)  12.9 us
    ppermute x3, starting transfers between devices, swap(): lax.ppermute(odd, axis, pairs(1))  8.18 us
    all_to_all x1, waiting for transfers between devices, local(): sums = lax.all_to_all(sums.reshape(group, 1, 128), ('gx', 'gy'), 0, 0)  7.88 us
    pallas_call x7, Pallas kernels, call(): pl.pallas_call(body, out_shape=[jax.ShapeDtypeStruct(s, f32) for s in out...  5.14 us
    ppermute x3, waiting for transfers between devices, swap(): lax.ppermute(even, axis, pairs(0))  3.15 us
  transfers between devices with their start and end apart: 7, of which 4 were waited for; matrix products, arithmetic and copies ran while one was open for 0% of the time, Pallas kernels for 3%

profile of v3, /device:TPU:1, one launch (start us, length us, event | category | flops | bytes accessed | tf_op | source)
XLA Modules:
  0.0 66.9 jit_solution(7912615733053614267)
XLA Ops:
  0.6 1.2 %shard_map.59 = (f32[4,2,8,128]{3,2,1,0:T(8,128)S(1)}, f32[4,2,8,128]{3,2,1,0:T(8,128)S(1)}, f32[3,8,8,128]{3,2,1,0:T(8,128)S(1)}, f32[8,8,128]{2,1,0:T(8,128)S(...) custom-call(f32[3,8,8,128]{3,2,1,0:T(8,128)} %force_ref.1, f32[8,8,128]{2,1,0:T(8,128)} %visc_ref.1, ...), custom_call_target="tpu_custom_call" | custom-call | tf_op jit(solution)/shard_map/pallas_call | solution.py:335
  1.8 0.7 collective-permute-start
  2.5 6.6 %collective-permute-start.1 = (f32[4,2,8,128]{3,2,1,0:T(8,128)S(1)}, f32[4,2,8,128]{3,2,1,0:T(8,128)S(1)}, u32[]{:S(2)}, u32[]{:S(2)}) collective-permute-start(f32[4,2,8,128]{3,2,1,0:T(8,128)S(1)} %get-tuple-element.33), channel_id=1, source_target_pairs={{0,1},{1,0},{2,3},{3,2},{4,5},{5,4},{6,7},{7,6},{8,9},{9,8},{10,11... | collective-permute-start | bytes 98312 | tf_op jit(solution)/shard_map/ppermute | solution.py:330
  9.1 0.3 shard_map.60
  9.4 0.0 collective-permute-done.odd_ref
  9.4 1.0 %collective-permute-done.1.even_ref = f32[4,2,8,128]{3,2,1,0:T(8,128)S(1)} collective-permute-done((f32[4,2,8,128]{3,2,1,0:T(8,128)S(1)}, f32[4,2,8,128]{3,2,1,0:T(8,128)S(1)}, u32[]{:S(2)}, u32[]{:S(2)}) %collective-permute-start.1) | collective-permute-done | bytes 32800 | tf_op jit(solution)/shard_map/ppermute | solution.py:330
  10.4 0.2 shard_map.61
  10.5 0.7 collective-permute-start.2
  11.2 5.6 %collective-permute-start.3 = (f32[2,8,128]{2,1,0:T(8,128)S(1)}, f32[2,8,128]{2,1,0:T(8,128)S(1)}, u32[]{:S(2)}, u32[]{:S(2)}) collective-permute-start(f32[2,8,128]{2,1,0:T(8,128)S(1)} %get-tuple-element.38), channel_id=1, source_target_pairs={{0,8},{8,0},{16,24},{24,16},{32,40},{40,32},{48,56},{56,48},{64,72... | collective-permute-start | bytes 24584 | tf_op jit(solution)/shard_map/ppermute | solution.py:330
  16.8 0.0 collective-permute-done.2.odd_ref
  16.8 1.0 %collective-permute-done.3.even_ref = f32[2,8,128]{2,1,0:T(8,128)S(1)} collective-permute-done((f32[2,8,128]{2,1,0:T(8,128)S(1)}, f32[2,8,128]{2,1,0:T(8,128)S(1)}, u32[]{:S(2)}, u32[]{:S(2)}) %collective-permute-start.3) | collective-permute-done | bytes 8224 | tf_op jit(solution)/shard_map/ppermute | solution.py:330
  17.8 0.1 shard_map.62
  17.9 6.9 %collective-permute-start.4 = (f32[136,128]{1,0:T(8,128)S(1)}, f32[136,128]{1,0:T(8,128)S(1)}, u32[]{:S(2)}, u32[]{:S(2)}) collective-permute-start(f32[136,128]{1,0:T(8,128)S(1)} %get-tuple-element.43), channel_id=1, source_target_pairs={{128,256},{256,128},{129,257},{257,129},{130,258},{258,130},{131,2... | collective-permute-start | bytes 208904 | tf_op jit(solution)/shard_map/ppermute | solution.py:330
  24.8 1.9 %collective-permute-start.5 = (f32[136,128]{1,0:T(8,128)S(1)}, f32[136,128]{1,0:T(8,128)S(1)}, u32[]{:S(2)}, u32[]{:S(2)}) collective-permute-start(f32[136,128]{1,0:T(8,128)S(1)} %get-tuple-element.44), channel_id=1, source_target_pairs={{0,128},{128,0},{256,384},{384,256},{1,129},{129,1},{257,385},{385... | collective-permute-start | bytes 208904 | tf_op jit(solution)/shard_map/ppermute | solution.py:330
  26.7 0.1 collective-permute-done.4.odd_ref
  26.8 1.2 %collective-permute-done.5.even_ref = f32[136,128]{1,0:T(8,128)S(1)} collective-permute-done((f32[136,128]{1,0:T(8,128)S(1)}, f32[136,128]{1,0:T(8,128)S(1)}, u32[]{:S(2)}, u32[]{:S(2)}) %collective-permute-start.5) | collective-permute-done | bytes 69664 | tf_op jit(solution)/shard_map/ppermute | solution.py:330
  28.0 2.2 %shard_map.63 = (f32[3,8,8,128]{3,2,1,0:T(8,128)S(1)}, f32[64,128]{1,0:T(8,128)}, f32[2,8,128]{2,1,0:T(8,128)S(1)}) custom-call(f32[48,8,128]{2,1,0:T(8,128)S(1)} %get-tuple-element.36.planes_ref, f32[2,8,128]{2,1,0:T(8,128)S(1)} %get-tuple-element.41.rl_ref, f32[2,8,128]{2,1,0:T(8,128)S(1)} %get-tuple-element.42.rr_ref, ...), custom_call_target="tpu_custom_call" | custom-call | flops 20480000 | bytes 262144 | tf_op jit(solution)/shard_map/pallas_call | solution.py:29
  30.1 13.6 %all-to-all-start = ((f32[64,1,128]{2,1,0:T(1,128)}), f32[64,1,128]{2,1,0:T(1,128)S(1)}, u32[]{:S(2)}, u32[]{:S(2)}) async-start(f32[64,1,128]{2,1,0:T(1,128)} %bitcast.1), calls=%async_computation | async-start | bytes 65536 | tf_op jit(solution)/shard_map/all_to_all | solution.py:374
  43.8 1.4 %shard_map.64.height_ref = f32[64,128]{1,0:T(8,128)S(1)} custom-call(f32[64,256]{1,0:T(8,128)S(1)} %get-tuple-element.46.height_ref, f32[64,256]{1,0:T(8,128)S(1)} %get-tuple-element.47.conduct_ref, f32[136,128]{1,0:T(8,128)S(1)} %collective-permute-done.4.odd_ref, f32[136,128]{1,0:T(8,128)S(1)} %collective-permute-done.5.even_ref), custom_call_target="tpu_custom_call" | custom-call | flops 20480000 | bytes 262144 | tf_op jit(solution)/shard_map/pallas_call | solution.py:29
  45.2 7.9 %all-to-all-done = f32[64,1,128]{2,1,0:T(1,128)S(1)} async-done(((f32[64,1,128]{2,1,0:T(1,128)}), f32[64,1,128]{2,1,0:T(1,128)S(1)}, u32[]{:S(2)}, u32[]{:S(2)}) %all-to-all-start) | async-done | bytes 32800 | tf_op jit(solution)/shard_map/all_to_all | solution.py:374
  53.1 0.1 shard_map.65
  53.1 12.9 %all_to_all.10.parts_ref = f32[8,8,128]{2,1,0:T(8,128)S(1)} all-to-all(f32[8,8,128]{2,1,0:T(8,128)S(1)} %shard_map.65), channel_id=1, replica_groups=mesh['gx'=4,'gy'=16,'gz'=8] {'gz'}, dimensions={0} | all-to-all | bytes 65536 | tf_op jit(solution)/shard_map/all_to_all | solution.py:377
  66.1 0.9 %shard_map.66 = (f32[3,8,8,128]{3,2,1,0:T(8,128)}, f32[64,128]{1,0:T(8,128)}) custom-call(f32[8,8,128]{2,1,0:T(8,128)S(1)} %all_to_all.10.parts_ref, f32[48,8,128]{2,1,0:T(8,128)S(1)} %get-tuple-element.36.planes_ref, f32[3,8,8,128]{3,2,1,0:T(8,128)S(1)} %get-tuple-element.50.image_ref, f32[64,128]{1,0:T(8,128)S(1)} %shard_map.64.height_ref), custom_call_target="tpu_custom_call" | custom-call | flops 20480000 | bytes 262144 | tf_op jit(solution)/shard_map/pallas_call | solution.py:29
Async XLA Ops:
  1.8 7.6 %collective-permute-start = (f32[4,2,8,128]{3,2,1,0:T(8,128)S(1)}, f32[4,2,8,128]{3,2,1,0:T(8,128)S(1)}, u32[]{:S(2)}, u32[]{:S(2)}) collective-permute-start(f32[4,2,8,128]{3,2,1,0:T(8,128)S(1)} %get-tuple-element.32), channel_id=1, source_target_pairs={{1,2},{2,1},{3,4},{4,3},{5,6},{6,5},{9,10},{10,9},{11,12},{12,11},... | collective-permute-start | bytes 98312 | tf_op jit(solution)/shard_map/ppermute | solution.py:330
  2.5 7.9 %collective-permute-start.1 = (f32[4,2,8,128]{3,2,1,0:T(8,128)S(1)}, f32[4,2,8,128]{3,2,1,0:T(8,128)S(1)}, u32[]{:S(2)}, u32[]{:S(2)}) collective-permute-start(f32[4,2,8,128]{3,2,1,0:T(8,128)S(1)} %get-tuple-element.33), channel_id=1, source_target_pairs={{0,1},{1,0},{2,3},{3,2},{4,5},{5,4},{6,7},{7,6},{8,9},{9,8},{10,11... | collective-permute-start | bytes 98312 | tf_op jit(solution)/shard_map/ppermute | solution.py:330
  10.5 6.3 %collective-permute-start.2 = (f32[2,8,128]{2,1,0:T(8,128)S(1)}, f32[2,8,128]{2,1,0:T(8,128)S(1)}, u32[]{:S(2)}, u32[]{:S(2)}) collective-permute-start(f32[2,8,128]{2,1,0:T(8,128)S(1)} %get-tuple-element.37), channel_id=1, source_target_pairs={{8,16},{16,8},{24,32},{32,24},{40,48},{48,40},{56,64},{64,56},{72,... | collective-permute-start | bytes 24584 | tf_op jit(solution)/shard_map/ppermute | solution.py:330
  11.2 6.6 %collective-permute-start.3 = (f32[2,8,128]{2,1,0:T(8,128)S(1)}, f32[2,8,128]{2,1,0:T(8,128)S(1)}, u32[]{:S(2)}, u32[]{:S(2)}) collective-permute-start(f32[2,8,128]{2,1,0:T(8,128)S(1)} %get-tuple-element.38), channel_id=1, source_target_pairs={{0,8},{8,0},{16,24},{24,16},{32,40},{40,32},{48,56},{56,48},{64,72... | collective-permute-start | bytes 24584 | tf_op jit(solution)/shard_map/ppermute | solution.py:330
  17.9 8.8 %collective-permute-start.4 = (f32[136,128]{1,0:T(8,128)S(1)}, f32[136,128]{1,0:T(8,128)S(1)}, u32[]{:S(2)}, u32[]{:S(2)}) collective-permute-start(f32[136,128]{1,0:T(8,128)S(1)} %get-tuple-element.43), channel_id=1, source_target_pairs={{128,256},{256,128},{129,257},{257,129},{130,258},{258,130},{131,2... | collective-permute-start | bytes 208904 | tf_op jit(solution)/shard_map/ppermute | solution.py:330
  24.8 3.2 %collective-permute-start.5 = (f32[136,128]{1,0:T(8,128)S(1)}, f32[136,128]{1,0:T(8,128)S(1)}, u32[]{:S(2)}, u32[]{:S(2)}) collective-permute-start(f32[136,128]{1,0:T(8,128)S(1)} %get-tuple-element.44), channel_id=1, source_target_pairs={{0,128},{128,0},{256,384},{384,256},{1,129},{129,1},{257,385},{385... | collective-permute-start | bytes 208904 | tf_op jit(solution)/shard_map/ppermute | solution.py:330
  30.1 22.9 %all-to-all-start = ((f32[64,1,128]{2,1,0:T(1,128)}), f32[64,1,128]{2,1,0:T(1,128)S(1)}, u32[]{:S(2)}, u32[]{:S(2)}) async-start(f32[64,1,128]{2,1,0:T(1,128)} %bitcast.1), calls=%async_computation | async-start | bytes 65536 | tf_op jit(solution)/shard_map/all_to_all | solution.py:374

commit v4 on v3

--- a/solution.py
+++ b/solution.py
@@ -92,14 +92,13 @@
     return lax.rem(lax.axis_index(axis), 2) == 0
 
 
-def fetch(force_ref, visc_ref, topo_ref, kappa_ref, odd_ref, even_ref, force_out, visc_out, topo_out, kappa_out, sems):
+def fetch(force_ref, visc_ref, odd_ref, even_ref, sems):
     depth = visc_ref.shape[0]
     start = jnp.where(is_even("gz"), 0, depth - 2)
     moves = []
     for target, first in ((odd_ref, start), (even_ref, depth - 2 - start)):
         moves.append((force_ref.at[:, pl.ds(first, 2)], target.at[0:3]))
         moves.append((visc_ref.at[pl.ds(first, 2)], target.at[3]))
-    moves += [(force_ref, force_out), (visc_ref, visc_out), (topo_ref, topo_out), (kappa_ref, kappa_out)]
     copies = [pltpu.make_async_copy(source, target, sems.at[i]) for i, (source, target) in enumerate(moves)]
     for copy in copies:
         copy.start()
@@ -199,7 +198,28 @@
     return before, after
 
 
-def operate(planes_ref, rl_ref, rr_ref, odd_ref, even_ref, image_ref, sums_ref, top_ref, x, w, diag):
+def steps(h, k):
+    rows = h.shape[0]
+    inside = k > 0.0
+    along = 0.5 * (k + rolled(k, 255, 1))
+    across = 0.5 * (k + rolled(k, rows - 1, 0))
+    for step in range(STEPS):
+        s = rolled(h, 255, 1) - h
+        q = along * s * lax.rsqrt(1.0 + s * s)
+        t = rolled(h, rows - 1, 0) - h
+        r = across * t * lax.rsqrt(1.0 + t * t)
+        change = (q - rolled(q, 1, 1)) + (r - rolled(r, 1, 0))
+        h = jnp.where(inside, h + TIME_STEP * change, 0.0)
+    return h
+
+
+def inner_rows(height_ref, conduct_ref, out_ref):
+    out_ref[...] = steps(height_ref[...], conduct_ref[...])[8:56, 0:128]
+
+
+def operate(
+    planes_ref, rl_ref, rr_ref, odd_ref, even_ref, height_ref, conduct_ref, inner_ref, image_ref, sums_ref, top_ref, out_ref, x, w, diag
+):
     lane = lanes((8, 128))
     row = lax.broadcasted_iota(jnp.int32, (8, 128), 0)
     pad = jnp.zeros((4, 128), f32)
@@ -209,6 +229,16 @@
         rows = slice(start, start + 2)
         return jnp.concatenate([after(rows), pad, before(rows)], axis=0)
 
+    def banded(source, base):
+        def joined(side):
+            return jnp.concatenate([side(slice(base, base + 8)), side(slice(base + 8, base + 16))], axis=1)
+
+        return jnp.concatenate([source[48:64, :], joined(after), joined(before), source[0:16, :]], axis=0)
+
+    band = steps(banded(height_ref, SURFACE_ROW), banded(conduct_ref, SURFACE_ROW + 16))
+    out_ref[0:8, :] = band[32:40, 0:128]
+    out_ref[8:56, :] = inner_ref[...]
+    out_ref[56:64, :] = band[8:16, 0:128]
     lower_l = around(PAIRS_ROW)
     lower_r = around(PAIRS_ROW + 2)
     for p in range(PLANES):
@@ -252,30 +282,6 @@
     top_ref[1] = w[p, 0:8, 0:128]
 
 
-def diffuse(height_ref, conduct_ref, odd_ref, even_ref, out_ref):
-    before, after = sided(odd_ref, even_ref, "gx")
-
-    def extended(source, base):
-        def joined(side):
-            return jnp.concatenate([side(slice(base, base + 8)), side(slice(base + 8, base + 16))], axis=1)
-
-        return jnp.concatenate([source[...], joined(after), joined(before)], axis=0)
-
-    h = extended(height_ref, SURFACE_ROW)
-    k = extended(conduct_ref, SURFACE_ROW + 16)
-    inside = k > 0.0
-    along = 0.5 * (k + rolled(k, 255, 1))
-    across = 0.5 * (k + rolled(k, 79, 0))
-    for step in range(STEPS):
-        s = rolled(h, 255, 1) - h
-        q = along * s * lax.rsqrt(1.0 + s * s)
-        t = rolled(h, 79, 0) - h
-        r = across * t * lax.rsqrt(1.0 + t * t)
-        change = (q - rolled(q, 1, 1)) + (r - rolled(r, 1, 0))
-        h = jnp.where(inside, h + TIME_STEP * change, 0.0)
-    out_ref[...] = h[0:64, 0:128]
-
-
 def middle(sums_ref, top_ref, out_ref):
     lane = lanes((8, 128))
     part = jnp.sum(sums_ref[...], axis=0, keepdims=True)
@@ -331,16 +337,14 @@
 
 
 def local(body_force, viscosity, topography, kappa):
-    inputs = (body_force, viscosity, topography, kappa)
-    odd, even, body_force, viscosity, topography, kappa = pl.pallas_call(
+    odd, even = pl.pallas_call(
         fetch,
-        out_shape=[jax.ShapeDtypeStruct((4, 2, 8, 128), f32)] * 2
-        + [jax.ShapeDtypeStruct(x.shape, x.dtype) for x in inputs],
-        in_specs=[pl.BlockSpec(memory_space=pltpu.HBM)] * 4,
-        out_specs=[vmem()] * 6,
-        scratch_shapes=[pltpu.SemaphoreType.DMA((8,))],
-        compiler_params=pltpu.CompilerParams(vmem_limit_bytes=4 << 20),
-    )(*[pltpu.with_memory_space_constraint(x, pltpu.HBM) for x in inputs])
+        out_shape=[jax.ShapeDtypeStruct((4, 2, 8, 128), f32)] * 2,
+        in_specs=[pl.BlockSpec(memory_space=pltpu.HBM)] * 2,
+        out_specs=[vmem()] * 2,
+        scratch_shapes=[pltpu.SemaphoreType.DMA((4,))],
+        compiler_params=pltpu.CompilerParams(vmem_limit_bytes=1 << 20),
+    )(*[pltpu.with_memory_space_constraint(x, pltpu.HBM) for x in (body_force, viscosity)])
     odd, even = swap(odd, even, "gz")
     load, height, conduct, left, right = call(
         surface_own,
@@ -360,19 +364,18 @@
     )
     odd, even = swap(odd, even, "gx")
     group = lax.axis_size("gx") * lax.axis_size("gy")
-    image, sums, top = call(
+    (inner,) = call(inner_rows, [(48, 128)], (height, conduct))
+    image, sums, top, height = call(
         operate,
-        [(3, 8, 8, 128), (group, 128), (2, 8, 128)],
-        (planes, from_left, from_right, odd, even),
+        [(3, 8, 8, 128), (group, 128), (2, 8, 128), (64, 128)],
+        (planes, from_left, from_right, odd, even, height, conduct, inner),
         [
             pltpu.VMEM((PLANES, 16, 256), f32),
             pltpu.VMEM((3 * DEPTHS, 16, 256), f32),
             pltpu.VMEM((DEPTHS, 8, 128), f32),
         ],
     )
-    (height,) = call(diffuse, [(64, 128)], (height, conduct, odd, even))
     sums = lax.all_to_all(sums.reshape(group, 1, 128), ("gx", "gy"), 0, 0)
-    sums, height = lax.optimization_barrier((sums, height))
     (parts,) = call(middle, [(lax.axis_size("gz"), 8, 128)], (sums.reshape(group, 128), top))
     parts = lax.all_to_all(parts, "gz", 0, 0)
     velocity, surface = call(

time: 67.3 us -> 67.3 us (level)
  blocking collectives: 12.9 us -> 36.1 us
  starting transfers between devices: 35.9 us -> 22 us
  waiting for transfers between devices: 11.1 us -> 1.03 us
  local copies, waits for them, and re-layouts: 0 us -> 1.36 us
    all_to_all x0 -> x1, blocking collectives: none -> 23.1 us  [local(): sums = lax.all_to_all(sums.reshape(group, 1, 128), ('gx', 'gy'), 0, 0)]
    all_to_all x1 -> x0, starting transfers between devices: 13.6 us -> none  [local(): sums = lax.all_to_all(sums.reshape(group, 1, 128), ('gx', 'gy'), 0, 0)]
    all_to_all x1 -> x0, waiting for transfers between devices: 7.88 us -> none  [local(): sums = lax.all_to_all(sums.reshape(group, 1, 128), ('gx', 'gy'), 0, 0)]
    ppermute x3, waiting for transfers between devices: 3.15 us -> 1.02 us  [swap(): lax.ppermute(even, axis, pairs(0))]
    unnamed x0 -> x8, local copies, waits for them, and re-layouts: none -> 1.36 us
  transfers between devices with their start and end apart: 7 -> 6, of which waited for: 4 -> 1; matrix products, arithmetic and copies ran while one was open for 0% -> 0% of each run, Pallas kernels for 3% -> 2%
where the time goes in v4:
time: 67.3 us; the launch traced here: 66.9 us
  blocking collectives  36.1 us (54%)
  starting transfers between devices  22 us (33%)
  Pallas kernels  5.66 us (8%)
  local copies, waits for them, and re-layouts  1.36 us (2%)
  waiting for transfers between devices  1.03 us (2%)
  between operations  0.8 us (1%)
    all_to_all x1, blocking collectives, local(): sums = lax.all_to_all(sums.reshape(group, 1, 128), ('gx', 'gy'), 0, 0)  23.1 us
    ppermute x3, starting transfers between devices, swap(): lax.ppermute(even, axis, pairs(0))  14.2 us
    all_to_all x1, blocking collectives, local(): parts = lax.all_to_all(parts, 'gz', 0, 0)  12.9 us
    ppermute x3, starting transfers between devices, swap(): lax.ppermute(odd, axis, pairs(1))  7.76 us
    pallas_call x7, Pallas kernels, call(): pl.pallas_call(body, out_shape=[jax.ShapeDtypeStruct(s, f32) for s in out...  4.81 us
    unnamed x8, local copies, waits for them, and re-layouts  1.36 us
  transfers between devices with their start and end apart: 6, of which 1 were waited for; matrix products, arithmetic and copies ran while one was open for 0% of the time, Pallas kernels for 2%

profile of v4, /device:TPU:1, one launch (start us, length us, event | category | flops | bytes accessed | tf_op | source)
XLA Modules:
  0.0 66.9 jit_solution(6236169332002185488)
XLA Ops:
  0.6 0.0 copy-start.2
  0.6 0.9 %shard_map.60 = (f32[4,2,8,128]{3,2,1,0:T(8,128)S(1)}, f32[4,2,8,128]{3,2,1,0:T(8,128)S(1)}) custom-call(f32[3,8,8,128]{3,2,1,0:T(8,128)} %force_ref.3, f32[8,8,128]{2,1,0:T(8,128)} %visc_ref.3), custom_call_target="tpu_custom_call" | custom-call | tf_op jit(solution)/shard_map/pallas_call | solution.py:340
  1.5 0.7 collective-permute-start
  2.2 0.0 copy-start
  2.2 6.7 %collective-permute-start.1 = (f32[4,2,8,128]{3,2,1,0:T(8,128)S(1)}, f32[4,2,8,128]{3,2,1,0:T(8,128)S(1)}, u32[]{:S(2)}, u32[]{:S(2)}) collective-permute-start(f32[4,2,8,128]{3,2,1,0:T(8,128)S(1)} %get-tuple-element.24), channel_id=1, source_target_pairs={{0,1},{1,0},{2,3},{3,2},{4,5},{5,4},{6,7},{7,6},{8,9},{9,8},{10,11... | collective-permute-start | bytes 98312 | tf_op jit(solution)/shard_map/ppermute | solution.py:336
  8.9 0.0 copy-done.2
  8.9 0.0 copy-start.1
  8.9 0.9 %copy-done.1 = f32[64,1024]{1,0:T(8,128)S(1)} copy-done((f32[64,1024]{1,0:T(8,128)S(1)}, f32[64,1024]{1,0:T(8,128)}, u32[]{:S(2)}) %copy-start.1) | copy-done | bytes 262168
  9.9 0.0 copy-start.3
  9.9 0.3 shard_map.59
  10.2 0.0 collective-permute-done.odd_ref
  10.2 0.0 collective-permute-done.1.even_ref
  10.2 0.0 copy-done
  10.2 0.4 copy-done.3
  10.6 0.2 shard_map.61
  10.8 0.7 collective-permute-start.2
  11.4 5.6 %collective-permute-start.3 = (f32[2,8,128]{2,1,0:T(8,128)S(1)}, f32[2,8,128]{2,1,0:T(8,128)S(1)}, u32[]{:S(2)}, u32[]{:S(2)}) collective-permute-start(f32[2,8,128]{2,1,0:T(8,128)S(1)} %get-tuple-element.29), channel_id=1, source_target_pairs={{0,8},{8,0},{16,24},{24,16},{32,40},{40,32},{48,56},{56,48},{64,72... | collective-permute-start | bytes 24584 | tf_op jit(solution)/shard_map/ppermute | solution.py:336
  17.0 0.0 collective-permute-done.2.odd_ref
  17.0 1.0 %collective-permute-done.3.even_ref = f32[2,8,128]{2,1,0:T(8,128)S(1)} collective-permute-done((f32[2,8,128]{2,1,0:T(8,128)S(1)}, f32[2,8,128]{2,1,0:T(8,128)S(1)}, u32[]{:S(2)}, u32[]{:S(2)}) %collective-permute-start.3) | collective-permute-done | bytes 8224 | tf_op jit(solution)/shard_map/ppermute | solution.py:336
  18.1 0.1 shard_map.62
  18.2 6.4 %collective-permute-start.4 = (f32[136,128]{1,0:T(8,128)S(1)}, f32[136,128]{1,0:T(8,128)S(1)}, u32[]{:S(2)}, u32[]{:S(2)}) collective-permute-start(f32[136,128]{1,0:T(8,128)S(1)} %get-tuple-element.34), channel_id=1, source_target_pairs={{128,256},{256,128},{129,257},{257,129},{130,258},{258,130},{131,2... | collective-permute-start | bytes 208904 | tf_op jit(solution)/shard_map/ppermute | solution.py:336
  24.6 1.9 %collective-permute-start.5 = (f32[136,128]{1,0:T(8,128)S(1)}, f32[136,128]{1,0:T(8,128)S(1)}, u32[]{:S(2)}, u32[]{:S(2)}) collective-permute-start(f32[136,128]{1,0:T(8,128)S(1)} %get-tuple-element.35), channel_id=1, source_target_pairs={{0,128},{128,0},{256,384},{384,256},{1,129},{129,1},{257,385},{385... | collective-permute-start | bytes 208904 | tf_op jit(solution)/shard_map/ppermute | solution.py:336
  26.5 1.3 %shard_map.63.inner_ref = f32[48,128]{1,0:T(8,128)S(1)} custom-call(f32[64,256]{1,0:T(8,128)S(1)} %get-tuple-element.36.height_ref, f32[64,256]{1,0:T(8,128)S(1)} %get-tuple-element.37.conduct_ref), custom_call_target="tpu_custom_call" | custom-call | flops 20480000 | bytes 262144 | tf_op jit(solution)/shard_map/pallas_call | solution.py:29
  27.9 0.0 collective-permute-done.4.odd_ref
  27.9 0.0 collective-permute-done.5.even_ref
  27.9 1.9 %shard_map.64 = (f32[3,8,8,128]{3,2,1,0:T(8,128)S(1)}, f32[64,128]{1,0:T(8,128)S(1)}, f32[2,8,128]{2,1,0:T(8,128)S(1)}, f32[64,128]{1,0:T(8,128)S(1)}) custom-call(f32[48,8,128]{2,1,0:T(8,128)S(1)} %get-tuple-element.27.planes_ref, f32[2,8,128]{2,1,0:T(8,128)S(1)} %get-tuple-element.32.rl_ref, f32[2,8,128]{2,1,0:T(8,128)S(1)} %get-tuple-element.33.rr_ref, ...), custom_call_target="tpu_custom_call" | custom-call | flops 20480000 | bytes 262144 | tf_op jit(solution)/shard_map/pallas_call | solution.py:29
  29.8 23.1 %all_to_all.10 = f32[64,1,128]{2,1,0:T(1,128)S(1)} all-to-all(f32[64,1,128]{2,1,0:T(1,128)S(1)} %bitcast.4), channel_id=1, replica_groups=mesh['gx'=4,'gy'=16,'gz'=8] {'gx','gy'}, dimensions={0} | all-to-all | bytes 65536 | tf_op jit(solution)/shard_map/all_to_all | solution.py:378
  53.0 0.1 shard_map.65
  53.0 12.9 %all_to_all.11.parts_ref = f32[8,8,128]{2,1,0:T(8,128)S(1)} all-to-all(f32[8,8,128]{2,1,0:T(8,128)S(1)} %shard_map.65), channel_id=1, replica_groups=mesh['gx'=4,'gy'=16,'gz'=8] {'gz'}, dimensions={0} | all-to-all | bytes 65536 | tf_op jit(solution)/shard_map/all_to_all | solution.py:380
  66.0 0.9 %shard_map.66 = (f32[3,8,8,128]{3,2,1,0:T(8,128)}, f32[64,128]{1,0:T(8,128)}) custom-call(f32[8,8,128]{2,1,0:T(8,128)S(1)} %all_to_all.11.parts_ref, f32[48,8,128]{2,1,0:T(8,128)S(1)} %get-tuple-element.27.planes_ref, f32[3,8,8,128]{3,2,1,0:T(8,128)S(1)} %get-tuple-element.40.image_ref, f32[64,128]{1,0:T(8,128)S(1)} %get-tuple-element.41.height_ref), custom_call_target="tpu_custom_call" | custom-call | flops 20480000 | bytes 262144 | tf_op jit(solution)/shard_map/pallas_call | solution.py:29
Async XLA Ops:
  0.6 8.3 %copy-start.2 = (bf16[64,1024]{1,0:T(8,128)(2,1)S(1)}, bf16[64,1024]{1,0:T(8,128)(2,1)}, u32[]{:S(2)}) copy-start(bf16[64,1024]{1,0:T(8,128)(2,1)} %kappa_ref.1) | copy-start | bytes 393220
  1.5 8.7 %collective-permute-start = (f32[4,2,8,128]{3,2,1,0:T(8,128)S(1)}, f32[4,2,8,128]{3,2,1,0:T(8,128)S(1)}, u32[]{:S(2)}, u32[]{:S(2)}) collective-permute-start(f32[4,2,8,128]{3,2,1,0:T(8,128)S(1)} %get-tuple-element.23), channel_id=1, source_target_pairs={{1,2},{2,1},{3,4},{4,3},{5,6},{6,5},{9,10},{10,9},{11,12},{12,11},... | collective-permute-start | bytes 98312 | tf_op jit(solution)/shard_map/ppermute | solution.py:336
  2.2 8.0 %copy-start = (f32[3,8,8,128]{3,2,1,0:T(8,128)S(1)}, f32[3,8,8,128]{3,2,1,0:T(8,128)}, u32[]{:S(2)}) copy-start(f32[3,8,8,128]{3,2,1,0:T(8,128)} %force_ref.3) | copy-start | bytes 294916
  2.2 8.0 %collective-permute-start.1 = (f32[4,2,8,128]{3,2,1,0:T(8,128)S(1)}, f32[4,2,8,128]{3,2,1,0:T(8,128)S(1)}, u32[]{:S(2)}, u32[]{:S(2)}) collective-permute-start(f32[4,2,8,128]{3,2,1,0:T(8,128)S(1)} %get-tuple-element.24), channel_id=1, source_target_pairs={{0,1},{1,0},{2,3},{3,2},{4,5},{5,4},{6,7},{7,6},{8,9},{9,8},{10,11... | collective-permute-start | bytes 98312 | tf_op jit(solution)/shard_map/ppermute | solution.py:336
  8.9 1.0 %copy-start.1 = (f32[64,1024]{1,0:T(8,128)S(1)}, f32[64,1024]{1,0:T(8,128)}, u32[]{:S(2)}) copy-start(f32[64,1024]{1,0:T(8,128)} %topo_ref.1) | copy-start | bytes 786436
  9.9 0.8 %copy-start.3 = (f32[8,8,128]{2,1,0:T(8,128)S(1)}, f32[8,8,128]{2,1,0:T(8,128)}, u32[]{:S(2)}) copy-start(f32[8,8,128]{2,1,0:T(8,128)} %visc_ref.3) | copy-start | bytes 98308
  10.8 6.3 %collective-permute-start.2 = (f32[2,8,128]{2,1,0:T(8,128)S(1)}, f32[2,8,128]{2,1,0:T(8,128)S(1)}, u32[]{:S(2)}, u32[]{:S(2)}) collective-permute-start(f32[2,8,128]{2,1,0:T(8,128)S(1)} %get-tuple-element.28), channel_id=1, source_target_pairs={{8,16},{16,8},{24,32},{32,24},{40,48},{48,40},{56,64},{64,56},{72,... | collective-permute-start | bytes 24584 | tf_op jit(solution)/shard_map/ppermute | solution.py:336
  11.4 6.6 %collective-permute-start.3 = (f32[2,8,128]{2,1,0:T(8,128)S(1)}, f32[2,8,128]{2,1,0:T(8,128)S(1)}, u32[]{:S(2)}, u32[]{:S(2)}) collective-permute-start(f32[2,8,128]{2,1,0:T(8,128)S(1)} %get-tuple-element.29), channel_id=1, source_target_pairs={{0,8},{8,0},{16,24},{24,16},{32,40},{40,32},{48,56},{56,48},{64,72... | collective-permute-start | bytes 24584 | tf_op jit(solution)/shard_map/ppermute | solution.py:336
  18.2 9.7 %collective-permute-start.4 = (f32[136,128]{1,0:T(8,128)S(1)}, f32[136,128]{1,0:T(8,128)S(1)}, u32[]{:S(2)}, u32[]{:S(2)}) collective-permute-start(f32[136,128]{1,0:T(8,128)S(1)} %get-tuple-element.34), channel_id=1, source_target_pairs={{128,256},{256,128},{129,257},{257,129},{130,258},{258,130},{131,2... | collective-permute-start | bytes 208904 | tf_op jit(solution)/shard_map/ppermute | solution.py:336
  24.6 3.3 %collective-permute-start.5 = (f32[136,128]{1,0:T(8,128)S(1)}, f32[136,128]{1,0:T(8,128)S(1)}, u32[]{:S(2)}, u32[]{:S(2)}) collective-permute-start(f32[136,128]{1,0:T(8,128)S(1)} %get-tuple-element.35), channel_id=1, source_target_pairs={{0,128},{128,0},{256,384},{384,256},{1,129},{129,1},{257,385},{385... | collective-permute-start | bytes 208904 | tf_op jit(solution)/shard_map/ppermute | solution.py:336

commit v5 on v4

--- a/solution.py
+++ b/solution.py
@@ -213,12 +213,8 @@
     return h
 
 
-def inner_rows(height_ref, conduct_ref, out_ref):
-    out_ref[...] = steps(height_ref[...], conduct_ref[...])[8:56, 0:128]
-
-
 def operate(
-    planes_ref, rl_ref, rr_ref, odd_ref, even_ref, height_ref, conduct_ref, inner_ref, image_ref, sums_ref, top_ref, out_ref, x, w, diag
+    planes_ref, rl_ref, rr_ref, odd_ref, even_ref, height_ref, conduct_ref, image_ref, sums_ref, top_ref, out_ref, x, w, diag
 ):
     lane = lanes((8, 128))
     row = lax.broadcasted_iota(jnp.int32, (8, 128), 0)
@@ -229,16 +225,14 @@
         rows = slice(start, start + 2)
         return jnp.concatenate([after(rows), pad, before(rows)], axis=0)
 
-    def banded(source, base):
+    def extended(source, base):
         def joined(side):
             return jnp.concatenate([side(slice(base, base + 8)), side(slice(base + 8, base + 16))], axis=1)
 
-        return jnp.concatenate([source[48:64, :], joined(after), joined(before), source[0:16, :]], axis=0)
-
-    band = steps(banded(height_ref, SURFACE_ROW), banded(conduct_ref, SURFACE_ROW + 16))
-    out_ref[0:8, :] = band[32:40, 0:128]
-    out_ref[8:56, :] = inner_ref[...]
-    out_ref[56:64, :] = band[8:16, 0:128]
+        return jnp.concatenate([source[...], joined(after), joined(before)], axis=0)
+
+    stepped = steps(extended(height_ref, SURFACE_ROW), extended(conduct_ref, SURFACE_ROW + 16))
+    out_ref[...] = stepped[0:64, 0:128]
     lower_l = around(PAIRS_ROW)
     lower_r = around(PAIRS_ROW + 2)
     for p in range(PLANES):
@@ -364,11 +358,10 @@
     )
     odd, even = swap(odd, even, "gx")
     group = lax.axis_size("gx") * lax.axis_size("gy")
-    (inner,) = call(inner_rows, [(48, 128)], (height, conduct))
     image, sums, top, height = call(
         operate,
         [(3, 8, 8, 128), (group, 128), (2, 8, 128), (64, 128)],
-        (planes, from_left, from_right, odd, even, height, conduct, inner),
+        (planes, from_left, from_right, odd, even, height, conduct),
         [
             pltpu.VMEM((PLANES, 16, 256), f32),
             pltpu.VMEM((3 * DEPTHS, 16, 256), f32),

time: 67.3 us -> 67.1 us (level)
  waiting for transfers between devices: 1.03 us -> 2.25 us
  Pallas kernels: 5.66 us -> 4.56 us
    ppermute x3, waiting for transfers between devices: 1.02 us -> 2.19 us  [swap(): lax.ppermute(even, axis, pairs(0))]
    pallas_call x7 -> x6, Pallas kernels: 4.81 us -> 3.7 us  [call(): pl.pallas_call(body, out_shape=[jax.ShapeDtypeStruct(s, f32) for s in out...]
  transfers between devices with their start and end apart: 6 -> 6, of which waited for: 1 -> 2; matrix products, arithmetic and copies ran while one was open for 0% -> 0% of each run, Pallas kernels for 2% -> 0%
where the time goes in v5:
time: 67.1 us; the launch traced here: 66.6 us
  blocking collectives  35.7 us (53%)
  starting transfers between devices  22 us (33%)
  Pallas kernels  4.56 us (7%)
  waiting for transfers between devices  2.25 us (3%)
  local copies, waits for them, and re-layouts  1.36 us (2%)
  between operations  0.77 us (1%)
    all_to_all x1, blocking collectives, local(): sums = lax.all_to_all(sums.reshape(group, 1, 128), ('gx', 'gy'), 0, 0)  22.8 us
    ppermute x3, starting transfers between devices, swap(): lax.ppermute(even, axis, pairs(0))  14.2 us
    all_to_all x1, blocking collectives, local(): parts = lax.all_to_all(parts, 'gz', 0, 0)  12.9 us
    ppermute x3, starting transfers between devices, swap(): lax.ppermute(odd, axis, pairs(1))  7.76 us
    pallas_call x6, Pallas kernels, call(): pl.pallas_call(body, out_shape=[jax.ShapeDtypeStruct(s, f32) for s in out...  3.7 us
    ppermute x3, waiting for transfers between devices, swap(): lax.ppermute(even, axis, pairs(0))  2.19 us
    unnamed x8, local copies, waits for them, and re-layouts  1.36 us
  transfers between devices with their start and end apart: 6, of which 2 were waited for; matrix products, arithmetic and copies ran while one was open for 0% of the time, Pallas kernels for 0%

profile of v5, /device:TPU:1, one launch (start us, length us, event | category | flops | bytes accessed | tf_op | source)
XLA Modules:
  0.0 66.6 jit_solution(9707508183440876110)
XLA Ops:
  0.6 0.0 copy-start.2
  0.6 0.9 %shard_map.60 = (f32[4,2,8,128]{3,2,1,0:T(8,128)S(1)}, f32[4,2,8,128]{3,2,1,0:T(8,128)S(1)}) custom-call(f32[3,8,8,128]{3,2,1,0:T(8,128)} %force_ref.3, f32[8,8,128]{2,1,0:T(8,128)} %visc_ref.3), custom_call_target="tpu_custom_call" | custom-call | tf_op jit(solution)/shard_map/pallas_call | solution.py:334
  1.5 0.7 collective-permute-start
  2.2 0.0 copy-start
  2.2 6.7 %collective-permute-start.1 = (f32[4,2,8,128]{3,2,1,0:T(8,128)S(1)}, f32[4,2,8,128]{3,2,1,0:T(8,128)S(1)}, u32[]{:S(2)}, u32[]{:S(2)}) collective-permute-start(f32[4,2,8,128]{3,2,1,0:T(8,128)S(1)} %get-tuple-element.24), channel_id=1, source_target_pairs={{0,1},{1,0},{2,3},{3,2},{4,5},{5,4},{6,7},{7,6},{8,9},{9,8},{10,11... | collective-permute-start | bytes 98312 | tf_op jit(solution)/shard_map/ppermute | solution.py:330
  8.9 0.0 copy-done.2
  8.9 0.0 copy-start.1
  8.9 0.9 %copy-done.1 = f32[64,1024]{1,0:T(8,128)S(1)} copy-done((f32[64,1024]{1,0:T(8,128)S(1)}, f32[64,1024]{1,0:T(8,128)}, u32[]{:S(2)}) %copy-start.1) | copy-done | bytes 262168
  9.9 0.0 copy-start.3
  9.9 0.3 shard_map.59
  10.2 0.0 collective-permute-done.odd_ref
  10.2 0.0 collective-permute-done.1.even_ref
  10.2 0.0 copy-done
  10.2 0.4 copy-done.3
  10.6 0.2 shard_map.61
  10.8 0.7 collective-permute-start.2
  11.4 5.6 %collective-permute-start.3 = (f32[2,8,128]{2,1,0:T(8,128)S(1)}, f32[2,8,128]{2,1,0:T(8,128)S(1)}, u32[]{:S(2)}, u32[]{:S(2)}) collective-permute-start(f32[2,8,128]{2,1,0:T(8,128)S(1)} %get-tuple-element.29), channel_id=1, source_target_pairs={{0,8},{8,0},{16,24},{24,16},{32,40},{40,32},{48,56},{56,48},{64,72... | collective-permute-start | bytes 24584 | tf_op jit(solution)/shard_map/ppermute | solution.py:330
  17.0 0.0 collective-permute-done.2.odd_ref
  17.0 1.0 %collective-permute-done.3.even_ref = f32[2,8,128]{2,1,0:T(8,128)S(1)} collective-permute-done((f32[2,8,128]{2,1,0:T(8,128)S(1)}, f32[2,8,128]{2,1,0:T(8,128)S(1)}, u32[]{:S(2)}, u32[]{:S(2)}) %collective-permute-start.3) | collective-permute-done | bytes 8224 | tf_op jit(solution)/shard_map/ppermute | solution.py:330
  18.1 0.1 shard_map.62
  18.2 6.4 %collective-permute-start.4 = (f32[136,128]{1,0:T(8,128)S(1)}, f32[136,128]{1,0:T(8,128)S(1)}, u32[]{:S(2)}, u32[]{:S(2)}) collective-permute-start(f32[136,128]{1,0:T(8,128)S(1)} %get-tuple-element.34), channel_id=1, source_target_pairs={{128,256},{256,128},{129,257},{257,129},{130,258},{258,130},{131,2... | collective-permute-start | bytes 208904 | tf_op jit(solution)/shard_map/ppermute | solution.py:330
  24.6 1.9 %collective-permute-start.5 = (f32[136,128]{1,0:T(8,128)S(1)}, f32[136,128]{1,0:T(8,128)S(1)}, u32[]{:S(2)}, u32[]{:S(2)}) collective-permute-start(f32[136,128]{1,0:T(8,128)S(1)} %get-tuple-element.35), channel_id=1, source_target_pairs={{0,128},{128,0},{256,384},{384,256},{1,129},{129,1},{257,385},{385... | collective-permute-start | bytes 208904 | tf_op jit(solution)/shard_map/ppermute | solution.py:330
  26.5 0.1 collective-permute-done.4.odd_ref
  26.6 1.2 %collective-permute-done.5.even_ref = f32[136,128]{1,0:T(8,128)S(1)} collective-permute-done((f32[136,128]{1,0:T(8,128)S(1)}, f32[136,128]{1,0:T(8,128)S(1)}, u32[]{:S(2)}, u32[]{:S(2)}) %collective-permute-start.5) | collective-permute-done | bytes 69664 | tf_op jit(solution)/shard_map/ppermute | solution.py:330
  27.8 2.2 %shard_map.63 = (f32[3,8,8,128]{3,2,1,0:T(8,128)S(1)}, f32[64,128]{1,0:T(8,128)S(1)}, f32[2,8,128]{2,1,0:T(8,128)S(1)}, f32[64,128]{1,0:T(8,128)S(1)}) custom-call(f32[48,8,128]{2,1,0:T(8,128)S(1)} %get-tuple-element.27.planes_ref, f32[2,8,128]{2,1,0:T(8,128)S(1)} %get-tuple-element.32.rl_ref, f32[2,8,128]{2,1,0:T(8,128)S(1)} %get-tuple-element.33.rr_ref, ...), custom_call_target="tpu_custom_call" | custom-call | flops 20480000 | bytes 262144 | tf_op jit(solution)/shard_map/pallas_call | solution.py:29
  29.9 22.8 %all_to_all.10 = f32[64,1,128]{2,1,0:T(1,128)S(1)} all-to-all(f32[64,1,128]{2,1,0:T(1,128)S(1)} %bitcast.4), channel_id=1, replica_groups=mesh['gx'=4,'gy'=16,'gz'=8] {'gx','gy'}, dimensions={0} | all-to-all | bytes 65536 | tf_op jit(solution)/shard_map/all_to_all | solution.py:371
  52.7 0.1 shard_map.64
  52.8 12.9 %all_to_all.11.parts_ref = f32[8,8,128]{2,1,0:T(8,128)S(1)} all-to-all(f32[8,8,128]{2,1,0:T(8,128)S(1)} %shard_map.64), channel_id=1, replica_groups=mesh['gx'=4,'gy'=16,'gz'=8] {'gz'}, dimensions={0} | all-to-all | bytes 65536 | tf_op jit(solution)/shard_map/all_to_all | solution.py:373
  65.7 0.9 %shard_map.65 = (f32[3,8,8,128]{3,2,1,0:T(8,128)}, f32[64,128]{1,0:T(8,128)}) custom-call(f32[8,8,128]{2,1,0:T(8,128)S(1)} %all_to_all.11.parts_ref, f32[48,8,128]{2,1,0:T(8,128)S(1)} %get-tuple-element.27.planes_ref, f32[3,8,8,128]{3,2,1,0:T(8,128)S(1)} %get-tuple-element.40.image_ref, f32[64,128]{1,0:T(8,128)S(1)} %get-tuple-element.41.height_ref), custom_call_target="tpu_custom_call" | custom-call | flops 20480000 | bytes 262144 | tf_op jit(solution)/shard_map/pallas_call | solution.py:29
Async XLA Ops:
  0.6 8.3 %copy-start.2 = (bf16[64,1024]{1,0:T(8,128)(2,1)S(1)}, bf16[64,1024]{1,0:T(8,128)(2,1)}, u32[]{:S(2)}) copy-start(bf16[64,1024]{1,0:T(8,128)(2,1)} %kappa_ref.1) | copy-start | bytes 393220
  1.5 8.7 %collective-permute-start = (f32[4,2,8,128]{3,2,1,0:T(8,128)S(1)}, f32[4,2,8,128]{3,2,1,0:T(8,128)S(1)}, u32[]{:S(2)}, u32[]{:S(2)}) collective-permute-start(f32[4,2,8,128]{3,2,1,0:T(8,128)S(1)} %get-tuple-element.23), channel_id=1, source_target_pairs={{1,2},{2,1},{3,4},{4,3},{5,6},{6,5},{9,10},{10,9},{11,12},{12,11},... | collective-permute-start | bytes 98312 | tf_op jit(solution)/shard_map/ppermute | solution.py:330
  2.2 8.0 %copy-start = (f32[3,8,8,128]{3,2,1,0:T(8,128)S(1)}, f32[3,8,8,128]{3,2,1,0:T(8,128)}, u32[]{:S(2)}) copy-start(f32[3,8,8,128]{3,2,1,0:T(8,128)} %force_ref.3) | copy-start | bytes 294916
  2.2 8.0 %collective-permute-start.1 = (f32[4,2,8,128]{3,2,1,0:T(8,128)S(1)}, f32[4,2,8,128]{3,2,1,0:T(8,128)S(1)}, u32[]{:S(2)}, u32[]{:S(2)}) collective-permute-start(f32[4,2,8,128]{3,2,1,0:T(8,128)S(1)} %get-tuple-element.24), channel_id=1, source_target_pairs={{0,1},{1,0},{2,3},{3,2},{4,5},{5,4},{6,7},{7,6},{8,9},{9,8},{10,11... | collective-permute-start | bytes 98312 | tf_op jit(solution)/shard_map/ppermute | solution.py:330
  8.9 1.0 %copy-start.1 = (f32[64,1024]{1,0:T(8,128)S(1)}, f32[64,1024]{1,0:T(8,128)}, u32[]{:S(2)}) copy-start(f32[64,1024]{1,0:T(8,128)} %topo_ref.1) | copy-start | bytes 786436
  9.9 0.8 %copy-start.3 = (f32[8,8,128]{2,1,0:T(8,128)S(1)}, f32[8,8,128]{2,1,0:T(8,128)}, u32[]{:S(2)}) copy-start(f32[8,8,128]{2,1,0:T(8,128)} %visc_ref.3) | copy-start | bytes 98308
  10.8 6.3 %collective-permute-start.2 = (f32[2,8,128]{2,1,0:T(8,128)S(1)}, f32[2,8,128]{2,1,0:T(8,128)S(1)}, u32[]{:S(2)}, u32[]{:S(2)}) collective-permute-start(f32[2,8,128]{2,1,0:T(8,128)S(1)} %get-tuple-element.28), channel_id=1, source_target_pairs={{8,16},{16,8},{24,32},{32,24},{40,48},{48,40},{56,64},{64,56},{72,... | collective-permute-start | bytes 24584 | tf_op jit(solution)/shard_map/ppermute | solution.py:330
  11.4 6.6 %collective-permute-start.3 = (f32[2,8,128]{2,1,0:T(8,128)S(1)}, f32[2,8,128]{2,1,0:T(8,128)S(1)}, u32[]{:S(2)}, u32[]{:S(2)}) collective-permute-start(f32[2,8,128]{2,1,0:T(8,128)S(1)} %get-tuple-element.29), channel_id=1, source_target_pairs={{0,8},{8,0},{16,24},{24,16},{32,40},{40,32},{48,56},{56,48},{64,72... | collective-permute-start | bytes 24584 | tf_op jit(solution)/shard_map/ppermute | solution.py:330
  18.2 8.4 %collective-permute-start.4 = (f32[136,128]{1,0:T(8,128)S(1)}, f32[136,128]{1,0:T(8,128)S(1)}, u32[]{:S(2)}, u32[]{:S(2)}) collective-permute-start(f32[136,128]{1,0:T(8,128)S(1)} %get-tuple-element.34), channel_id=1, source_target_pairs={{128,256},{256,128},{129,257},{257,129},{130,258},{258,130},{131,2... | collective-permute-start | bytes 208904 | tf_op jit(solution)/shard_map/ppermute | solution.py:330
  24.6 3.2 %collective-permute-start.5 = (f32[136,128]{1,0:T(8,128)S(1)}, f32[136,128]{1,0:T(8,128)S(1)}, u32[]{:S(2)}, u32[]{:S(2)}) collective-permute-start(f32[136,128]{1,0:T(8,128)S(1)} %get-tuple-element.35), channel_id=1, source_target_pairs={{0,128},{128,0},{256,384},{384,256},{1,129},{129,1},{257,385},{385... | collective-permute-start | bytes 208904 | tf_op jit(solution)/shard_map/ppermute | solution.py:330

commit v6 on v5

--- a/solution.py
+++ b/solution.py
@@ -14,8 +14,8 @@
 
 DEPTHS = 12
 PLANES = 4 * DEPTHS
-PAIRS_ROW = 2 * PLANES
-SURFACE_ROW = PAIRS_ROW + 8
+COLUMN_ROW = 8 * DEPTHS
+SURFACE_ROW = COLUMN_ROW + 8
 GX_ROWS = SURFACE_ROW + 32
 
 f32 = jnp.float32
@@ -126,9 +126,10 @@
                     plane = plane + load_ref[...]
             p = field * DEPTHS + depth
             planes_ref[p] = plane
-            mask = lane // 2 == p
-            left = jnp.where(mask, rolled(plane, 2 * p), left)
-            right = jnp.where(mask, rolled(plane, 2 * p - 126), right)
+            first = 8 * depth + 2 * field
+            mask = lane // 2 == first // 2
+            left = jnp.where(mask, rolled(plane, first), left)
+            right = jnp.where(mask, rolled(plane, first - 126), right)
     rightward = is_even("gy")
     odd_out[0] = jnp.where(rightward, left, right)
     even_out[0] = jnp.where(rightward, right, left)
@@ -136,28 +137,54 @@
     even_out[1] = jnp.where(rightward, sr_ref[...], sl_ref[...])
 
 
-def prepare_rows(planes_ref, odd_ref, even_ref, height_ref, conduct_ref, odd_out, even_out, rl_ref, rr_ref, height_out, conduct_out):
+def edge_rows(planes_ref, low_ref, high_ref):
+    for depth in range(DEPTHS):
+        for field in range(4):
+            plane = planes_ref.at[field * DEPTHS + depth]
+            near = 8 * depth + field
+            low_ref[near : near + 1, :] = plane[0:1, :]
+            low_ref[near + 4 : near + 5, :] = plane[1:2, :]
+            high_ref[near : near + 1, :] = plane[7:8, :]
+            high_ref[near + 4 : near + 5, :] = plane[6:7, :]
+
+
+def prepare_rows(
+    low_ref, high_ref, own_odd, own_even, odd_ref, even_ref, height_ref, conduct_ref,
+    odd_out, even_out, column_ref, height_out, conduct_out,
+):
+    g = lax.axis_index("gz")
+    last = lax.axis_size("gz") - 1
+    lane = lanes((8, 128))
     rightward = is_even("gy")
-    for i in range(2):
-        rl_ref[i] = jnp.where(rightward, odd_ref[i], even_ref[i])
-        rr_ref[i] = jnp.where(rightward, even_ref[i], odd_ref[i])
+
+    def chosen(first, second, i):
+        return jnp.where(rightward, first[i], second[i])
+
+    before, after = chosen(odd_ref, even_ref, 0), chosen(even_ref, odd_ref, 0)
+    before_surface, after_surface = chosen(odd_ref, even_ref, 1), chosen(even_ref, odd_ref, 1)
+    side = lax.rem(lane, 2) == 0
+    levels = (
+        jnp.where(side, chosen(own_odd, own_even, 0), chosen(own_even, own_odd, 0)),
+        jnp.where(side, rolled(before, -1), rolled(after, 1)),
+        jnp.where(side, before, after),
+    )
     downward = is_even("gx")
 
     def send(rows, low, high):
         odd_out[rows, :] = jnp.where(downward, low, high)
         even_out[rows, :] = jnp.where(downward, high, low)
 
-    g = lax.axis_index("gz")
-    last = lax.axis_size("gz") - 1
-    lane = lanes((8, 128))
-    for p in range(PLANES):
-        send(slice(2 * p, 2 * p + 2), planes_ref[p, 0:2, :], planes_ref[p, 6:8, :])
-    pad = jnp.zeros((4, 128), f32)
+    for depth in range(DEPTHS):
+        rows = slice(8 * depth, 8 * depth + 8)
+        send(rows, low_ref[rows, :], high_ref[rows, :])
+    pad = [jnp.zeros((2, 128), f32)]
     send(
-        slice(PAIRS_ROW, SURFACE_ROW),
-        jnp.concatenate([rl_ref[0, 0:2, :], rr_ref[0, 0:2, :], pad], axis=0),
-        jnp.concatenate([rl_ref[0, 6:8, :], rr_ref[0, 6:8, :], pad], axis=0),
-    )
+        slice(COLUMN_ROW, SURFACE_ROW),
+        jnp.concatenate([x[0:2] for x in levels] + pad, axis=0),
+        jnp.concatenate([x[6:8] for x in levels] + pad, axis=0),
+    )
+    for i in range(3):
+        column_ref[i] = levels[i]
     slot = 0
     for index, (source, target) in enumerate(((height_ref, height_out), (conduct_ref, conduct_out))):
         base = SURFACE_ROW + 16 * index
@@ -165,8 +192,8 @@
             rows = slice(8 * r, 8 * r + 8)
             main = source[rows, 0:128]
             side = source[rows, 128:256]
-            side = jnp.where((g == 0) & (lane >= 120), rolled(rl_ref[1], 120 - 8 * slot), side)
-            side = jnp.where((g == last) & (lane < 8), rolled(rr_ref[1], -8 * slot), side)
+            side = jnp.where((g == 0) & (lane >= 120), rolled(before_surface, 120 - 8 * slot), side)
+            side = jnp.where((g == last) & (lane < 8), rolled(after_surface, -8 * slot), side)
             target[rows, 0:128] = main
             target[rows, 128:256] = side
             if r == 0:
@@ -177,13 +204,61 @@
             slot += 1
 
 
-def stencil(before, here, after):
+def weighted(before, here, after):
     outer = before + after
-    a = FACE * here + EDGE * outer
-    b = EDGE * here + CORNER * outer
-    both = a + rolled(b, 1, 0) + rolled(b, 15, 0)
-    rows = rolled(a, 1, 0) + rolled(a, 15, 0)
-    return FACE * outer + rows + rolled(both, 1, 1) + rolled(both, 255, 1)
+    return outer, FACE * here + EDGE * outer, EDGE * here + CORNER * outer
+
+
+def pair(x):
+    return rolled(x, 1, 0) + rolled(x, x.shape[0] - 1, 0)
+
+
+def lane_pair(x, lane, first, last):
+    return jnp.where(lane == 0, first, rolled(x, 1)) + jnp.where(lane == 127, last, rolled(x, 127))
+
+
+def row_pair(x, row, edge, field):
+    up = jnp.where(row == 0, rolled(edge, -field, 0), rolled(x, 1, 0))
+    return up + jnp.where(row == 7, rolled(edge, 3 - field, 0), rolled(x, 7, 0))
+
+
+def to_first(x, depth, field):
+    return rolled(x, -(8 * depth + 2 * field))
+
+
+def to_last(x, depth, field):
+    return rolled(x, 126 - (8 * depth + 2 * field))
+
+
+def spread_rows(x, row):
+    field = lax.rem(row, 4)
+    for f in range(3):
+        x = jnp.where(field == f, rolled(x, f - 3, 0), x)
+    return x
+
+
+def spread_columns(x, lane):
+    field = lax.rem(lane, 8) // 2
+    for f in range(3):
+        x = jnp.where(field == f, rolled(x, 2 * (f - 3)), x)
+    return x
+
+
+def column_sums(levels):
+    parts = [weighted(rolled(x, 8), x, rolled(x, 120)) for x in levels]
+    (_, ai, bi), (outer, an, bn), (_, af, bf) = parts
+    beside = an + pair(bn)
+    return FACE * outer + pair(an) + (ai + af) + pair(bi + bf), beside
+
+
+def beside_rows(beside, depth, row):
+    near = jnp.where(row < 4, jnp.broadcast_to(beside[15:16], (8, 128)), jnp.broadcast_to(beside[8:9], (8, 128)))
+    field = lax.rem(row, 4)
+    first, last = to_first(near, depth, 0), to_last(near, depth, 0)
+    for f in range(1, 4):
+        first = jnp.where(field == f, to_first(near, depth, f), first)
+        last = jnp.where(field == f, to_last(near, depth, f), last)
+    return first, last
 
 
 def sided(odd_ref, even_ref, axis):
@@ -214,16 +289,13 @@
 
 
 def operate(
-    planes_ref, rl_ref, rr_ref, odd_ref, even_ref, height_ref, conduct_ref, image_ref, sums_ref, top_ref, out_ref, x, w, diag
+    planes_ref, low_ref, high_ref, column_ref, odd_ref, even_ref, height_ref, conduct_ref,
+    image_ref, sums_ref, top_ref, out_ref,
 ):
     lane = lanes((8, 128))
     row = lax.broadcasted_iota(jnp.int32, (8, 128), 0)
-    pad = jnp.zeros((4, 128), f32)
+    wide = lanes((16, 128))
     before, after = sided(odd_ref, even_ref, "gx")
-
-    def around(start):
-        rows = slice(start, start + 2)
-        return jnp.concatenate([after(rows), pad, before(rows)], axis=0)
 
     def extended(source, base):
         def joined(side):
@@ -233,47 +305,83 @@
 
     stepped = steps(extended(height_ref, SURFACE_ROW), extended(conduct_ref, SURFACE_ROW + 16))
     out_ref[...] = stepped[0:64, 0:128]
-    lower_l = around(PAIRS_ROW)
-    lower_r = around(PAIRS_ROW + 2)
-    for p in range(PLANES):
-        x[p, 0:8, 0:128] = planes_ref[p]
-        x[p, 8:16, 0:128] = around(2 * p)
-        for start, l, r in ((0, rl_ref[0], rr_ref[0]), (8, lower_l, lower_r)):
-            side = jnp.where(lane < 2, rolled(r, -2 * p), 0.0)
-            side = jnp.where(lane >= 126, rolled(l, 126 - 2 * p), side)
-            x[p, start : start + 8, 128:256] = side
+    columns = []
+    for i in range(3):
+        rows = slice(COLUMN_ROW + 2 * i, COLUMN_ROW + 2 * i + 2)
+        columns.append(jnp.concatenate([column_ref[i], after(rows), jnp.zeros((4, 128), f32), before(rows)], axis=0))
+    column_eta = [spread_columns(x, wide) for x in columns]
+    column_sum, beside = column_sums(columns)
+    column_sum_eta, beside_eta = column_sums([x * y for x, y in zip(columns, column_eta)])
+    near_eta = column_eta[1]
+    column_diag = DRAG + TOTAL * near_eta + spread_columns(column_sum, wide)
+    column_image = columns[1] * column_diag - near_eta * column_sum - column_sum_eta
+    column_image = jnp.where(near_eta > 0.0, column_image, 0.0)
+    rows_of, rows_eta = [], []
+    for depth in range(DEPTHS):
+        rows = slice(8 * depth, 8 * depth + 8)
+        b, a = before(rows), after(rows)
+        found = (
+            jnp.where(row < 4, low_ref[rows, :], rolled(high_ref[rows, :], 4, 0)),
+            jnp.where(row < 4, b, rolled(a, 4, 0)),
+            jnp.where(row < 4, rolled(b, 4, 0), a),
+        )
+        rows_of.append(found)
+        rows_eta.append([spread_rows(x, row) for x in found])
+    rows_product = [[x * y for x, y in zip(found, etas)] for found, etas in zip(rows_of, rows_eta)]
+
+    def row_sums(levels, depth, beside_columns):
+        parts = [weighted(levels[depth - 1][i], levels[depth][i], levels[depth + 1][i]) for i in range(3)]
+        (_, ai, bi), (outer, an, bn), (_, af, bf) = parts
+        first, last = beside_rows(beside_columns, depth, row)
+        return FACE * outer + (ai + af) + lane_pair(an + (bi + bf), lane, first, last), an, bn
+
+    def plane_sum(three, an, bn, beside_columns, depth, field):
+        outer, a, b = weighted(*three)
+        both = a + row_pair(b, row, bn, field)
+        own = beside_columns[0:8]
+        sides = lane_pair(both, lane, to_first(own, depth, field), to_last(own, depth, field))
+        return FACE * outer + row_pair(a, row, an, field) + sides
+
+    def plane(field, depth):
+        return planes_ref[field * DEPTHS + depth]
+
+    image, row_image, diagonal = {}, {}, {}
     for depth in range(1, DEPTHS - 1):
-        e = [x[3 * DEPTHS + depth + i] for i in (-1, 0, 1)]
-        d = (DRAG + TOTAL * e[1]) + stencil(*e)
-        diag[depth] = d[0:8, 0:128]
-        inside = e[1] > 0.0
+        row_sum, an, bn = row_sums(rows_of, depth, beside)
+        row_sum_eta, an_eta, bn_eta = row_sums(rows_product, depth, beside_eta)
+        near, eta = rows_of[depth][1], rows_eta[depth][1]
+        diag = DRAG + TOTAL * eta + spread_rows(row_sum, row)
+        row_image[depth] = jnp.where(eta > 0.0, near * diag - eta * row_sum - row_sum_eta, 0.0)
+        e = [plane(3, depth + i) for i in (-1, 0, 1)]
+        diag = DRAG + TOTAL * e[1] + plane_sum(e, an, bn, beside, depth, 3)
+        diagonal[depth] = diag
         for c in range(3):
-            v = [x[c * DEPTHS + depth + i] for i in (-1, 0, 1)]
-            ev = [e[i] * v[i] for i in range(3)]
-            out = v[1] * d - e[1] * stencil(*v) - stencil(*ev)
-            w[c * DEPTHS + depth] = jnp.where(inside, out, 0.0)
+            v = [plane(c, depth + i) for i in (-1, 0, 1)]
+            ev = [x * y for x, y in zip(e, v)]
+            out = v[1] * diag - e[1] * plane_sum(v, an, bn, beside, depth, c)
+            out = out - plane_sum(ev, an_eta, bn_eta, beside_eta, depth, c)
+            image[c, depth] = jnp.where(e[1] > 0.0, out, 0.0)
+    _, an, bn = weighted(rolled(column_image, 8), column_image, rolled(column_image, 120))
+    beside = an + pair(bn)
     m = [jnp.zeros((8, 128), f32) for _ in range(4)]
     for depth in range(2, DEPTHS - 2):
-        e = x[3 * DEPTHS + depth, 0:8, 0:128]
-        d = diag[depth]
+        _, an, bn = weighted(row_image[depth - 1], row_image[depth], row_image[depth + 1])
+        e = plane(3, depth)
         for c in range(3):
-            p = c * DEPTHS + depth
-            s = stencil(w[p - 1], w[p], w[p + 1])[0:8, 0:128]
-            v = x[p, 0:8, 0:128]
-            q = w[p, 0:8, 0:128]
+            s = plane_sum([image[c, depth + i] for i in (-1, 0, 1)], an, bn, beside, depth, c)
+            v, q = plane(c, depth), image[c, depth]
             image_ref[c, depth - 2] = q
             m[0] = m[0] + v * v
             m[1] = m[1] + v * q
             m[2] = m[2] + q * q
-            m[3] = m[3] + q * (q * d - 2.0 * (e * s))
+            m[3] = m[3] + q * (q * diagonal[depth] - 2.0 * (e * s))
     total = jnp.zeros((8, 128), f32)
     for k in range(4):
         total = jnp.where(lane == k, jnp.sum(m[k]), total)
     for i in range(sums_ref.shape[0] // 8):
         sums_ref[8 * i : 8 * i + 8, :] = total
-    p = 2 * DEPTHS + DEPTHS - 3
-    top_ref[0] = x[p, 0:8, 0:128]
-    top_ref[1] = w[p, 0:8, 0:128]
+    top_ref[0] = plane(2, DEPTHS - 3)
+    top_ref[1] = image[2, DEPTHS - 3]
 
 
 def middle(sums_ref, top_ref, out_ref):
@@ -350,23 +458,20 @@
         [(PLANES, 8, 128), (2, 8, 128), (2, 8, 128)],
         (body_force, viscosity, load, odd, even, left, right),
     )
+    own = (odd, even)
     odd, even = swap(odd, even, "gy")
-    odd, even, from_left, from_right, height, conduct = call(
+    low, high = call(edge_rows, [(COLUMN_ROW, 128)] * 2, (planes,))
+    odd, even, columns, height, conduct = call(
         prepare_rows,
-        [(GX_ROWS, 128), (GX_ROWS, 128), (2, 8, 128), (2, 8, 128), (64, 256), (64, 256)],
-        (planes, odd, even, height, conduct),
+        [(GX_ROWS, 128), (GX_ROWS, 128), (3, 8, 128), (64, 256), (64, 256)],
+        (low, high, *own, odd, even, height, conduct),
     )
     odd, even = swap(odd, even, "gx")
     group = lax.axis_size("gx") * lax.axis_size("gy")
     image, sums, top, height = call(
         operate,
         [(3, 8, 8, 128), (group, 128), (2, 8, 128), (64, 128)],
-        (planes, from_left, from_right, odd, even, height, conduct),
-        [
-            pltpu.VMEM((PLANES, 16, 256), f32),
-            pltpu.VMEM((3 * DEPTHS, 16, 256), f32),
-            pltpu.VMEM((DEPTHS, 8, 128), f32),
-        ],
+        (planes, low, high, columns, odd, even, height, conduct),
     )
     sums = lax.all_to_all(sums.reshape(group, 1, 128), ("gx", "gy"), 0, 0)
     (parts,) = call(middle, [(lax.axis_size("gz"), 8, 128)], (sums.reshape(group, 128), top))

time: 67.1 us -> 66.6 us (level)
    pallas_call x6 -> x7, Pallas kernels: 3.7 us -> 3.27 us  [call(): pl.pallas_call(body, out_shape=[jax.ShapeDtypeStruct(s, f32) for s in out...]
  transfers between devices with their start and end apart: 6 -> 6, of which waited for: 2 -> 2; matrix products, arithmetic and copies ran while one was open for 0% -> 0% of each run, Pallas kernels for 0% -> 1%
where the time goes in v6:
time: 66.6 us; the launch traced here: 66.1 us
  blocking collectives  35.7 us (54%)
  starting transfers between devices  22 us (33%)
  Pallas kernels  4.13 us (6%)
  waiting for transfers between devices  2.17 us (3%)
  local copies, waits for them, and re-layouts  1.36 us (2%)
  between operations  0.79 us (1%)
    all_to_all x1, blocking collectives, local(): sums = lax.all_to_all(sums.reshape(group, 1, 128), ('gx', 'gy'), 0, 0)  22.8 us
    ppermute x3, starting transfers between devices, swap(): lax.ppermute(even, axis, pairs(0))  14.2 us
    all_to_all x1, blocking collectives, local(): parts = lax.all_to_all(parts, 'gz', 0, 0)  12.9 us
    ppermute x3, starting transfers between devices, swap(): lax.ppermute(odd, axis, pairs(1))  7.76 us
    pallas_call x7, Pallas kernels, call(): pl.pallas_call(body, out_shape=[jax.ShapeDtypeStruct(s, f32) for s in out...  3.27 us
    ppermute x3, waiting for transfers between devices, swap(): lax.ppermute(even, axis, pairs(0))  2.11 us
    unnamed x8, local copies, waits for them, and re-layouts  1.36 us
  transfers between devices with their start and end apart: 6, of which 2 were waited for; matrix products, arithmetic and copies ran while one was open for 0% of the time, Pallas kernels for 1%

profile of v6, /device:TPU:1, one launch (start us, length us, event | category | flops | bytes accessed | tf_op | source)
XLA Modules:
  0.0 66.1 jit_solution(2217720224547620973)
XLA Ops:
  0.6 0.0 copy-start.2
  0.6 0.9 %shard_map.60 = (f32[4,2,8,128]{3,2,1,0:T(8,128)S(1)}, f32[4,2,8,128]{3,2,1,0:T(8,128)S(1)}) custom-call(f32[3,8,8,128]{3,2,1,0:T(8,128)} %force_ref.3, f32[8,8,128]{2,1,0:T(8,128)} %visc_ref.3), custom_call_target="tpu_custom_call" | custom-call | tf_op jit(solution)/shard_map/pallas_call | solution.py:442
  1.5 0.7 %collective-permute-start = (f32[4,2,8,128]{3,2,1,0:T(8,128)S(1)}, f32[4,2,8,128]{3,2,1,0:T(8,128)S(1)}, u32[]{:S(2)}, u32[]{:S(2)}) collective-permute-start(f32[4,2,8,128]{3,2,1,0:T(8,128)S(1)} %get-tuple-element.24), channel_id=1, source_target_pairs={{1,2},{2,1},{3,4},{4,3},{5,6},{6,5},{9,10},{10,9},{11,12},{12,11},... | collective-permute-start | bytes 98312 | tf_op jit(solution)/shard_map/ppermute | solution.py:438
  2.2 0.0 copy-start
  2.2 6.7 %collective-permute-start.1 = (f32[4,2,8,128]{3,2,1,0:T(8,128)S(1)}, f32[4,2,8,128]{3,2,1,0:T(8,128)S(1)}, u32[]{:S(2)}, u32[]{:S(2)}) collective-permute-start(f32[4,2,8,128]{3,2,1,0:T(8,128)S(1)} %get-tuple-element.25), channel_id=1, source_target_pairs={{0,1},{1,0},{2,3},{3,2},{4,5},{5,4},{6,7},{7,6},{8,9},{9,8},{10,11... | collective-permute-start | bytes 98312 | tf_op jit(solution)/shard_map/ppermute | solution.py:438
  8.9 0.0 copy-done.2
  8.9 0.0 copy-start.1
  8.9 0.9 %copy-done.1 = f32[64,1024]{1,0:T(8,128)S(1)} copy-done((f32[64,1024]{1,0:T(8,128)S(1)}, f32[64,1024]{1,0:T(8,128)}, u32[]{:S(2)}) %copy-start.1) | copy-done | bytes 262168
  9.9 0.0 copy-start.3
  9.9 0.3 shard_map.59
  10.2 0.0 collective-permute-done.odd_ref
  10.2 0.0 collective-permute-done.1.even_ref
  10.2 0.0 copy-done
  10.2 0.4 copy-done.3
  10.6 0.2 shard_map.61
  10.8 0.7 collective-permute-start.2
  11.4 5.6 %collective-permute-start.3 = (f32[2,8,128]{2,1,0:T(8,128)S(1)}, f32[2,8,128]{2,1,0:T(8,128)S(1)}, u32[]{:S(2)}, u32[]{:S(2)}) collective-permute-start(f32[2,8,128]{2,1,0:T(8,128)S(1)} %get-tuple-element.32.own_even), channel_id=1, source_target_pairs={{0,8},{8,0},{16,24},{24,16},{32,40},{40,32},{48,56},{56,48},{64,72... | collective-permute-start | bytes 24584 | tf_op jit(solution)/shard_map/ppermute | solution.py:438
  17.0 0.1 shard_map.62
  17.1 0.0 collective-permute-done.2.odd_ref
  17.1 0.9 %collective-permute-done.3.even_ref = f32[2,8,128]{2,1,0:T(8,128)S(1)} collective-permute-done((f32[2,8,128]{2,1,0:T(8,128)S(1)}, f32[2,8,128]{2,1,0:T(8,128)S(1)}, u32[]{:S(2)}, u32[]{:S(2)}) %collective-permute-start.3) | collective-permute-done | bytes 8224 | tf_op jit(solution)/shard_map/ppermute | solution.py:438
  18.1 0.1 shard_map.63
  18.2 6.4 %collective-permute-start.4 = (f32[136,128]{1,0:T(8,128)S(1)}, f32[136,128]{1,0:T(8,128)S(1)}, u32[]{:S(2)}, u32[]{:S(2)}) collective-permute-start(f32[136,128]{1,0:T(8,128)S(1)} %get-tuple-element.36), channel_id=1, source_target_pairs={{128,256},{256,128},{129,257},{257,129},{130,258},{258,130},{131,2... | collective-permute-start | bytes 208904 | tf_op jit(solution)/shard_map/ppermute | solution.py:438
  24.6 1.9 %collective-permute-start.5 = (f32[136,128]{1,0:T(8,128)S(1)}, f32[136,128]{1,0:T(8,128)S(1)}, u32[]{:S(2)}, u32[]{:S(2)}) collective-permute-start(f32[136,128]{1,0:T(8,128)S(1)} %get-tuple-element.37), channel_id=1, source_target_pairs={{0,128},{128,0},{256,384},{384,256},{1,129},{129,1},{257,385},{385... | collective-permute-start | bytes 208904 | tf_op jit(solution)/shard_map/ppermute | solution.py:438
  26.5 0.1 collective-permute-done.4.odd_ref
  26.6 1.2 %collective-permute-done.5.even_ref = f32[136,128]{1,0:T(8,128)S(1)} collective-permute-done((f32[136,128]{1,0:T(8,128)S(1)}, f32[136,128]{1,0:T(8,128)S(1)}, u32[]{:S(2)}, u32[]{:S(2)}) %collective-permute-start.5) | collective-permute-done | bytes 69664 | tf_op jit(solution)/shard_map/ppermute | solution.py:438
  27.8 1.7 %shard_map.64 = (f32[3,8,8,128]{3,2,1,0:T(8,128)S(1)}, f32[64,128]{1,0:T(8,128)S(1)}, f32[2,8,128]{2,1,0:T(8,128)S(1)}, f32[64,128]{1,0:T(8,128)S(1)}) custom-call(f32[48,8,128]{2,1,0:T(8,128)S(1)} %get-tuple-element.28.planes_ref, f32[96,128]{1,0:T(8,128)S(1)} %get-tuple-element.29.low_ref, f32[96,128]{1,0:T(8,128)S(1)} %get-tuple-element.30.high_ref, ...), custom_call_target="tpu_custom_call" | custom-call | flops 20480000 | bytes 262144 | tf_op jit(solution)/shard_map/pallas_call | solution.py:29
  29.4 22.8 %all_to_all.10 = f32[64,1,128]{2,1,0:T(1,128)S(1)} all-to-all(f32[64,1,128]{2,1,0:T(1,128)S(1)} %bitcast.4), channel_id=1, replica_groups=mesh['gx'=4,'gy'=16,'gz'=8] {'gx','gy'}, dimensions={0} | all-to-all | bytes 65536 | tf_op jit(solution)/shard_map/all_to_all | solution.py:476
  52.2 0.1 shard_map.65
  52.3 12.9 %all_to_all.11.parts_ref = f32[8,8,128]{2,1,0:T(8,128)S(1)} all-to-all(f32[8,8,128]{2,1,0:T(8,128)S(1)} %shard_map.65), channel_id=1, replica_groups=mesh['gx'=4,'gy'=16,'gz'=8] {'gz'}, dimensions={0} | all-to-all | bytes 65536 | tf_op jit(solution)/shard_map/all_to_all | solution.py:478
  65.2 0.9 %shard_map.66 = (f32[3,8,8,128]{3,2,1,0:T(8,128)}, f32[64,128]{1,0:T(8,128)}) custom-call(f32[8,8,128]{2,1,0:T(8,128)S(1)} %all_to_all.11.parts_ref, f32[48,8,128]{2,1,0:T(8,128)S(1)} %get-tuple-element.28.planes_ref, f32[3,8,8,128]{3,2,1,0:T(8,128)S(1)} %get-tuple-element.42.image_ref, f32[64,128]{1,0:T(8,128)S(1)} %get-tuple-element.43.height_ref), custom_call_target="tpu_custom_call" | custom-call | flops 20480000 | bytes 262144 | tf_op jit(solution)/shard_map/pallas_call | solution.py:29
Async XLA Ops:
  0.6 8.3 %copy-start.2 = (bf16[64,1024]{1,0:T(8,128)(2,1)S(1)}, bf16[64,1024]{1,0:T(8,128)(2,1)}, u32[]{:S(2)}) copy-start(bf16[64,1024]{1,0:T(8,128)(2,1)} %kappa_ref.1) | copy-start | bytes 393220
  1.5 8.7 %collective-permute-start = (f32[4,2,8,128]{3,2,1,0:T(8,128)S(1)}, f32[4,2,8,128]{3,2,1,0:T(8,128)S(1)}, u32[]{:S(2)}, u32[]{:S(2)}) collective-permute-start(f32[4,2,8,128]{3,2,1,0:T(8,128)S(1)} %get-tuple-element.24), channel_id=1, source_target_pairs={{1,2},{2,1},{3,4},{4,3},{5,6},{6,5},{9,10},{10,9},{11,12},{12,11},... | collective-permute-start | bytes 98312 | tf_op jit(solution)/shard_map/ppermute | solution.py:438
  2.2 8.0 %copy-start = (f32[3,8,8,128]{3,2,1,0:T(8,128)S(1)}, f32[3,8,8,128]{3,2,1,0:T(8,128)}, u32[]{:S(2)}) copy-start(f32[3,8,8,128]{3,2,1,0:T(8,128)} %force_ref.3) | copy-start | bytes 294916
  2.2 8.0 %collective-permute-start.1 = (f32[4,2,8,128]{3,2,1,0:T(8,128)S(1)}, f32[4,2,8,128]{3,2,1,0:T(8,128)S(1)}, u32[]{:S(2)}, u32[]{:S(2)}) collective-permute-start(f32[4,2,8,128]{3,2,1,0:T(8,128)S(1)} %get-tuple-element.25), channel_id=1, source_target_pairs={{0,1},{1,0},{2,3},{3,2},{4,5},{5,4},{6,7},{7,6},{8,9},{9,8},{10,11... | collective-permute-start | bytes 98312 | tf_op jit(solution)/shard_map/ppermute | solution.py:438
  8.9 1.0 %copy-start.1 = (f32[64,1024]{1,0:T(8,128)S(1)}, f32[64,1024]{1,0:T(8,128)}, u32[]{:S(2)}) copy-start(f32[64,1024]{1,0:T(8,128)} %topo_ref.1) | copy-start | bytes 786436
  9.9 0.8 %copy-start.3 = (f32[8,8,128]{2,1,0:T(8,128)S(1)}, f32[8,8,128]{2,1,0:T(8,128)}, u32[]{:S(2)}) copy-start(f32[8,8,128]{2,1,0:T(8,128)} %visc_ref.3) | copy-start | bytes 98308
  10.8 6.3 %collective-permute-start.2 = (f32[2,8,128]{2,1,0:T(8,128)S(1)}, f32[2,8,128]{2,1,0:T(8,128)S(1)}, u32[]{:S(2)}, u32[]{:S(2)}) collective-permute-start(f32[2,8,128]{2,1,0:T(8,128)S(1)} %get-tuple-element.31.own_odd), channel_id=1, source_target_pairs={{8,16},{16,8},{24,32},{32,24},{40,48},{48,40},{56,64},{64,56},{72,... | collective-permute-start | bytes 24584 | tf_op jit(solution)/shard_map/ppermute | solution.py:438
  11.4 6.6 %collective-permute-start.3 = (f32[2,8,128]{2,1,0:T(8,128)S(1)}, f32[2,8,128]{2,1,0:T(8,128)S(1)}, u32[]{:S(2)}, u32[]{:S(2)}) collective-permute-start(f32[2,8,128]{2,1,0:T(8,128)S(1)} %get-tuple-element.32.own_even), channel_id=1, source_target_pairs={{0,8},{8,0},{16,24},{24,16},{32,40},{40,32},{48,56},{56,48},{64,72... | collective-permute-start | bytes 24584 | tf_op jit(solution)/shard_map/ppermute | solution.py:438
  18.2 8.4 %collective-permute-start.4 = (f32[136,128]{1,0:T(8,128)S(1)}, f32[136,128]{1,0:T(8,128)S(1)}, u32[]{:S(2)}, u32[]{:S(2)}) collective-permute-start(f32[136,128]{1,0:T(8,128)S(1)} %get-tuple-element.36), channel_id=1, source_target_pairs={{128,256},{256,128},{129,257},{257,129},{130,258},{258,130},{131,2... | collective-permute-start | bytes 208904 | tf_op jit(solution)/shard_map/ppermute | solution.py:438
  24.6 3.2 %collective-permute-start.5 = (f32[136,128]{1,0:T(8,128)S(1)}, f32[136,128]{1,0:T(8,128)S(1)}, u32[]{:S(2)}, u32[]{:S(2)}) collective-permute-start(f32[136,128]{1,0:T(8,128)S(1)} %get-tuple-element.37), channel_id=1, source_target_pairs={{0,128},{128,0},{256,384},{384,256},{1,129},{129,1},{257,385},{385... | collective-permute-start | bytes 208904 | tf_op jit(solution)/shard_map/ppermute | solution.py:438

commit v7 on v6

--- a/solution.py
+++ b/solution.py
@@ -106,35 +106,53 @@
         copy.wait()
 
 
-def assemble(force_ref, visc_ref, load_ref, odd_ref, even_ref, sl_ref, sr_ref, planes_ref, odd_out, even_out):
-    upward = is_even("gz")
+def packed(plane, depth, field, left, right, lane):
+    first = 8 * depth + 2 * field
+    mask = lane // 2 == first // 2
+    left = jnp.where(mask, rolled(plane, first), left)
+    return left, jnp.where(mask, rolled(plane, first - 126), right)
+
+
+def own_planes(force_ref, visc_ref, load_ref, sl_ref, sr_ref, planes_ref, left_ref, right_ref):
     lane = lanes((8, 128))
     left = jnp.zeros((8, 128), f32)
     right = jnp.zeros((8, 128), f32)
+    depths = visc_ref.shape[0]
+    for field in range(4):
+        for depth in range(depths):
+            plane = visc_ref[depth] if field == 3 else force_ref[field, depth]
+            if field == 2 and depth == depths - 1:
+                plane = plane + load_ref[...]
+            planes_ref[field, depth] = plane
+            left, right = packed(plane, depth + 2, field, left, right, lane)
+    left_ref[0] = left
+    right_ref[0] = right
+    left_ref[1] = sl_ref[...]
+    right_ref[1] = sr_ref[...]
+
+
+def assemble(own_ref, odd_ref, even_ref, left_ref, right_ref, planes_ref, odd_out, even_out):
+    upward = is_even("gz")
+    lane = lanes((8, 128))
+    left, right = left_ref[0], right_ref[0]
     for field in range(4):
         for depth in range(DEPTHS):
+            p = field * DEPTHS + depth
+            if 2 <= depth < DEPTHS - 2:
+                planes_ref[p] = own_ref[field, depth - 2]
+                continue
             if depth < 2:
                 plane = jnp.where(upward, odd_ref[field, depth], even_ref[field, depth])
-            elif depth >= DEPTHS - 2:
+            else:
                 i = depth - (DEPTHS - 2)
                 plane = jnp.where(upward, even_ref[field, i], odd_ref[field, i])
-            elif field == 3:
-                plane = visc_ref[depth - 2]
-            else:
-                plane = force_ref[field, depth - 2]
-                if field == 2 and depth == DEPTHS - 3:
-                    plane = plane + load_ref[...]
-            p = field * DEPTHS + depth
             planes_ref[p] = plane
-            first = 8 * depth + 2 * field
-            mask = lane // 2 == first // 2
-            left = jnp.where(mask, rolled(plane, first), left)
-            right = jnp.where(mask, rolled(plane, first - 126), right)
+            left, right = packed(plane, depth, field, left, right, lane)
     rightward = is_even("gy")
     odd_out[0] = jnp.where(rightward, left, right)
     even_out[0] = jnp.where(rightward, right, left)
-    odd_out[1] = jnp.where(rightward, sl_ref[...], sr_ref[...])
-    even_out[1] = jnp.where(rightward, sr_ref[...], sl_ref[...])
+    odd_out[1] = jnp.where(rightward, left_ref[1], right_ref[1])
+    even_out[1] = jnp.where(rightward, right_ref[1], left_ref[1])
 
 
 def edge_rows(planes_ref, low_ref, high_ref):
@@ -273,23 +291,29 @@
     return before, after
 
 
+def flux(conduct, slope):
+    return conduct * slope * lax.rsqrt(1.0 + slope * slope)
+
+
 def steps(h, k):
     rows = h.shape[0]
     inside = k > 0.0
     along = 0.5 * (k + rolled(k, 255, 1))
+    along_before = rolled(along, 1, 1)
     across = 0.5 * (k + rolled(k, rows - 1, 0))
     for step in range(STEPS):
-        s = rolled(h, 255, 1) - h
-        q = along * s * lax.rsqrt(1.0 + s * s)
-        t = rolled(h, rows - 1, 0) - h
-        r = across * t * lax.rsqrt(1.0 + t * t)
-        change = (q - rolled(q, 1, 1)) + (r - rolled(r, 1, 0))
-        h = jnp.where(inside, h + TIME_STEP * change, 0.0)
+        q = flux(along, rolled(h, 255, 1) - h) - flux(along_before, h - rolled(h, 1, 1))
+        r = flux(across, rolled(h, rows - 1, 0) - h)
+        h = jnp.where(inside, h + TIME_STEP * (q + (r - rolled(r, 1, 0))), 0.0)
     return h
 
 
+def inner_rows(height_ref, conduct_ref, out_ref):
+    out_ref[...] = steps(height_ref[...], conduct_ref[...])[8:56, 0:128]
+
+
 def operate(
-    planes_ref, low_ref, high_ref, column_ref, odd_ref, even_ref, height_ref, conduct_ref,
+    planes_ref, low_ref, high_ref, column_ref, odd_ref, even_ref, height_ref, conduct_ref, inner_ref,
     image_ref, sums_ref, top_ref, out_ref,
 ):
     lane = lanes((8, 128))
@@ -297,14 +321,16 @@
     wide = lanes((16, 128))
     before, after = sided(odd_ref, even_ref, "gx")
 
-    def extended(source, base):
+    def banded(source, base):
         def joined(side):
             return jnp.concatenate([side(slice(base, base + 8)), side(slice(base + 8, base + 16))], axis=1)
 
-        return jnp.concatenate([source[...], joined(after), joined(before)], axis=0)
-
-    stepped = steps(extended(height_ref, SURFACE_ROW), extended(conduct_ref, SURFACE_ROW + 16))
-    out_ref[...] = stepped[0:64, 0:128]
+        return jnp.concatenate([source[48:64, :], joined(after), joined(before), source[0:16, :]], axis=0)
+
+    band = steps(banded(height_ref, SURFACE_ROW), banded(conduct_ref, SURFACE_ROW + 16))
+    out_ref[0:8, :] = band[32:40, 0:128]
+    out_ref[8:56, :] = inner_ref[...]
+    out_ref[56:64, :] = band[8:16, 0:128]
     columns = []
     for i in range(3):
         rows = slice(COLUMN_ROW + 2 * i, COLUMN_ROW + 2 * i + 2)
@@ -377,7 +403,12 @@
             m[3] = m[3] + q * (q * diagonal[depth] - 2.0 * (e * s))
     total = jnp.zeros((8, 128), f32)
     for k in range(4):
-        total = jnp.where(lane == k, jnp.sum(m[k]), total)
+        part = m[k]
+        for amount in (64, 32, 16):
+            part = part + rolled(part, amount)
+        total = jnp.where(lane // 16 == 2 + k, part, total)
+    for amount in (4, 2, 1):
+        total = total + rolled(total, amount, 0)
     for i in range(sums_ref.shape[0] // 8):
         sums_ref[8 * i : 8 * i + 8, :] = total
     top_ref[0] = plane(2, DEPTHS - 3)
@@ -387,8 +418,7 @@
 def middle(sums_ref, top_ref, out_ref):
     lane = lanes((8, 128))
     part = jnp.sum(sums_ref[...], axis=0, keepdims=True)
-    base = jnp.broadcast_to(rolled(part, 32), (8, 128))
-    base = jnp.where((lane >= 32) & (lane < 36), base, 0.0)
+    base = jnp.broadcast_to(part, (8, 128))
     for j in range(out_ref.shape[0]):
         piece = jnp.where(lane < 16, rolled(top_ref[0], -16 * j), base)
         out_ref[j] = jnp.where(lane // 16 == 1, rolled(top_ref[1], 16 - 16 * j), piece)
@@ -402,7 +432,7 @@
         total = total + parts_ref[j, 0:1, :]
 
     def moment(k):
-        return jnp.sum(jnp.where(lane == 32 + k, total, 0.0), axis=1, keepdims=True)
+        return jnp.sum(jnp.where(lane // 16 == 2 + k, total, 0.0), axis=1, keepdims=True)
 
     m0, m1, m2, m3 = (moment(k) for k in range(4))
     first = m0 / m1
@@ -453,10 +483,15 @@
         [(8, 128), (64, 256), (64, 256), (8, 128), (8, 128)],
         (topography, kappa),
     )
+    planes, left, right = call(
+        own_planes,
+        [(4, 8, 8, 128), (2, 8, 128), (2, 8, 128)],
+        (body_force, viscosity, load, left, right),
+    )
     planes, odd, even = call(
         assemble,
         [(PLANES, 8, 128), (2, 8, 128), (2, 8, 128)],
-        (body_force, viscosity, load, odd, even, left, right),
+        (planes, odd, even, left, right),
     )
     own = (odd, even)
     odd, even = swap(odd, even, "gy")
@@ -467,11 +502,12 @@
         (low, high, *own, odd, even, height, conduct),
     )
     odd, even = swap(odd, even, "gx")
+    (inner,) = call(inner_rows, [(48, 128)], (height, conduct))
     group = lax.axis_size("gx") * lax.axis_size("gy")
     image, sums, top, height = call(
         operate,
         [(3, 8, 8, 128), (group, 128), (2, 8, 128), (64, 128)],
-        (planes, low, high, columns, odd, even, height, conduct),
+        (planes, low, high, columns, odd, even, height, conduct, inner),
     )
     sums = lax.all_to_all(sums.reshape(group, 1, 128), ("gx", "gy"), 0, 0)
     (parts,) = call(middle, [(lax.axis_size("gz"), 8, 128)], (sums.reshape(group, 128), top))

time: 66.6 us -> 66.2 us (level)
  waiting for transfers between devices: 2.17 us -> 1.23 us
    ppermute x3, waiting for transfers between devices: 2.11 us -> 1.22 us  [swap(): lax.ppermute(even, axis, pairs(0))]
    pallas_call x7 -> x9, Pallas kernels: 3.27 us -> 3.93 us  [call(): pl.pallas_call(body, out_shape=[jax.ShapeDtypeStruct(s, f32) for s in out...]
  transfers between devices with their start and end apart: 6 -> 6, of which waited for: 2 -> 2; matrix products, arithmetic and copies ran while one was open for 0% -> 0% of each run, Pallas kernels for 1% -> 2%
where the time goes in v7:
time: 66.2 us; the launch traced here: 65.8 us
  blocking collectives  35.8 us (54%)
  starting transfers between devices  21.8 us (33%)
  Pallas kernels  4.78 us (7%)
  local copies, waits for them, and re-layouts  1.39 us (2%)
  waiting for transfers between devices  1.23 us (2%)
  between operations  0.8 us (1%)
    all_to_all x1, blocking collectives, local(): sums = lax.all_to_all(sums.reshape(group, 1, 128), ('gx', 'gy'), 0, 0)  22.9 us
    ppermute x3, starting transfers between devices, swap(): lax.ppermute(even, axis, pairs(0))  14.2 us
    all_to_all x1, blocking collectives, local(): parts = lax.all_to_all(parts, 'gz', 0, 0)  12.9 us
    ppermute x3, starting transfers between devices, swap(): lax.ppermute(odd, axis, pairs(1))  7.6 us
    pallas_call x9, Pallas kernels, call(): pl.pallas_call(body, out_shape=[jax.ShapeDtypeStruct(s, f32) for s in out...  3.93 us
    unnamed x8, local copies, waits for them, and re-layouts  1.39 us
  transfers between devices with their start and end apart: 6, of which 2 were waited for; matrix products, arithmetic and copies ran while one was open for 0% of the time, Pallas kernels for 2%

profile of v7, /device:TPU:1, one launch (start us, length us, event | category | flops | bytes accessed | tf_op | source)
XLA Modules:
  0.0 65.8 jit_solution(8020059585906665200)
XLA Ops:
  0.6 0.0 copy-start.2
  0.6 0.9 %shard_map.61 = (f32[4,2,8,128]{3,2,1,0:T(8,128)S(1)}, f32[4,2,8,128]{3,2,1,0:T(8,128)S(1)}) custom-call(f32[3,8,8,128]{3,2,1,0:T(8,128)} %force_ref.3, f32[8,8,128]{2,1,0:T(8,128)} %visc_ref.3), custom_call_target="tpu_custom_call" | custom-call | tf_op jit(solution)/shard_map/pallas_call | solution.py:472
  1.5 0.7 %collective-permute-start = (f32[4,2,8,128]{3,2,1,0:T(8,128)S(1)}, f32[4,2,8,128]{3,2,1,0:T(8,128)S(1)}, u32[]{:S(2)}, u32[]{:S(2)}) collective-permute-start(f32[4,2,8,128]{3,2,1,0:T(8,128)S(1)} %get-tuple-element.30), channel_id=1, source_target_pairs={{1,2},{2,1},{3,4},{4,3},{5,6},{6,5},{9,10},{10,9},{11,12},{12,11},... | collective-permute-start | bytes 98312 | tf_op jit(solution)/shard_map/ppermute | solution.py:468
  2.2 0.0 copy-start
  2.2 6.7 %collective-permute-start.1 = (f32[4,2,8,128]{3,2,1,0:T(8,128)S(1)}, f32[4,2,8,128]{3,2,1,0:T(8,128)S(1)}, u32[]{:S(2)}, u32[]{:S(2)}) collective-permute-start(f32[4,2,8,128]{3,2,1,0:T(8,128)S(1)} %get-tuple-element.31), channel_id=1, source_target_pairs={{0,1},{1,0},{2,3},{3,2},{4,5},{5,4},{6,7},{7,6},{8,9},{9,8},{10,11... | collective-permute-start | bytes 98312 | tf_op jit(solution)/shard_map/ppermute | solution.py:468
  8.9 0.0 copy-done.2
  8.9 0.0 copy-start.1
  8.9 0.9 %copy-done.1 = f32[64,1024]{1,0:T(8,128)S(1)} copy-done((f32[64,1024]{1,0:T(8,128)S(1)}, f32[64,1024]{1,0:T(8,128)}, u32[]{:S(2)}) %copy-start.1) | copy-done | bytes 262168
  9.9 0.0 copy-start.3
  9.9 0.3 shard_map.59
  10.2 0.0 copy-done
  10.2 0.4 copy-done.3
  10.6 0.1 shard_map.60
  10.7 0.0 collective-permute-done.odd_ref
  10.8 0.0 collective-permute-done.1.even_ref
  10.8 0.1 shard_map.62
  10.9 0.7 %collective-permute-start.2 = (f32[2,8,128]{2,1,0:T(8,128)S(1)}, f32[2,8,128]{2,1,0:T(8,128)S(1)}, u32[]{:S(2)}, u32[]{:S(2)}) collective-permute-start(f32[2,8,128]{2,1,0:T(8,128)S(1)} %get-tuple-element.37.own_odd), channel_id=1, source_target_pairs={{8,16},{16,8},{24,32},{32,24},{40,48},{48,40},{56,64},{64,56},{72,... | collective-permute-start | bytes 24584 | tf_op jit(solution)/shard_map/ppermute | solution.py:468
  11.5 5.6 %collective-permute-start.3 = (f32[2,8,128]{2,1,0:T(8,128)S(1)}, f32[2,8,128]{2,1,0:T(8,128)S(1)}, u32[]{:S(2)}, u32[]{:S(2)}) collective-permute-start(f32[2,8,128]{2,1,0:T(8,128)S(1)} %get-tuple-element.38.own_even), channel_id=1, source_target_pairs={{0,8},{8,0},{16,24},{24,16},{32,40},{40,32},{48,56},{56,48},{64,72... | collective-permute-start | bytes 24584 | tf_op jit(solution)/shard_map/ppermute | solution.py:468
  17.1 0.1 shard_map.63
  17.2 0.0 collective-permute-done.2.odd_ref
  17.2 0.9 %collective-permute-done.3.even_ref = f32[2,8,128]{2,1,0:T(8,128)S(1)} collective-permute-done((f32[2,8,128]{2,1,0:T(8,128)S(1)}, f32[2,8,128]{2,1,0:T(8,128)S(1)}, u32[]{:S(2)}, u32[]{:S(2)}) %collective-permute-start.3) | collective-permute-done | bytes 8224 | tf_op jit(solution)/shard_map/ppermute | solution.py:468
  18.2 0.1 shard_map.64
  18.3 6.3 %collective-permute-start.4 = (f32[136,128]{1,0:T(8,128)S(1)}, f32[136,128]{1,0:T(8,128)S(1)}, u32[]{:S(2)}, u32[]{:S(2)}) collective-permute-start(f32[136,128]{1,0:T(8,128)S(1)} %get-tuple-element.42), channel_id=1, source_target_pairs={{128,256},{256,128},{129,257},{257,129},{130,258},{258,130},{131,2... | collective-permute-start | bytes 208904 | tf_op jit(solution)/shard_map/ppermute | solution.py:468
  24.6 1.9 %collective-permute-start.5 = (f32[136,128]{1,0:T(8,128)S(1)}, f32[136,128]{1,0:T(8,128)S(1)}, u32[]{:S(2)}, u32[]{:S(2)}) collective-permute-start(f32[136,128]{1,0:T(8,128)S(1)} %get-tuple-element.43), channel_id=1, source_target_pairs={{0,128},{128,0},{256,384},{384,256},{1,129},{129,1},{257,385},{385... | collective-permute-start | bytes 208904 | tf_op jit(solution)/shard_map/ppermute | solution.py:468
  26.5 0.9 %shard_map.65.inner_ref = f32[48,128]{1,0:T(8,128)S(1)} custom-call(f32[64,256]{1,0:T(8,128)S(1)} %get-tuple-element.44.height_ref, f32[64,256]{1,0:T(8,128)S(1)} %get-tuple-element.45.conduct_ref), custom_call_target="tpu_custom_call" | custom-call | flops 20480000 | bytes 262144 | tf_op jit(solution)/shard_map/pallas_call | solution.py:29
  27.4 0.0 collective-permute-done.4.odd_ref
  27.4 0.3 collective-permute-done.5.even_ref
  27.7 1.3 %shard_map.66 = (f32[3,8,8,128]{3,2,1,0:T(8,128)S(1)}, f32[64,128]{1,0:T(8,128)S(1)}, f32[2,8,128]{2,1,0:T(8,128)S(1)}, f32[64,128]{1,0:T(8,128)S(1)}) custom-call(f32[48,8,128]{2,1,0:T(8,128)S(1)} %get-tuple-element.34.planes_ref, f32[96,128]{1,0:T(8,128)S(1)} %get-tuple-element.35.low_ref, f32[96,128]{1,0:T(8,128)S(1)} %get-tuple-element.36.high_ref, ...), custom_call_target="tpu_custom_call" | custom-call | flops 20480000 | bytes 262144 | tf_op jit(solution)/shard_map/pallas_call | solution.py:29
  29.0 22.9 %all_to_all.10 = f32[64,1,128]{2,1,0:T(1,128)S(1)} all-to-all(f32[64,1,128]{2,1,0:T(1,128)S(1)} %bitcast.4), channel_id=1, replica_groups=mesh['gx'=4,'gy'=16,'gz'=8] {'gx','gy'}, dimensions={0} | all-to-all | bytes 65536 | tf_op jit(solution)/shard_map/all_to_all | solution.py:512
  51.9 0.1 shard_map.67
  52.0 12.9 %all_to_all.11.parts_ref = f32[8,8,128]{2,1,0:T(8,128)S(1)} all-to-all(f32[8,8,128]{2,1,0:T(8,128)S(1)} %shard_map.67), channel_id=1, replica_groups=mesh['gx'=4,'gy'=16,'gz'=8] {'gz'}, dimensions={0} | all-to-all | bytes 65536 | tf_op jit(solution)/shard_map/all_to_all | solution.py:514
  64.9 0.9 %shard_map.68 = (f32[3,8,8,128]{3,2,1,0:T(8,128)}, f32[64,128]{1,0:T(8,128)}) custom-call(f32[8,8,128]{2,1,0:T(8,128)S(1)} %all_to_all.11.parts_ref, f32[48,8,128]{2,1,0:T(8,128)S(1)} %get-tuple-element.34.planes_ref, f32[3,8,8,128]{3,2,1,0:T(8,128)S(1)} %get-tuple-element.48.image_ref, f32[64,128]{1,0:T(8,128)S(1)} %get-tuple-element.49.height_ref), custom_call_target="tpu_custom_call" | custom-call | flops 20480000 | bytes 262144 | tf_op jit(solution)/shard_map/pallas_call | solution.py:29
Async XLA Ops:
  0.6 8.3 %copy-start.2 = (bf16[64,1024]{1,0:T(8,128)(2,1)S(1)}, bf16[64,1024]{1,0:T(8,128)(2,1)}, u32[]{:S(2)}) copy-start(bf16[64,1024]{1,0:T(8,128)(2,1)} %kappa_ref.1) | copy-start | bytes 393220
  1.5 9.2 %collective-permute-start = (f32[4,2,8,128]{3,2,1,0:T(8,128)S(1)}, f32[4,2,8,128]{3,2,1,0:T(8,128)S(1)}, u32[]{:S(2)}, u32[]{:S(2)}) collective-permute-start(f32[4,2,8,128]{3,2,1,0:T(8,128)S(1)} %get-tuple-element.30), channel_id=1, source_target_pairs={{1,2},{2,1},{3,4},{4,3},{5,6},{6,5},{9,10},{10,9},{11,12},{12,11},... | collective-permute-start | bytes 98312 | tf_op jit(solution)/shard_map/ppermute | solution.py:468
  2.2 8.0 %copy-start = (f32[3,8,8,128]{3,2,1,0:T(8,128)S(1)}, f32[3,8,8,128]{3,2,1,0:T(8,128)}, u32[]{:S(2)}) copy-start(f32[3,8,8,128]{3,2,1,0:T(8,128)} %force_ref.3) | copy-start | bytes 294916
  2.2 8.6 %collective-permute-start.1 = (f32[4,2,8,128]{3,2,1,0:T(8,128)S(1)}, f32[4,2,8,128]{3,2,1,0:T(8,128)S(1)}, u32[]{:S(2)}, u32[]{:S(2)}) collective-permute-start(f32[4,2,8,128]{3,2,1,0:T(8,128)S(1)} %get-tuple-element.31), channel_id=1, source_target_pairs={{0,1},{1,0},{2,3},{3,2},{4,5},{5,4},{6,7},{7,6},{8,9},{9,8},{10,11... | collective-permute-start | bytes 98312 | tf_op jit(solution)/shard_map/ppermute | solution.py:468
  8.9 1.0 %copy-start.1 = (f32[64,1024]{1,0:T(8,128)S(1)}, f32[64,1024]{1,0:T(8,128)}, u32[]{:S(2)}) copy-start(f32[64,1024]{1,0:T(8,128)} %topo_ref.1) | copy-start | bytes 786436
  9.9 0.8 %copy-start.3 = (f32[8,8,128]{2,1,0:T(8,128)S(1)}, f32[8,8,128]{2,1,0:T(8,128)}, u32[]{:S(2)}) copy-start(f32[8,8,128]{2,1,0:T(8,128)} %visc_ref.3) | copy-start | bytes 98308
  10.9 6.3 %collective-permute-start.2 = (f32[2,8,128]{2,1,0:T(8,128)S(1)}, f32[2,8,128]{2,1,0:T(8,128)S(1)}, u32[]{:S(2)}, u32[]{:S(2)}) collective-permute-start(f32[2,8,128]{2,1,0:T(8,128)S(1)} %get-tuple-element.37.own_odd), channel_id=1, source_target_pairs={{8,16},{16,8},{24,32},{32,24},{40,48},{48,40},{56,64},{64,56},{72,... | collective-permute-start | bytes 24584 | tf_op jit(solution)/shard_map/ppermute | solution.py:468
  11.5 6.6 %collective-permute-start.3 = (f32[2,8,128]{2,1,0:T(8,128)S(1)}, f32[2,8,128]{2,1,0:T(8,128)S(1)}, u32[]{:S(2)}, u32[]{:S(2)}) collective-permute-start(f32[2,8,128]{2,1,0:T(8,128)S(1)} %get-tuple-element.38.own_even), channel_id=1, source_target_pairs={{0,8},{8,0},{16,24},{24,16},{32,40},{40,32},{48,56},{56,48},{64,72... | collective-permute-start | bytes 24584 | tf_op jit(solution)/shard_map/ppermute | solution.py:468
  18.3 9.1 %collective-permute-start.4 = (f32[136,128]{1,0:T(8,128)S(1)}, f32[136,128]{1,0:T(8,128)S(1)}, u32[]{:S(2)}, u32[]{:S(2)}) collective-permute-start(f32[136,128]{1,0:T(8,128)S(1)} %get-tuple-element.42), channel_id=1, source_target_pairs={{128,256},{256,128},{129,257},{257,129},{130,258},{258,130},{131,2... | collective-permute-start | bytes 208904 | tf_op jit(solution)/shard_map/ppermute | solution.py:468
  24.6 3.2 %collective-permute-start.5 = (f32[136,128]{1,0:T(8,128)S(1)}, f32[136,128]{1,0:T(8,128)S(1)}, u32[]{:S(2)}, u32[]{:S(2)}) collective-permute-start(f32[136,128]{1,0:T(8,128)S(1)} %get-tuple-element.43), channel_id=1, source_target_pairs={{0,128},{128,0},{256,384},{384,256},{1,129},{129,1},{257,385},{385... | collective-permute-start | bytes 208904 | tf_op jit(solution)/shard_map/ppermute | solution.py:468

commit v8 on v7

--- a/solution.py
+++ b/solution.py
@@ -46,7 +46,16 @@
     return x if amount == 0 else pltpu.roll(x, amount, axis)
 
 
-def surface_own(topo_ref, kappa_ref, load_ref, height_ref, conduct_ref, left_ref, right_ref):
+def own_block(
+    force_hbm, visc_hbm, topo_hbm, kappa_hbm, planes_ref, left_ref, right_ref, height_ref, conduct_ref,
+    force_ref, visc_ref, topo_ref, kappa_ref, sems,
+):
+    moves = ((topo_hbm, topo_ref), (kappa_hbm, kappa_ref), (force_hbm, force_ref), (visc_hbm, visc_ref))
+    copies = [pltpu.make_async_copy(source, target, sems.at[i]) for i, (source, target) in enumerate(moves)]
+    for copy in copies:
+        copy.start()
+    for copy in copies:
+        copy.wait()
     g = lax.axis_index("gz")
     last = lax.axis_size("gz") - 1
     lane = lanes((8, 128))
@@ -62,7 +71,7 @@
     load = jnp.zeros((8, 128), f32)
     for v in range(8):
         load = load + rolled(sums[8 * v : 8 * v + 8], 16 * v)
-    load_ref[...] = jnp.where(g == last, load * (-LOAD_GAIN / 64.0), 0.0)
+    load = jnp.where(g == last, load * (-LOAD_GAIN / 64.0), 0.0)
     wide = lanes((64, 128))
     own = pl.ds(pl.multiple_of(g * 128, 128), 128)
     before = pl.ds(pl.multiple_of(jnp.maximum(g - 1, 0) * 128, 128), 128)
@@ -84,8 +93,20 @@
             left = jnp.where(mask, rolled(head[8 * r : 8 * r + 8], 8 * slot), left)
             right = jnp.where(mask, rolled(tail[8 * r : 8 * r + 8], 8 * slot - 120), right)
             slot += 1
-    left_ref[...] = left
-    right_ref[...] = right
+    left_ref[1] = left
+    right_ref[1] = right
+    left = jnp.zeros((8, 128), f32)
+    right = jnp.zeros((8, 128), f32)
+    depths = visc_ref.shape[0]
+    for field in range(4):
+        for depth in range(depths):
+            plane = visc_ref[depth] if field == 3 else force_ref[field, depth]
+            if field == 2 and depth == depths - 1:
+                plane = plane + load
+            planes_ref[field, depth] = plane
+            left, right = packed(plane, depth + 2, field, left, right, lane)
+    left_ref[0] = left
+    right_ref[0] = right
 
 
 def is_even(axis):
@@ -111,24 +132,6 @@
     mask = lane // 2 == first // 2
     left = jnp.where(mask, rolled(plane, first), left)
     return left, jnp.where(mask, rolled(plane, first - 126), right)
-
-
-def own_planes(force_ref, visc_ref, load_ref, sl_ref, sr_ref, planes_ref, left_ref, right_ref):
-    lane = lanes((8, 128))
-    left = jnp.zeros((8, 128), f32)
-    right = jnp.zeros((8, 128), f32)
-    depths = visc_ref.shape[0]
-    for field in range(4):
-        for depth in range(depths):
-            plane = visc_ref[depth] if field == 3 else force_ref[field, depth]
-            if field == 2 and depth == depths - 1:
-                plane = plane + load_ref[...]
-            planes_ref[field, depth] = plane
-            left, right = packed(plane, depth + 2, field, left, right, lane)
-    left_ref[0] = left
-    right_ref[0] = right
-    left_ref[1] = sl_ref[...]
-    right_ref[1] = sr_ref[...]
 
 
 def assemble(own_ref, odd_ref, even_ref, left_ref, right_ref, planes_ref, odd_out, even_out):
@@ -469,6 +472,9 @@
 
 
 def local(body_force, viscosity, topography, kappa):
+    inputs = [
+        pltpu.with_memory_space_constraint(x, pltpu.HBM) for x in (body_force, viscosity, topography, kappa)
+    ]
     odd, even = pl.pallas_call(
         fetch,
         out_shape=[jax.ShapeDtypeStruct((4, 2, 8, 128), f32)] * 2,
@@ -476,18 +482,20 @@
         out_specs=[vmem()] * 2,
         scratch_shapes=[pltpu.SemaphoreType.DMA((4,))],
         compiler_params=pltpu.CompilerParams(vmem_limit_bytes=1 << 20),
-    )(*[pltpu.with_memory_space_constraint(x, pltpu.HBM) for x in (body_force, viscosity)])
+    )(*inputs[:2])
     odd, even = swap(odd, even, "gz")
-    load, height, conduct, left, right = call(
-        surface_own,
-        [(8, 128), (64, 256), (64, 256), (8, 128), (8, 128)],
-        (topography, kappa),
-    )
-    planes, left, right = call(
-        own_planes,
-        [(4, 8, 8, 128), (2, 8, 128), (2, 8, 128)],
-        (body_force, viscosity, load, left, right),
-    )
+    planes, left, right, height, conduct = pl.pallas_call(
+        own_block,
+        out_shape=[
+            jax.ShapeDtypeStruct(shape, f32)
+            for shape in ((4, 8, 8, 128), (2, 8, 128), (2, 8, 128), (64, 256), (64, 256))
+        ],
+        in_specs=[pl.BlockSpec(memory_space=pltpu.HBM)] * 4,
+        out_specs=[vmem()] * 5,
+        scratch_shapes=[pltpu.VMEM(x.shape, x.dtype) for x in inputs] + [pltpu.SemaphoreType.DMA((4,))],
+        compiler_params=pltpu.CompilerParams(vmem_limit_bytes=8 << 20),
+        cost_estimate=pl.CostEstimate(flops=20000 * 1024, bytes_accessed=1 << 18, transcendentals=0),
+    )(*inputs)
     planes, odd, even = call(
         assemble,
         [(PLANES, 8, 128), (2, 8, 128), (2, 8, 128)],

time: 66.2 us -> 66 us (level)
  local copies, waits for them, and re-layouts: 1.39 us -> 0 us
  Pallas kernels: 4.78 us -> 5.77 us
    pallas_call x0 -> x1, Pallas kernels: none -> 1.46 us  [local(): pl.pallas_call(own_block, out_shape=[jax.ShapeDtypeStruct(shape, f32) for...]
    unnamed x8 -> x0, local copies, waits for them, and re-layouts: 1.39 us -> none
    pallas_call x9 -> x7, Pallas kernels: 3.93 us -> 3.49 us  [call(): pl.pallas_call(body, out_shape=[jax.ShapeDtypeStruct(s, f32) for s in out...]
  transfers between devices with their start and end apart: 6 -> 6, of which waited for: 2 -> 2; matrix products, arithmetic and copies ran while one was open for 0% -> 0% of each run, Pallas kernels for 2% -> 4%
where the time goes in v8:
time: 66 us; the launch traced here: 65.6 us
  blocking collectives  35.8 us (54%)
  starting transfers between devices  22 us (33%)
  Pallas kernels  5.77 us (9%)
  waiting for transfers between devices  1.23 us (2%)
  between operations  0.76 us (1%)
    all_to_all x1, blocking collectives, local(): sums = lax.all_to_all(sums.reshape(group, 1, 128), ('gx', 'gy'), 0, 0)  22.9 us
    ppermute x3, starting transfers between devices, swap(): lax.ppermute(even, axis, pairs(0))  14.1 us
    all_to_all x1, blocking collectives, local(): parts = lax.all_to_all(parts, 'gz', 0, 0)  12.9 us
    ppermute x3, starting transfers between devices, swap(): lax.ppermute(odd, axis, pairs(1))  7.98 us
    pallas_call x7, Pallas kernels, call(): pl.pallas_call(body, out_shape=[jax.ShapeDtypeStruct(s, f32) for s in out...  3.49 us
    pallas_call x1, Pallas kernels, local(): pl.pallas_call(own_block, out_shape=[jax.ShapeDtypeStruct(shape, f32) for...  1.46 us
  transfers between devices with their start and end apart: 6, of which 2 were waited for; matrix products, arithmetic and copies ran while one was open for 0% of the time, Pallas kernels for 4%

profile of v8, /device:TPU:1, one launch (start us, length us, event | category | flops | bytes accessed | tf_op | source)
XLA Modules:
  0.0 65.6 jit_solution(18114668826800621204)
XLA Ops:
  0.6 0.8 %shard_map.60 = (f32[4,2,8,128]{3,2,1,0:T(8,128)S(1)}, f32[4,2,8,128]{3,2,1,0:T(8,128)S(1)}) custom-call(f32[3,8,8,128]{3,2,1,0:T(8,128)} %force_ref.1, f32[8,8,128]{2,1,0:T(8,128)} %visc_ref.1), custom_call_target="tpu_custom_call" | custom-call | tf_op jit(solution)/shard_map/pallas_call | solution.py:478
  1.5 0.7 %collective-permute-start = (f32[4,2,8,128]{3,2,1,0:T(8,128)S(1)}, f32[4,2,8,128]{3,2,1,0:T(8,128)S(1)}, u32[]{:S(2)}, u32[]{:S(2)}) collective-permute-start(f32[4,2,8,128]{3,2,1,0:T(8,128)S(1)} %get-tuple-element.24), channel_id=1, source_target_pairs={{1,2},{2,1},{3,4},{4,3},{5,6},{6,5},{9,10},{10,9},{11,12},{12,11},... | collective-permute-start | bytes 98312 | tf_op jit(solution)/shard_map/ppermute | solution.py:471
  2.1 6.6 %collective-permute-start.1 = (f32[4,2,8,128]{3,2,1,0:T(8,128)S(1)}, f32[4,2,8,128]{3,2,1,0:T(8,128)S(1)}, u32[]{:S(2)}, u32[]{:S(2)}) collective-permute-start(f32[4,2,8,128]{3,2,1,0:T(8,128)S(1)} %get-tuple-element.25), channel_id=1, source_target_pairs={{0,1},{1,0},{2,3},{3,2},{4,5},{5,4},{6,7},{7,6},{8,9},{9,8},{10,11... | collective-permute-start | bytes 98312 | tf_op jit(solution)/shard_map/ppermute | solution.py:471
  8.7 1.5 %shard_map.59 = (f32[4,8,8,128]{3,2,1,0:T(8,128)S(1)}, f32[2,8,128]{2,1,0:T(8,128)S(1)}, f32[2,8,128]{2,1,0:T(8,128)S(1)}, f32[64,256]{1,0:T(8,128)S(1)}, f32[64,256]{1,0:T(8,128)S(1)}) custom-call(f32[3,8,8,128]{3,2,1,0:T(8,128)} %force_ref.1, f32[8,8,128]{2,1,0:T(8,128)} %visc_ref.1, f32[64,1024]{1,0:T(8,128)} %topo_hbm.1, bf16[64,1024]{1,0:T(8,128)(2,1)} %kappa_hbm.1), custom_call_target="tpu_custom_call" | custom-call | flops 20480000 | bytes 262144 | tf_op jit(solution)/shard_map/pallas_call | solution.py:487
  10.2 0.0 collective-permute-done.odd_ref
  10.2 0.0 collective-permute-done.1.even_ref
  10.2 0.1 shard_map.61
  10.3 0.7 %collective-permute-start.2 = (f32[2,8,128]{2,1,0:T(8,128)S(1)}, f32[2,8,128]{2,1,0:T(8,128)S(1)}, u32[]{:S(2)}, u32[]{:S(2)}) collective-permute-start(f32[2,8,128]{2,1,0:T(8,128)S(1)} %get-tuple-element.31.own_odd), channel_id=1, source_target_pairs={{8,16},{16,8},{24,32},{32,24},{40,48},{48,40},{56,64},{64,56},{72,... | collective-permute-start | bytes 24584 | tf_op jit(solution)/shard_map/ppermute | solution.py:471
  11.0 5.6 %collective-permute-start.3 = (f32[2,8,128]{2,1,0:T(8,128)S(1)}, f32[2,8,128]{2,1,0:T(8,128)S(1)}, u32[]{:S(2)}, u32[]{:S(2)}) collective-permute-start(f32[2,8,128]{2,1,0:T(8,128)S(1)} %get-tuple-element.32.own_even), channel_id=1, source_target_pairs={{0,8},{8,0},{16,24},{24,16},{32,40},{40,32},{48,56},{56,48},{64,72... | collective-permute-start | bytes 24584 | tf_op jit(solution)/shard_map/ppermute | solution.py:471
  16.6 0.1 shard_map.62
  16.6 0.0 collective-permute-done.2.odd_ref
  16.6 0.9 %collective-permute-done.3.even_ref = f32[2,8,128]{2,1,0:T(8,128)S(1)} collective-permute-done((f32[2,8,128]{2,1,0:T(8,128)S(1)}, f32[2,8,128]{2,1,0:T(8,128)S(1)}, u32[]{:S(2)}, u32[]{:S(2)}) %collective-permute-start.3) | collective-permute-done | bytes 8224 | tf_op jit(solution)/shard_map/ppermute | solution.py:471
  17.6 0.1 shard_map.63
  17.7 6.7 %collective-permute-start.4 = (f32[136,128]{1,0:T(8,128)S(1)}, f32[136,128]{1,0:T(8,128)S(1)}, u32[]{:S(2)}, u32[]{:S(2)}) collective-permute-start(f32[136,128]{1,0:T(8,128)S(1)} %get-tuple-element.36), channel_id=1, source_target_pairs={{128,256},{256,128},{129,257},{257,129},{130,258},{258,130},{131,2... | collective-permute-start | bytes 208904 | tf_op jit(solution)/shard_map/ppermute | solution.py:471
  24.4 1.9 %collective-permute-start.5 = (f32[136,128]{1,0:T(8,128)S(1)}, f32[136,128]{1,0:T(8,128)S(1)}, u32[]{:S(2)}, u32[]{:S(2)}) collective-permute-start(f32[136,128]{1,0:T(8,128)S(1)} %get-tuple-element.37), channel_id=1, source_target_pairs={{0,128},{128,0},{256,384},{384,256},{1,129},{129,1},{257,385},{385... | collective-permute-start | bytes 208904 | tf_op jit(solution)/shard_map/ppermute | solution.py:471
  26.3 0.9 %shard_map.64.inner_ref = f32[48,128]{1,0:T(8,128)S(1)} custom-call(f32[64,256]{1,0:T(8,128)S(1)} %get-tuple-element.38.height_ref, f32[64,256]{1,0:T(8,128)S(1)} %get-tuple-element.39.conduct_ref), custom_call_target="tpu_custom_call" | custom-call | flops 20480000 | bytes 262144 | tf_op jit(solution)/shard_map/pallas_call | solution.py:29
  27.2 0.0 collective-permute-done.4.odd_ref
  27.2 0.3 collective-permute-done.5.even_ref
  27.5 1.3 %shard_map.65 = (f32[3,8,8,128]{3,2,1,0:T(8,128)S(1)}, f32[64,128]{1,0:T(8,128)S(1)}, f32[2,8,128]{2,1,0:T(8,128)S(1)}, f32[64,128]{1,0:T(8,128)S(1)}) custom-call(f32[48,8,128]{2,1,0:T(8,128)S(1)} %get-tuple-element.28.planes_ref, f32[96,128]{1,0:T(8,128)S(1)} %get-tuple-element.29.low_ref, f32[96,128]{1,0:T(8,128)S(1)} %get-tuple-element.30.high_ref, ...), custom_call_target="tpu_custom_call" | custom-call | flops 20480000 | bytes 262144 | tf_op jit(solution)/shard_map/pallas_call | solution.py:29
  28.8 22.9 %all_to_all.10 = f32[64,1,128]{2,1,0:T(1,128)S(1)} all-to-all(f32[64,1,128]{2,1,0:T(1,128)S(1)} %bitcast.4), channel_id=1, replica_groups=mesh['gx'=4,'gy'=16,'gz'=8] {'gx','gy'}, dimensions={0} | all-to-all | bytes 65536 | tf_op jit(solution)/shard_map/all_to_all | solution.py:520
  51.7 0.1 shard_map.66
  51.8 12.9 %all_to_all.11.parts_ref = f32[8,8,128]{2,1,0:T(8,128)S(1)} all-to-all(f32[8,8,128]{2,1,0:T(8,128)S(1)} %shard_map.66), channel_id=1, replica_groups=mesh['gx'=4,'gy'=16,'gz'=8] {'gz'}, dimensions={0} | all-to-all | bytes 65536 | tf_op jit(solution)/shard_map/all_to_all | solution.py:522
  64.7 0.9 %shard_map.67 = (f32[3,8,8,128]{3,2,1,0:T(8,128)}, f32[64,128]{1,0:T(8,128)}) custom-call(f32[8,8,128]{2,1,0:T(8,128)S(1)} %all_to_all.11.parts_ref, f32[48,8,128]{2,1,0:T(8,128)S(1)} %get-tuple-element.28.planes_ref, f32[3,8,8,128]{3,2,1,0:T(8,128)S(1)} %get-tuple-element.42.image_ref, f32[64,128]{1,0:T(8,128)S(1)} %get-tuple-element.43.height_ref), custom_call_target="tpu_custom_call" | custom-call | flops 20480000 | bytes 262144 | tf_op jit(solution)/shard_map/pallas_call | solution.py:29
Async XLA Ops:
  1.5 8.7 %collective-permute-start = (f32[4,2,8,128]{3,2,1,0:T(8,128)S(1)}, f32[4,2,8,128]{3,2,1,0:T(8,128)S(1)}, u32[]{:S(2)}, u32[]{:S(2)}) collective-permute-start(f32[4,2,8,128]{3,2,1,0:T(8,128)S(1)} %get-tuple-element.24), channel_id=1, source_target_pairs={{1,2},{2,1},{3,4},{4,3},{5,6},{6,5},{9,10},{10,9},{11,12},{12,11},... | collective-permute-start | bytes 98312 | tf_op jit(solution)/shard_map/ppermute | solution.py:471
  2.1 8.1 %collective-permute-start.1 = (f32[4,2,8,128]{3,2,1,0:T(8,128)S(1)}, f32[4,2,8,128]{3,2,1,0:T(8,128)S(1)}, u32[]{:S(2)}, u32[]{:S(2)}) collective-permute-start(f32[4,2,8,128]{3,2,1,0:T(8,128)S(1)} %get-tuple-element.25), channel_id=1, source_target_pairs={{0,1},{1,0},{2,3},{3,2},{4,5},{5,4},{6,7},{7,6},{8,9},{9,8},{10,11... | collective-permute-start | bytes 98312 | tf_op jit(solution)/shard_map/ppermute | solution.py:471
  10.3 6.3 %collective-permute-start.2 = (f32[2,8,128]{2,1,0:T(8,128)S(1)}, f32[2,8,128]{2,1,0:T(8,128)S(1)}, u32[]{:S(2)}, u32[]{:S(2)}) collective-permute-start(f32[2,8,128]{2,1,0:T(8,128)S(1)} %get-tuple-element.31.own_odd), channel_id=1, source_target_pairs={{8,16},{16,8},{24,32},{32,24},{40,48},{48,40},{56,64},{64,56},{72,... | collective-permute-start | bytes 24584 | tf_op jit(solution)/shard_map/ppermute | solution.py:471
  11.0 6.6 %collective-permute-start.3 = (f32[2,8,128]{2,1,0:T(8,128)S(1)}, f32[2,8,128]{2,1,0:T(8,128)S(1)}, u32[]{:S(2)}, u32[]{:S(2)}) collective-permute-start(f32[2,8,128]{2,1,0:T(8,128)S(1)} %get-tuple-element.32.own_even), channel_id=1, source_target_pairs={{0,8},{8,0},{16,24},{24,16},{32,40},{40,32},{48,56},{56,48},{64,72... | collective-permute-start | bytes 24584 | tf_op jit(solution)/shard_map/ppermute | solution.py:471
  17.7 9.5 %collective-permute-start.4 = (f32[136,128]{1,0:T(8,128)S(1)}, f32[136,128]{1,0:T(8,128)S(1)}, u32[]{:S(2)}, u32[]{:S(2)}) collective-permute-start(f32[136,128]{1,0:T(8,128)S(1)} %get-tuple-element.36), channel_id=1, source_target_pairs={{128,256},{256,128},{129,257},{257,129},{130,258},{258,130},{131,2... | collective-permute-start | bytes 208904 | tf_op jit(solution)/shard_map/ppermute | solution.py:471
  24.4 3.2 %collective-permute-start.5 = (f32[136,128]{1,0:T(8,128)S(1)}, f32[136,128]{1,0:T(8,128)S(1)}, u32[]{:S(2)}, u32[]{:S(2)}) collective-permute-start(f32[136,128]{1,0:T(8,128)S(1)} %get-tuple-element.37), channel_id=1, source_target_pairs={{0,128},{128,0},{256,384},{384,256},{1,129},{129,1},{257,385},{385... | collective-permute-start | bytes 208904 | tf_op jit(solution)/shard_map/ppermute | solution.py:471

commit v9 on v8

--- a/solution.py
+++ b/solution.py
@@ -427,9 +427,15 @@
         out_ref[j] = jnp.where(lane // 16 == 1, rolled(top_ref[1], 16 - 16 * j), piece)
 
 
-def finish(parts_ref, planes_ref, image_ref, height_ref, velocity_ref, surface_ref):
+def finish(parts_ref, planes_ref, image_ref, height_ref, velocity_hbm, surface_hbm, velocity_ref, surface_ref, sems):
     count = parts_ref.shape[0]
     lane = lanes((1, 128))
+    top = parts_ref[count - 1]
+    top = jnp.where(lanes((16, 128)) < 16, jnp.concatenate([top, rolled(top, -16)], axis=0), 0.0)
+    spread = (
+        lax.broadcasted_iota(jnp.int32, (128, 128), 1) // 8 == lax.broadcasted_iota(jnp.int32, (128, 128), 0)
+    ).astype(f32)
+    wide = jnp.dot(top, spread, precision=lax.Precision.HIGHEST, preferred_element_type=f32)
     total = parts_ref[0, 0:1, :]
     for j in range(1, count):
         total = total + parts_ref[j, 0:1, :]
@@ -447,16 +453,16 @@
     for c in range(3):
         for depth in range(8):
             velocity_ref[c, depth] = on_force * planes_ref[c * DEPTHS + depth + 2] + on_image * image_ref[c, depth]
-    top = parts_ref[count - 1]
-    rise = on_force * top + on_image * rolled(top, -16)
-    spread = (
-        lax.broadcasted_iota(jnp.int32, (128, 128), 1) // 8 == lax.broadcasted_iota(jnp.int32, (128, 128), 0)
-    ).astype(f32)
-    rise = jnp.where(lanes((8, 128)) < 16, rise, 0.0)
-    wide = (STEPS * TIME_STEP) * jnp.dot(rise, spread, precision=lax.Precision.HIGHEST, preferred_element_type=f32)
+    velocity_copy = pltpu.make_async_copy(velocity_ref, velocity_hbm, sems.at[0])
+    velocity_copy.start()
+    rise = (STEPS * TIME_STEP) * (on_force * wide[0:8] + on_image * wide[8:16])
     for r in range(8):
         rows = slice(8 * r, 8 * r + 8)
-        surface_ref[rows, :] = height_ref[rows, :] + jnp.broadcast_to(wide[r : r + 1, :], (8, 128))
+        surface_ref[rows, :] = height_ref[rows, :] + jnp.broadcast_to(rise[r : r + 1, :], (8, 128))
+    surface_copy = pltpu.make_async_copy(surface_ref, surface_hbm, sems.at[1])
+    surface_copy.start()
+    velocity_copy.wait()
+    surface_copy.wait()
 
 
 def swap(odd, even, axis):
@@ -520,9 +526,15 @@
     sums = lax.all_to_all(sums.reshape(group, 1, 128), ("gx", "gy"), 0, 0)
     (parts,) = call(middle, [(lax.axis_size("gz"), 8, 128)], (sums.reshape(group, 128), top))
     parts = lax.all_to_all(parts, "gz", 0, 0)
-    velocity, surface = call(
-        finish, [(3, 8, 8, 128), (64, 128)], (parts, planes, image, height)
-    )
+    shapes = ((3, 8, 8, 128), (64, 128))
+    velocity, surface = pl.pallas_call(
+        finish,
+        out_shape=[jax.ShapeDtypeStruct(shape, f32) for shape in shapes],
+        in_specs=[vmem()] * 4,
+        out_specs=[pl.BlockSpec(memory_space=pltpu.HBM)] * 2,
+        scratch_shapes=[pltpu.VMEM(shape, f32) for shape in shapes] + [pltpu.SemaphoreType.DMA((2,))],
+        compiler_params=pltpu.CompilerParams(vmem_limit_bytes=8 << 20),
+    )(parts, planes, image, height)
     return velocity, surface
 
 

time: 66 us -> 65.9 us (level)
    pallas_call x7 -> x6, Pallas kernels: 3.49 us -> 2.6 us  [call(): pl.pallas_call(body, out_shape=[jax.ShapeDtypeStruct(s, f32) for s in out...]
    pallas_call x0 -> x1, Pallas kernels: none -> 0.86 us  [local(): pl.pallas_call(finish, out_shape=[jax.ShapeDtypeStruct(shape, f32) for sh...]
where the time goes in v9:
time: 65.9 us; the launch traced here: 65.5 us
  blocking collectives  35.8 us (54%)
  starting transfers between devices  22 us (33%)
  Pallas kernels  5.74 us (9%)
  waiting for transfers between devices  1.23 us (2%)
  between operations  0.76 us (1%)
    all_to_all x1, blocking collectives, local(): sums = lax.all_to_all(sums.reshape(group, 1, 128), ('gx', 'gy'), 0, 0)  22.9 us
    ppermute x3, starting transfers between devices, swap(): lax.ppermute(even, axis, pairs(0))  14.1 us
    all_to_all x1, blocking collectives, local(): parts = lax.all_to_all(parts, 'gz', 0, 0)  12.9 us
    ppermute x3, starting transfers between devices, swap(): lax.ppermute(odd, axis, pairs(1))  7.98 us
    pallas_call x6, Pallas kernels, call(): pl.pallas_call(body, out_shape=[jax.ShapeDtypeStruct(s, f32) for s in out...  2.6 us
    pallas_call x1, Pallas kernels, local(): pl.pallas_call(own_block, out_shape=[jax.ShapeDtypeStruct(shape, f32) for...  1.46 us
  transfers between devices with their start and end apart: 6, of which 2 were waited for; matrix products, arithmetic and copies ran while one was open for 0% of the time, Pallas kernels for 4%

profile of v9, /device:TPU:1, one launch (start us, length us, event | category | flops | bytes accessed | tf_op | source)
XLA Modules:
  0.0 65.5 jit_solution(7042156413493313202)
XLA Ops:
  0.6 0.8 %shard_map.60 = (f32[4,2,8,128]{3,2,1,0:T(8,128)S(1)}, f32[4,2,8,128]{3,2,1,0:T(8,128)S(1)}) custom-call(f32[3,8,8,128]{3,2,1,0:T(8,128)} %force_ref.1, f32[8,8,128]{2,1,0:T(8,128)} %visc_ref.1), custom_call_target="tpu_custom_call" | custom-call | tf_op jit(solution)/shard_map/pallas_call | solution.py:484
  1.5 0.7 %collective-permute-start = (f32[4,2,8,128]{3,2,1,0:T(8,128)S(1)}, f32[4,2,8,128]{3,2,1,0:T(8,128)S(1)}, u32[]{:S(2)}, u32[]{:S(2)}) collective-permute-start(f32[4,2,8,128]{3,2,1,0:T(8,128)S(1)} %get-tuple-element.24), channel_id=1, source_target_pairs={{1,2},{2,1},{3,4},{4,3},{5,6},{6,5},{9,10},{10,9},{11,12},{12,11},... | collective-permute-start | bytes 98312 | tf_op jit(solution)/shard_map/ppermute | solution.py:477
  2.1 6.6 %collective-permute-start.1 = (f32[4,2,8,128]{3,2,1,0:T(8,128)S(1)}, f32[4,2,8,128]{3,2,1,0:T(8,128)S(1)}, u32[]{:S(2)}, u32[]{:S(2)}) collective-permute-start(f32[4,2,8,128]{3,2,1,0:T(8,128)S(1)} %get-tuple-element.25), channel_id=1, source_target_pairs={{0,1},{1,0},{2,3},{3,2},{4,5},{5,4},{6,7},{7,6},{8,9},{9,8},{10,11... | collective-permute-start | bytes 98312 | tf_op jit(solution)/shard_map/ppermute | solution.py:477
  8.7 1.5 %shard_map.59 = (f32[4,8,8,128]{3,2,1,0:T(8,128)S(1)}, f32[2,8,128]{2,1,0:T(8,128)S(1)}, f32[2,8,128]{2,1,0:T(8,128)S(1)}, f32[64,256]{1,0:T(8,128)S(1)}, f32[64,256]{1,0:T(8,128)S(1)}) custom-call(f32[3,8,8,128]{3,2,1,0:T(8,128)} %force_ref.1, f32[8,8,128]{2,1,0:T(8,128)} %visc_ref.1, f32[64,1024]{1,0:T(8,128)} %topo_hbm.1, bf16[64,1024]{1,0:T(8,128)(2,1)} %kappa_hbm.1), custom_call_target="tpu_custom_call" | custom-call | flops 20480000 | bytes 262144 | tf_op jit(solution)/shard_map/pallas_call | solution.py:493
  10.2 0.0 collective-permute-done.odd_ref
  10.2 0.0 collective-permute-done.1.even_ref
  10.2 0.1 shard_map.61
  10.3 0.7 %collective-permute-start.2 = (f32[2,8,128]{2,1,0:T(8,128)S(1)}, f32[2,8,128]{2,1,0:T(8,128)S(1)}, u32[]{:S(2)}, u32[]{:S(2)}) collective-permute-start(f32[2,8,128]{2,1,0:T(8,128)S(1)} %get-tuple-element.31.own_odd), channel_id=1, source_target_pairs={{8,16},{16,8},{24,32},{32,24},{40,48},{48,40},{56,64},{64,56},{72,... | collective-permute-start | bytes 24584 | tf_op jit(solution)/shard_map/ppermute | solution.py:477
  11.0 5.6 %collective-permute-start.3 = (f32[2,8,128]{2,1,0:T(8,128)S(1)}, f32[2,8,128]{2,1,0:T(8,128)S(1)}, u32[]{:S(2)}, u32[]{:S(2)}) collective-permute-start(f32[2,8,128]{2,1,0:T(8,128)S(1)} %get-tuple-element.32.own_even), channel_id=1, source_target_pairs={{0,8},{8,0},{16,24},{24,16},{32,40},{40,32},{48,56},{56,48},{64,72... | collective-permute-start | bytes 24584 | tf_op jit(solution)/shard_map/ppermute | solution.py:477
  16.6 0.1 shard_map.62
  16.6 0.0 collective-permute-done.2.odd_ref
  16.6 0.9 %collective-permute-done.3.even_ref = f32[2,8,128]{2,1,0:T(8,128)S(1)} collective-permute-done((f32[2,8,128]{2,1,0:T(8,128)S(1)}, f32[2,8,128]{2,1,0:T(8,128)S(1)}, u32[]{:S(2)}, u32[]{:S(2)}) %collective-permute-start.3) | collective-permute-done | bytes 8224 | tf_op jit(solution)/shard_map/ppermute | solution.py:477
  17.6 0.1 shard_map.63
  17.7 6.7 %collective-permute-start.4 = (f32[136,128]{1,0:T(8,128)S(1)}, f32[136,128]{1,0:T(8,128)S(1)}, u32[]{:S(2)}, u32[]{:S(2)}) collective-permute-start(f32[136,128]{1,0:T(8,128)S(1)} %get-tuple-element.36), channel_id=1, source_target_pairs={{128,256},{256,128},{129,257},{257,129},{130,258},{258,130},{131,2... | collective-permute-start | bytes 208904 | tf_op jit(solution)/shard_map/ppermute | solution.py:477
  24.4 1.9 %collective-permute-start.5 = (f32[136,128]{1,0:T(8,128)S(1)}, f32[136,128]{1,0:T(8,128)S(1)}, u32[]{:S(2)}, u32[]{:S(2)}) collective-permute-start(f32[136,128]{1,0:T(8,128)S(1)} %get-tuple-element.37), channel_id=1, source_target_pairs={{0,128},{128,0},{256,384},{384,256},{1,129},{129,1},{257,385},{385... | collective-permute-start | bytes 208904 | tf_op jit(solution)/shard_map/ppermute | solution.py:477
  26.3 0.9 %shard_map.64.inner_ref = f32[48,128]{1,0:T(8,128)S(1)} custom-call(f32[64,256]{1,0:T(8,128)S(1)} %get-tuple-element.38.height_ref, f32[64,256]{1,0:T(8,128)S(1)} %get-tuple-element.39.conduct_ref), custom_call_target="tpu_custom_call" | custom-call | flops 20480000 | bytes 262144 | tf_op jit(solution)/shard_map/pallas_call | solution.py:29
  27.2 0.0 collective-permute-done.4.odd_ref
  27.2 0.3 collective-permute-done.5.even_ref
  27.5 1.3 %shard_map.65 = (f32[3,8,8,128]{3,2,1,0:T(8,128)S(1)}, f32[64,128]{1,0:T(8,128)S(1)}, f32[2,8,128]{2,1,0:T(8,128)S(1)}, f32[64,128]{1,0:T(8,128)S(1)}) custom-call(f32[48,8,128]{2,1,0:T(8,128)S(1)} %get-tuple-element.28.planes_ref, f32[96,128]{1,0:T(8,128)S(1)} %get-tuple-element.29.low_ref, f32[96,128]{1,0:T(8,128)S(1)} %get-tuple-element.30.high_ref, ...), custom_call_target="tpu_custom_call" | custom-call | flops 20480000 | bytes 262144 | tf_op jit(solution)/shard_map/pallas_call | solution.py:29
  28.8 22.9 %all_to_all.10 = f32[64,1,128]{2,1,0:T(1,128)S(1)} all-to-all(f32[64,1,128]{2,1,0:T(1,128)S(1)} %bitcast.4), channel_id=1, replica_groups=mesh['gx'=4,'gy'=16,'gz'=8] {'gx','gy'}, dimensions={0} | all-to-all | bytes 65536 | tf_op jit(solution)/shard_map/all_to_all | solution.py:526
  51.7 0.1 shard_map.66
  51.8 12.9 %all_to_all.11.parts_ref = f32[8,8,128]{2,1,0:T(8,128)S(1)} all-to-all(f32[8,8,128]{2,1,0:T(8,128)S(1)} %shard_map.66), channel_id=1, replica_groups=mesh['gx'=4,'gy'=16,'gz'=8] {'gz'}, dimensions={0} | all-to-all | bytes 65536 | tf_op jit(solution)/shard_map/all_to_all | solution.py:528
  64.7 0.9 %shard_map.67 = (f32[3,8,8,128]{3,2,1,0:T(8,128)}, f32[64,128]{1,0:T(8,128)}) custom-call(f32[8,8,128]{2,1,0:T(8,128)S(1)} %all_to_all.11.parts_ref, f32[48,8,128]{2,1,0:T(8,128)S(1)} %get-tuple-element.28.planes_ref, f32[3,8,8,128]{3,2,1,0:T(8,128)S(1)} %get-tuple-element.42.image_ref, f32[64,128]{1,0:T(8,128)S(1)} %get-tuple-element.43.height_ref), custom_call_target="tpu_custom_call" | custom-call | tf_op jit(solution)/shard_map/pallas_call | solution.py:530
Async XLA Ops:
  1.5 8.7 %collective-permute-start = (f32[4,2,8,128]{3,2,1,0:T(8,128)S(1)}, f32[4,2,8,128]{3,2,1,0:T(8,128)S(1)}, u32[]{:S(2)}, u32[]{:S(2)}) collective-permute-start(f32[4,2,8,128]{3,2,1,0:T(8,128)S(1)} %get-tuple-element.24), channel_id=1, source_target_pairs={{1,2},{2,1},{3,4},{4,3},{5,6},{6,5},{9,10},{10,9},{11,12},{12,11},... | collective-permute-start | bytes 98312 | tf_op jit(solution)/shard_map/ppermute | solution.py:477
  2.1 8.1 %collective-permute-start.1 = (f32[4,2,8,128]{3,2,1,0:T(8,128)S(1)}, f32[4,2,8,128]{3,2,1,0:T(8,128)S(1)}, u32[]{:S(2)}, u32[]{:S(2)}) collective-permute-start(f32[4,2,8,128]{3,2,1,0:T(8,128)S(1)} %get-tuple-element.25), channel_id=1, source_target_pairs={{0,1},{1,0},{2,3},{3,2},{4,5},{5,4},{6,7},{7,6},{8,9},{9,8},{10,11... | collective-permute-start | bytes 98312 | tf_op jit(solution)/shard_map/ppermute | solution.py:477
  10.3 6.3 %collective-permute-start.2 = (f32[2,8,128]{2,1,0:T(8,128)S(1)}, f32[2,8,128]{2,1,0:T(8,128)S(1)}, u32[]{:S(2)}, u32[]{:S(2)}) collective-permute-start(f32[2,8,128]{2,1,0:T(8,128)S(1)} %get-tuple-element.31.own_odd), channel_id=1, source_target_pairs={{8,16},{16,8},{24,32},{32,24},{40,48},{48,40},{56,64},{64,56},{72,... | collective-permute-start | bytes 24584 | tf_op jit(solution)/shard_map/ppermute | solution.py:477
  11.0 6.6 %collective-permute-start.3 = (f32[2,8,128]{2,1,0:T(8,128)S(1)}, f32[2,8,128]{2,1,0:T(8,128)S(1)}, u32[]{:S(2)}, u32[]{:S(2)}) collective-permute-start(f32[2,8,128]{2,1,0:T(8,128)S(1)} %get-tuple-element.32.own_even), channel_id=1, source_target_pairs={{0,8},{8,0},{16,24},{24,16},{32,40},{40,32},{48,56},{56,48},{64,72... | collective-permute-start | bytes 24584 | tf_op jit(solution)/shard_map/ppermute | solution.py:477
  17.7 9.5 %collective-permute-start.4 = (f32[136,128]{1,0:T(8,128)S(1)}, f32[136,128]{1,0:T(8,128)S(1)}, u32[]{:S(2)}, u32[]{:S(2)}) collective-permute-start(f32[136,128]{1,0:T(8,128)S(1)} %get-tuple-element.36), channel_id=1, source_target_pairs={{128,256},{256,128},{129,257},{257,129},{130,258},{258,130},{131,2... | collective-permute-start | bytes 208904 | tf_op jit(solution)/shard_map/ppermute | solution.py:477
  24.4 3.2 %collective-permute-start.5 = (f32[136,128]{1,0:T(8,128)S(1)}, f32[136,128]{1,0:T(8,128)S(1)}, u32[]{:S(2)}, u32[]{:S(2)}) collective-permute-start(f32[136,128]{1,0:T(8,128)S(1)} %get-tuple-element.37), channel_id=1, source_target_pairs={{0,128},{128,0},{256,384},{384,256},{1,129},{129,1},{257,385},{385... | collective-permute-start | bytes 208904 | tf_op jit(solution)/shard_map/ppermute | solution.py:477

commit v10 on v9

--- a/solution.py
+++ b/solution.py
@@ -317,7 +317,7 @@
 
 def operate(
     planes_ref, low_ref, high_ref, column_ref, odd_ref, even_ref, height_ref, conduct_ref, inner_ref,
-    image_ref, sums_ref, top_ref, out_ref,
+    image_ref, parts_ref, out_ref,
 ):
     lane = lanes((8, 128))
     row = lax.broadcasted_iota(jnp.int32, (8, 128), 0)
@@ -412,22 +412,21 @@
         total = jnp.where(lane // 16 == 2 + k, part, total)
     for amount in (4, 2, 1):
         total = total + rolled(total, amount, 0)
+    top = (plane(2, DEPTHS - 3), image[2, DEPTHS - 3])
+    for j in range(parts_ref.shape[0]):
+        piece = jnp.where(lane < 16, rolled(top[0], -16 * j), total)
+        parts_ref[j] = jnp.where(lane // 16 == 1, rolled(top[1], 16 - 16 * j), piece)
+
+
+def middle(parts_ref, sums_ref):
+    total = parts_ref[0]
+    for j in range(1, parts_ref.shape[0]):
+        total = total + parts_ref[j]
     for i in range(sums_ref.shape[0] // 8):
         sums_ref[8 * i : 8 * i + 8, :] = total
-    top_ref[0] = plane(2, DEPTHS - 3)
-    top_ref[1] = image[2, DEPTHS - 3]
-
-
-def middle(sums_ref, top_ref, out_ref):
-    lane = lanes((8, 128))
-    part = jnp.sum(sums_ref[...], axis=0, keepdims=True)
-    base = jnp.broadcast_to(part, (8, 128))
-    for j in range(out_ref.shape[0]):
-        piece = jnp.where(lane < 16, rolled(top_ref[0], -16 * j), base)
-        out_ref[j] = jnp.where(lane // 16 == 1, rolled(top_ref[1], 16 - 16 * j), piece)
-
-
-def finish(parts_ref, planes_ref, image_ref, height_ref, velocity_hbm, surface_hbm, velocity_ref, surface_ref, sems):
+
+
+def finish(sums_ref, parts_ref, planes_ref, image_ref, height_ref, velocity_hbm, surface_hbm, velocity_ref, surface_ref, sems):
     count = parts_ref.shape[0]
     lane = lanes((1, 128))
     top = parts_ref[count - 1]
@@ -436,9 +435,7 @@
         lax.broadcasted_iota(jnp.int32, (128, 128), 1) // 8 == lax.broadcasted_iota(jnp.int32, (128, 128), 0)
     ).astype(f32)
     wide = jnp.dot(top, spread, precision=lax.Precision.HIGHEST, preferred_element_type=f32)
-    total = parts_ref[0, 0:1, :]
-    for j in range(1, count):
-        total = total + parts_ref[j, 0:1, :]
+    total = jnp.sum(sums_ref[...], axis=0, keepdims=True)
 
     def moment(k):
         return jnp.sum(jnp.where(lane // 16 == 2 + k, total, 0.0), axis=1, keepdims=True)
@@ -518,23 +515,23 @@
     odd, even = swap(odd, even, "gx")
     (inner,) = call(inner_rows, [(48, 128)], (height, conduct))
     group = lax.axis_size("gx") * lax.axis_size("gy")
-    image, sums, top, height = call(
+    image, parts, height = call(
         operate,
-        [(3, 8, 8, 128), (group, 128), (2, 8, 128), (64, 128)],
+        [(3, 8, 8, 128), (lax.axis_size("gz"), 8, 128), (64, 128)],
         (planes, low, high, columns, odd, even, height, conduct, inner),
     )
-    sums = lax.all_to_all(sums.reshape(group, 1, 128), ("gx", "gy"), 0, 0)
-    (parts,) = call(middle, [(lax.axis_size("gz"), 8, 128)], (sums.reshape(group, 128), top))
     parts = lax.all_to_all(parts, "gz", 0, 0)
+    (sums,) = call(middle, [(group, 128)], (parts,))
+    sums = lax.all_to_all(sums.reshape(group, 1, 128), ("gx", "gy"), 0, 0).reshape(group, 128)
     shapes = ((3, 8, 8, 128), (64, 128))
     velocity, surface = pl.pallas_call(
         finish,
         out_shape=[jax.ShapeDtypeStruct(shape, f32) for shape in shapes],
-        in_specs=[vmem()] * 4,
+        in_specs=[vmem()] * 5,
         out_specs=[pl.BlockSpec(memory_space=pltpu.HBM)] * 2,
         scratch_shapes=[pltpu.VMEM(shape, f32) for shape in shapes] + [pltpu.SemaphoreType.DMA((2,))],
         compiler_params=pltpu.CompilerParams(vmem_limit_bytes=8 << 20),
-    )(parts, planes, image, height)
+    )(sums, parts, planes, image, height)
     return velocity, surface
 
 

time: 65.9 us -> 67.3 us (1.021)
  blocking collectives: 35.8 us -> 37.2 us
    all_to_all x1, blocking collectives: 22.9 us -> 24.3 us  [local(): lax.all_to_all(sums.reshape(group, 1, 128), ('gx', 'gy'), 0, 0)]
where the time goes in v10:
time: 67.3 us; the launch traced here: 66.9 us
  blocking collectives  37.2 us (55%)
  starting transfers between devices  22 us (33%)
  Pallas kernels  5.67 us (8%)
  waiting for transfers between devices  1.23 us (2%)
  between operations  0.76 us (1%)
    all_to_all x1, blocking collectives, local(): lax.all_to_all(sums.reshape(group, 1, 128), ('gx', 'gy'), 0, 0)  24.3 us
    ppermute x3, starting transfers between devices, swap(): lax.ppermute(even, axis, pairs(0))  14.1 us
    all_to_all x1, blocking collectives, local(): parts = lax.all_to_all(parts, 'gz', 0, 0)  12.9 us
    ppermute x3, starting transfers between devices, swap(): lax.ppermute(odd, axis, pairs(1))  7.98 us
    pallas_call x6, Pallas kernels, call(): pl.pallas_call(body, out_shape=[jax.ShapeDtypeStruct(s, f32) for s in out...  2.53 us
    pallas_call x1, Pallas kernels, local(): pl.pallas_call(own_block, out_shape=[jax.ShapeDtypeStruct(shape, f32) for...  1.46 us
  transfers between devices with their start and end apart: 6, of which 2 were waited for; matrix products, arithmetic and copies ran while one was open for 0% of the time, Pallas kernels for 4%

profile of v10, /device:TPU:1, one launch (start us, length us, event | category | flops | bytes accessed | tf_op | source)
XLA Modules:
  0.0 66.9 jit_solution(12566819040314806684)
XLA Ops:
  0.6 0.8 %shard_map.60 = (f32[4,2,8,128]{3,2,1,0:T(8,128)S(1)}, f32[4,2,8,128]{3,2,1,0:T(8,128)S(1)}) custom-call(f32[3,8,8,128]{3,2,1,0:T(8,128)} %force_ref.1, f32[8,8,128]{2,1,0:T(8,128)} %visc_ref.1), custom_call_target="tpu_custom_call" | custom-call | tf_op jit(solution)/shard_map/pallas_call | solution.py:481
  1.5 0.7 collective-permute-start
  2.1 6.6 %collective-permute-start.1 = (f32[4,2,8,128]{3,2,1,0:T(8,128)S(1)}, f32[4,2,8,128]{3,2,1,0:T(8,128)S(1)}, u32[]{:S(2)}, u32[]{:S(2)}) collective-permute-start(f32[4,2,8,128]{3,2,1,0:T(8,128)S(1)} %get-tuple-element.24), channel_id=1, source_target_pairs={{0,1},{1,0},{2,3},{3,2},{4,5},{5,4},{6,7},{7,6},{8,9},{9,8},{10,11... | collective-permute-start | bytes 98312 | tf_op jit(solution)/shard_map/ppermute | solution.py:474
  8.7 1.5 %shard_map.59 = (f32[4,8,8,128]{3,2,1,0:T(8,128)S(1)}, f32[2,8,128]{2,1,0:T(8,128)S(1)}, f32[2,8,128]{2,1,0:T(8,128)S(1)}, f32[64,256]{1,0:T(8,128)S(1)}, f32[64,256]{1,0:T(8,128)S(1)}) custom-call(f32[3,8,8,128]{3,2,1,0:T(8,128)} %force_ref.1, f32[8,8,128]{2,1,0:T(8,128)} %visc_ref.1, f32[64,1024]{1,0:T(8,128)} %topo_hbm.1, bf16[64,1024]{1,0:T(8,128)(2,1)} %kappa_hbm.1), custom_call_target="tpu_custom_call" | custom-call | flops 20480000 | bytes 262144 | tf_op jit(solution)/shard_map/pallas_call | solution.py:490
  10.2 0.0 collective-permute-done.odd_ref
  10.2 0.0 collective-permute-done.1.even_ref
  10.2 0.1 shard_map.61
  10.3 0.7 collective-permute-start.2
  11.0 5.6 %collective-permute-start.3 = (f32[2,8,128]{2,1,0:T(8,128)S(1)}, f32[2,8,128]{2,1,0:T(8,128)S(1)}, u32[]{:S(2)}, u32[]{:S(2)}) collective-permute-start(f32[2,8,128]{2,1,0:T(8,128)S(1)} %get-tuple-element.31.own_even), channel_id=1, source_target_pairs={{0,8},{8,0},{16,24},{24,16},{32,40},{40,32},{48,56},{56,48},{64,72... | collective-permute-start | bytes 24584 | tf_op jit(solution)/shard_map/ppermute | solution.py:474
  16.6 0.1 shard_map.62
  16.6 0.0 collective-permute-done.2.odd_ref
  16.6 0.9 %collective-permute-done.3.even_ref = f32[2,8,128]{2,1,0:T(8,128)S(1)} collective-permute-done((f32[2,8,128]{2,1,0:T(8,128)S(1)}, f32[2,8,128]{2,1,0:T(8,128)S(1)}, u32[]{:S(2)}, u32[]{:S(2)}) %collective-permute-start.3) | collective-permute-done | bytes 8224 | tf_op jit(solution)/shard_map/ppermute | solution.py:474
  17.6 0.1 shard_map.63
  17.7 6.7 %collective-permute-start.4 = (f32[136,128]{1,0:T(8,128)S(1)}, f32[136,128]{1,0:T(8,128)S(1)}, u32[]{:S(2)}, u32[]{:S(2)}) collective-permute-start(f32[136,128]{1,0:T(8,128)S(1)} %get-tuple-element.35), channel_id=1, source_target_pairs={{128,256},{256,128},{129,257},{257,129},{130,258},{258,130},{131,2... | collective-permute-start | bytes 208904 | tf_op jit(solution)/shard_map/ppermute | solution.py:474
  24.4 1.9 %collective-permute-start.5 = (f32[136,128]{1,0:T(8,128)S(1)}, f32[136,128]{1,0:T(8,128)S(1)}, u32[]{:S(2)}, u32[]{:S(2)}) collective-permute-start(f32[136,128]{1,0:T(8,128)S(1)} %get-tuple-element.36), channel_id=1, source_target_pairs={{0,128},{128,0},{256,384},{384,256},{1,129},{129,1},{257,385},{385... | collective-permute-start | bytes 208904 | tf_op jit(solution)/shard_map/ppermute | solution.py:474
  26.3 0.9 %shard_map.64.inner_ref = f32[48,128]{1,0:T(8,128)S(1)} custom-call(f32[64,256]{1,0:T(8,128)S(1)} %get-tuple-element.37.height_ref, f32[64,256]{1,0:T(8,128)S(1)} %get-tuple-element.38.conduct_ref), custom_call_target="tpu_custom_call" | custom-call | flops 20480000 | bytes 262144 | tf_op jit(solution)/shard_map/pallas_call | solution.py:29
  27.2 0.0 collective-permute-done.4.odd_ref
  27.2 0.3 collective-permute-done.5.even_ref
  27.5 1.3 %shard_map.65 = (f32[3,8,8,128]{3,2,1,0:T(8,128)S(1)}, f32[8,8,128]{2,1,0:T(8,128)S(1)}, f32[64,128]{1,0:T(8,128)S(1)}) custom-call(f32[48,8,128]{2,1,0:T(8,128)S(1)} %get-tuple-element.27.planes_ref, f32[96,128]{1,0:T(8,128)S(1)} %get-tuple-element.28.low_ref, f32[96,128]{1,0:T(8,128)S(1)} %get-tuple-element.29.high_ref, ...), custom_call_target="tpu_custom_call" | custom-call | flops 20480000 | bytes 262144 | tf_op jit(solution)/shard_map/pallas_call | solution.py:29
  28.8 12.9 %all_to_all.10.parts_ref = f32[8,8,128]{2,1,0:T(8,128)S(1)} all-to-all(f32[8,8,128]{2,1,0:T(8,128)S(1)} %get-tuple-element.39), channel_id=1, replica_groups=mesh['gx'=4,'gy'=16,'gz'=8] {'gz'}, dimensions={0} | all-to-all | bytes 65536 | tf_op jit(solution)/shard_map/all_to_all | solution.py:523
  41.8 24.3 %all_to_all.11 = f32[64,1,128]{2,1,0:T(1,128)S(1)} all-to-all(f32[64,1,128]{2,1,0:T(1,128)S(1)} %bitcast.5), channel_id=1, replica_groups=mesh['gx'=4,'gy'=16,'gz'=8] {'gx','gy'}, dimensions={0} | all-to-all | bytes 65536 | tf_op jit(solution)/shard_map/all_to_all | solution.py:525
  66.1 0.9 %shard_map.67 = (f32[3,8,8,128]{3,2,1,0:T(8,128)}, f32[64,128]{1,0:T(8,128)}) custom-call(f32[64,128]{1,0:T(8,128)S(1)} %bitcast.4, f32[8,8,128]{2,1,0:T(8,128)S(1)} %all_to_all.10.parts_ref, f32[48,8,128]{2,1,0:T(8,128)S(1)} %get-tuple-element.27.planes_ref, f32[3,8,8,128]{3,2,1,0:T(8,128)S(1)} %get-tuple-element.40.image_ref, ...), custom_call_target="tpu_custom_call" | custom-call | tf_op jit(solution)/shard_map/pallas_call | solution.py:527
  (1 shorter events, 0.0 us)
Async XLA Ops:
  1.5 8.7 %collective-permute-start = (f32[4,2,8,128]{3,2,1,0:T(8,128)S(1)}, f32[4,2,8,128]{3,2,1,0:T(8,128)S(1)}, u32[]{:S(2)}, u32[]{:S(2)}) collective-permute-start(f32[4,2,8,128]{3,2,1,0:T(8,128)S(1)} %get-tuple-element.23), channel_id=1, source_target_pairs={{1,2},{2,1},{3,4},{4,3},{5,6},{6,5},{9,10},{10,9},{11,12},{12,11},... | collective-permute-start | bytes 98312 | tf_op jit(solution)/shard_map/ppermute | solution.py:474
  2.1 8.1 %collective-permute-start.1 = (f32[4,2,8,128]{3,2,1,0:T(8,128)S(1)}, f32[4,2,8,128]{3,2,1,0:T(8,128)S(1)}, u32[]{:S(2)}, u32[]{:S(2)}) collective-permute-start(f32[4,2,8,128]{3,2,1,0:T(8,128)S(1)} %get-tuple-element.24), channel_id=1, source_target_pairs={{0,1},{1,0},{2,3},{3,2},{4,5},{5,4},{6,7},{7,6},{8,9},{9,8},{10,11... | collective-permute-start | bytes 98312 | tf_op jit(solution)/shard_map/ppermute | solution.py:474
  10.3 6.3 %collective-permute-start.2 = (f32[2,8,128]{2,1,0:T(8,128)S(1)}, f32[2,8,128]{2,1,0:T(8,128)S(1)}, u32[]{:S(2)}, u32[]{:S(2)}) collective-permute-start(f32[2,8,128]{2,1,0:T(8,128)S(1)} %get-tuple-element.30.own_odd), channel_id=1, source_target_pairs={{8,16},{16,8},{24,32},{32,24},{40,48},{48,40},{56,64},{64,56},{72,... | collective-permute-start | bytes 24584 | tf_op jit(solution)/shard_map/ppermute | solution.py:474
  11.0 6.6 %collective-permute-start.3 = (f32[2,8,128]{2,1,0:T(8,128)S(1)}, f32[2,8,128]{2,1,0:T(8,128)S(1)}, u32[]{:S(2)}, u32[]{:S(2)}) collective-permute-start(f32[2,8,128]{2,1,0:T(8,128)S(1)} %get-tuple-element.31.own_even), channel_id=1, source_target_pairs={{0,8},{8,0},{16,24},{24,16},{32,40},{40,32},{48,56},{56,48},{64,72... | collective-permute-start | bytes 24584 | tf_op jit(solution)/shard_map/ppermute | solution.py:474
  17.7 9.5 %collective-permute-start.4 = (f32[136,128]{1,0:T(8,128)S(1)}, f32[136,128]{1,0:T(8,128)S(1)}, u32[]{:S(2)}, u32[]{:S(2)}) collective-permute-start(f32[136,128]{1,0:T(8,128)S(1)} %get-tuple-element.35), channel_id=1, source_target_pairs={{128,256},{256,128},{129,257},{257,129},{130,258},{258,130},{131,2... | collective-permute-start | bytes 208904 | tf_op jit(solution)/shard_map/ppermute | solution.py:474
  24.4 3.2 %collective-permute-start.5 = (f32[136,128]{1,0:T(8,128)S(1)}, f32[136,128]{1,0:T(8,128)S(1)}, u32[]{:S(2)}, u32[]{:S(2)}) collective-permute-start(f32[136,128]{1,0:T(8,128)S(1)} %get-tuple-element.36), channel_id=1, source_target_pairs={{0,128},{128,0},{256,384},{384,256},{1,129},{129,1},{257,385},{385... | collective-permute-start | bytes 208904 | tf_op jit(solution)/shard_map/ppermute | solution.py:474

commit v11 on v9

--- a/solution.py
+++ b/solution.py
@@ -171,7 +171,7 @@
 
 def prepare_rows(
     low_ref, high_ref, own_odd, own_even, odd_ref, even_ref, height_ref, conduct_ref,
-    odd_out, even_out, column_ref, height_out, conduct_out,
+    even_out, odd_out, column_ref, height_out, conduct_out,
 ):
     g = lax.axis_index("gz")
     last = lax.axis_size("gz") - 1
@@ -316,7 +316,7 @@
 
 
 def operate(
-    planes_ref, low_ref, high_ref, column_ref, odd_ref, even_ref, height_ref, conduct_ref, inner_ref,
+    planes_ref, low_ref, high_ref, column_ref, even_ref, odd_ref, height_ref, conduct_ref, inner_ref,
     image_ref, sums_ref, top_ref, out_ref,
 ):
     lane = lanes((8, 128))
@@ -465,7 +465,7 @@
     surface_copy.wait()
 
 
-def swap(odd, even, axis):
+def swap(odd, even, axis, even_first=False):
     count = lax.axis_size(axis)
 
     def pairs(start):
@@ -474,6 +474,9 @@
             found += [(i, i + 1), (i + 1, i)]
         return found
 
+    if even_first:
+        even = lax.ppermute(even, axis, pairs(0))
+        return lax.ppermute(odd, axis, pairs(1)), even
     return lax.ppermute(odd, axis, pairs(1)), lax.ppermute(even, axis, pairs(0))
 
 
@@ -510,18 +513,18 @@
     own = (odd, even)
     odd, even = swap(odd, even, "gy")
     low, high = call(edge_rows, [(COLUMN_ROW, 128)] * 2, (planes,))
-    odd, even, columns, height, conduct = call(
+    even, odd, columns, height, conduct = call(
         prepare_rows,
         [(GX_ROWS, 128), (GX_ROWS, 128), (3, 8, 128), (64, 256), (64, 256)],
         (low, high, *own, odd, even, height, conduct),
     )
-    odd, even = swap(odd, even, "gx")
+    odd, even = swap(odd, even, "gx", even_first=True)
     (inner,) = call(inner_rows, [(48, 128)], (height, conduct))
     group = lax.axis_size("gx") * lax.axis_size("gy")
     image, sums, top, height = call(
         operate,
         [(3, 8, 8, 128), (group, 128), (2, 8, 128), (64, 128)],
-        (planes, low, high, columns, odd, even, height, conduct, inner),
+        (planes, low, high, columns, even, odd, height, conduct, inner),
     )
     sums = lax.all_to_all(sums.reshape(group, 1, 128), ("gx", "gy"), 0, 0)
     (parts,) = call(middle, [(lax.axis_size("gz"), 8, 128)], (sums.reshape(group, 128), top))

time: 65.9 us -> 67.2 us (1.020)
  waiting for transfers between devices: 1.23 us -> 2.47 us
    ppermute x0 -> x2, starting transfers between devices: none -> 8.58 us  [the longest x1 5.42 us: swap(): even = lax.ppermute(even, axis, pairs(0))]
    ppermute x3 -> x2, starting transfers between devices: 7.98 us -> 1.32 us  [swap(): lax.ppermute(odd, axis, pairs(1))]
    ppermute x3 -> x2, starting transfers between devices: 14.1 us -> 12.1 us  [swap(): lax.ppermute(even, axis, pairs(0))]
    ppermute x0 -> x2, waiting for transfers between devices: none -> 1.53 us  [the longest x1 1.53 us: swap(): return (lax.ppermute(odd, axis, pairs(1)), even)]
where the time goes in v11:
time: 67.2 us; the launch traced here: 66.8 us
  blocking collectives  35.8 us (53%)
  starting transfers between devices  22 us (33%)
  Pallas kernels  5.74 us (9%)
  waiting for transfers between devices  2.47 us (4%)
  between operations  0.76 us (1%)
    all_to_all x1, blocking collectives, local(): sums = lax.all_to_all(sums.reshape(group, 1, 128), ('gx', 'gy'), 0, 0)  22.9 us
    all_to_all x1, blocking collectives, local(): parts = lax.all_to_all(parts, 'gz', 0, 0)  12.9 us
    ppermute x2, starting transfers between devices, swap(): lax.ppermute(even, axis, pairs(0))  12.1 us
    ppermute x1, starting transfers between devices, swap(): even = lax.ppermute(even, axis, pairs(0))  5.42 us
    ppermute x1, starting transfers between devices, swap(): return (lax.ppermute(odd, axis, pairs(1)), even)  3.15 us
    pallas_call x6, Pallas kernels, call(): pl.pallas_call(body, out_shape=[jax.ShapeDtypeStruct(s, f32) for s in out...  2.6 us
    ppermute x1, waiting for transfers between devices, swap(): return (lax.ppermute(odd, axis, pairs(1)), even)  1.53 us
    pallas_call x1, Pallas kernels, local(): pl.pallas_call(own_block, out_shape=[jax.ShapeDtypeStruct(shape, f32) for...  1.46 us
  transfers between devices with their start and end apart: 6, of which 2 were waited for; matrix products, arithmetic and copies ran while one was open for 0% of the time, Pallas kernels for 4%

profile of v11, /device:TPU:1, one launch (start us, length us, event | category | flops | bytes accessed | tf_op | source)
XLA Modules:
  0.0 66.8 jit_solution(14525441564674663569)
XLA Ops:
  0.6 0.8 %shard_map.60 = (f32[4,2,8,128]{3,2,1,0:T(8,128)S(1)}, f32[4,2,8,128]{3,2,1,0:T(8,128)S(1)}) custom-call(f32[3,8,8,128]{3,2,1,0:T(8,128)} %force_ref.1, f32[8,8,128]{2,1,0:T(8,128)} %visc_ref.1), custom_call_target="tpu_custom_call" | custom-call | tf_op jit(solution)/shard_map/pallas_call | solution.py:487
  1.5 0.7 collective-permute-start
  2.1 6.6 %collective-permute-start.1 = (f32[4,2,8,128]{3,2,1,0:T(8,128)S(1)}, f32[4,2,8,128]{3,2,1,0:T(8,128)S(1)}, u32[]{:S(2)}, u32[]{:S(2)}) collective-permute-start(f32[4,2,8,128]{3,2,1,0:T(8,128)S(1)} %get-tuple-element.25), channel_id=1, source_target_pairs={{0,1},{1,0},{2,3},{3,2},{4,5},{5,4},{6,7},{7,6},{8,9},{9,8},{10,11... | collective-permute-start | bytes 98312 | tf_op jit(solution)/shard_map/ppermute | solution.py:480
  8.7 1.5 %shard_map.59 = (f32[4,8,8,128]{3,2,1,0:T(8,128)S(1)}, f32[2,8,128]{2,1,0:T(8,128)S(1)}, f32[2,8,128]{2,1,0:T(8,128)S(1)}, f32[64,256]{1,0:T(8,128)S(1)}, f32[64,256]{1,0:T(8,128)S(1)}) custom-call(f32[3,8,8,128]{3,2,1,0:T(8,128)} %force_ref.1, f32[8,8,128]{2,1,0:T(8,128)} %visc_ref.1, f32[64,1024]{1,0:T(8,128)} %topo_hbm.1, bf16[64,1024]{1,0:T(8,128)(2,1)} %kappa_hbm.1), custom_call_target="tpu_custom_call" | custom-call | flops 20480000 | bytes 262144 | tf_op jit(solution)/shard_map/pallas_call | solution.py:496
  10.2 0.0 collective-permute-done.odd_ref
  10.2 0.0 collective-permute-done.1.even_ref
  10.2 0.1 shard_map.61
  10.3 0.7 collective-permute-start.2
  11.0 5.6 %collective-permute-start.3 = (f32[2,8,128]{2,1,0:T(8,128)S(1)}, f32[2,8,128]{2,1,0:T(8,128)S(1)}, u32[]{:S(2)}, u32[]{:S(2)}) collective-permute-start(f32[2,8,128]{2,1,0:T(8,128)S(1)} %get-tuple-element.32.own_even), channel_id=1, source_target_pairs={{0,8},{8,0},{16,24},{24,16},{32,40},{40,32},{48,56},{56,48},{64,72... | collective-permute-start | bytes 24584 | tf_op jit(solution)/shard_map/ppermute | solution.py:480
  16.6 0.1 shard_map.62
  16.6 0.0 collective-permute-done.2.odd_ref
  16.6 0.9 %collective-permute-done.3.even_ref = f32[2,8,128]{2,1,0:T(8,128)S(1)} collective-permute-done((f32[2,8,128]{2,1,0:T(8,128)S(1)}, f32[2,8,128]{2,1,0:T(8,128)S(1)}, u32[]{:S(2)}, u32[]{:S(2)}) %collective-permute-start.3) | collective-permute-done | bytes 8224 | tf_op jit(solution)/shard_map/ppermute | solution.py:480
  17.6 0.1 shard_map.63
  17.7 5.4 %collective-permute-start.4 = (f32[136,128]{1,0:T(8,128)S(1)}, f32[136,128]{1,0:T(8,128)S(1)}, u32[]{:S(2)}, u32[]{:S(2)}) collective-permute-start(f32[136,128]{1,0:T(8,128)S(1)} %get-tuple-element.36), channel_id=1, source_target_pairs={{0,128},{128,0},{256,384},{384,256},{1,129},{129,1},{257,385},{385... | collective-permute-start | bytes 208904 | tf_op jit(solution)/shard_map/ppermute | solution.py:478
  23.1 3.2 %collective-permute-start.5 = (f32[136,128]{1,0:T(8,128)S(1)}, f32[136,128]{1,0:T(8,128)S(1)}, u32[]{:S(2)}, u32[]{:S(2)}) collective-permute-start(f32[136,128]{1,0:T(8,128)S(1)} %get-tuple-element.37), channel_id=1, source_target_pairs={{128,256},{256,128},{129,257},{257,129},{130,258},{258,130},{131,2... | collective-permute-start | bytes 208904 | tf_op jit(solution)/shard_map/ppermute | solution.py:479
  26.3 0.9 %shard_map.64.inner_ref = f32[48,128]{1,0:T(8,128)S(1)} custom-call(f32[64,256]{1,0:T(8,128)S(1)} %get-tuple-element.38.height_ref, f32[64,256]{1,0:T(8,128)S(1)} %get-tuple-element.39.conduct_ref), custom_call_target="tpu_custom_call" | custom-call | flops 20480000 | bytes 262144 | tf_op jit(solution)/shard_map/pallas_call | solution.py:29
  27.2 0.0 collective-permute-done.4.even_ref
  27.2 1.5 %collective-permute-done.5.odd_ref = f32[136,128]{1,0:T(8,128)S(1)} collective-permute-done((f32[136,128]{1,0:T(8,128)S(1)}, f32[136,128]{1,0:T(8,128)S(1)}, u32[]{:S(2)}, u32[]{:S(2)}) %collective-permute-start.5) | collective-permute-done | bytes 69664 | tf_op jit(solution)/shard_map/ppermute | solution.py:479
  28.8 1.3 %shard_map.65 = (f32[3,8,8,128]{3,2,1,0:T(8,128)S(1)}, f32[64,128]{1,0:T(8,128)S(1)}, f32[2,8,128]{2,1,0:T(8,128)S(1)}, f32[64,128]{1,0:T(8,128)S(1)}) custom-call(f32[48,8,128]{2,1,0:T(8,128)S(1)} %get-tuple-element.28.planes_ref, f32[96,128]{1,0:T(8,128)S(1)} %get-tuple-element.29.low_ref, f32[96,128]{1,0:T(8,128)S(1)} %get-tuple-element.30.high_ref, ...), custom_call_target="tpu_custom_call" | custom-call | flops 20480000 | bytes 262144 | tf_op jit(solution)/shard_map/pallas_call | solution.py:29
  30.1 22.9 %all_to_all.10 = f32[64,1,128]{2,1,0:T(1,128)S(1)} all-to-all(f32[64,1,128]{2,1,0:T(1,128)S(1)} %bitcast.4), channel_id=1, replica_groups=mesh['gx'=4,'gy'=16,'gz'=8] {'gx','gy'}, dimensions={0} | all-to-all | bytes 65536 | tf_op jit(solution)/shard_map/all_to_all | solution.py:529
  53.0 0.1 shard_map.66
  53.0 12.9 %all_to_all.11.parts_ref = f32[8,8,128]{2,1,0:T(8,128)S(1)} all-to-all(f32[8,8,128]{2,1,0:T(8,128)S(1)} %shard_map.66), channel_id=1, replica_groups=mesh['gx'=4,'gy'=16,'gz'=8] {'gz'}, dimensions={0} | all-to-all | bytes 65536 | tf_op jit(solution)/shard_map/all_to_all | solution.py:531
  66.0 0.9 %shard_map.67 = (f32[3,8,8,128]{3,2,1,0:T(8,128)}, f32[64,128]{1,0:T(8,128)}) custom-call(f32[8,8,128]{2,1,0:T(8,128)S(1)} %all_to_all.11.parts_ref, f32[48,8,128]{2,1,0:T(8,128)S(1)} %get-tuple-element.28.planes_ref, f32[3,8,8,128]{3,2,1,0:T(8,128)S(1)} %get-tuple-element.42.image_ref, f32[64,128]{1,0:T(8,128)S(1)} %get-tuple-element.43.height_ref), custom_call_target="tpu_custom_call" | custom-call | tf_op jit(solution)/shard_map/pallas_call | solution.py:533
Async XLA Ops:
  1.5 8.7 %collective-permute-start = (f32[4,2,8,128]{3,2,1,0:T(8,128)S(1)}, f32[4,2,8,128]{3,2,1,0:T(8,128)S(1)}, u32[]{:S(2)}, u32[]{:S(2)}) collective-permute-start(f32[4,2,8,128]{3,2,1,0:T(8,128)S(1)} %get-tuple-element.24), channel_id=1, source_target_pairs={{1,2},{2,1},{3,4},{4,3},{5,6},{6,5},{9,10},{10,9},{11,12},{12,11},... | collective-permute-start | bytes 98312 | tf_op jit(solution)/shard_map/ppermute | solution.py:480
  2.1 8.1 %collective-permute-start.1 = (f32[4,2,8,128]{3,2,1,0:T(8,128)S(1)}, f32[4,2,8,128]{3,2,1,0:T(8,128)S(1)}, u32[]{:S(2)}, u32[]{:S(2)}) collective-permute-start(f32[4,2,8,128]{3,2,1,0:T(8,128)S(1)} %get-tuple-element.25), channel_id=1, source_target_pairs={{0,1},{1,0},{2,3},{3,2},{4,5},{5,4},{6,7},{7,6},{8,9},{9,8},{10,11... | collective-permute-start | bytes 98312 | tf_op jit(solution)/shard_map/ppermute | solution.py:480
  10.3 6.3 %collective-permute-start.2 = (f32[2,8,128]{2,1,0:T(8,128)S(1)}, f32[2,8,128]{2,1,0:T(8,128)S(1)}, u32[]{:S(2)}, u32[]{:S(2)}) collective-permute-start(f32[2,8,128]{2,1,0:T(8,128)S(1)} %get-tuple-element.31.own_odd), channel_id=1, source_target_pairs={{8,16},{16,8},{24,32},{32,24},{40,48},{48,40},{56,64},{64,56},{72,... | collective-permute-start | bytes 24584 | tf_op jit(solution)/shard_map/ppermute | solution.py:480
  11.0 6.6 %collective-permute-start.3 = (f32[2,8,128]{2,1,0:T(8,128)S(1)}, f32[2,8,128]{2,1,0:T(8,128)S(1)}, u32[]{:S(2)}, u32[]{:S(2)}) collective-permute-start(f32[2,8,128]{2,1,0:T(8,128)S(1)} %get-tuple-element.32.own_even), channel_id=1, source_target_pairs={{0,8},{8,0},{16,24},{24,16},{32,40},{40,32},{48,56},{56,48},{64,72... | collective-permute-start | bytes 24584 | tf_op jit(solution)/shard_map/ppermute | solution.py:480
  17.7 9.5 %collective-permute-start.4 = (f32[136,128]{1,0:T(8,128)S(1)}, f32[136,128]{1,0:T(8,128)S(1)}, u32[]{:S(2)}, u32[]{:S(2)}) collective-permute-start(f32[136,128]{1,0:T(8,128)S(1)} %get-tuple-element.36), channel_id=1, source_target_pairs={{0,128},{128,0},{256,384},{384,256},{1,129},{129,1},{257,385},{385... | collective-permute-start | bytes 208904 | tf_op jit(solution)/shard_map/ppermute | solution.py:478
  23.1 5.6 %collective-permute-start.5 = (f32[136,128]{1,0:T(8,128)S(1)}, f32[136,128]{1,0:T(8,128)S(1)}, u32[]{:S(2)}, u32[]{:S(2)}) collective-permute-start(f32[136,128]{1,0:T(8,128)S(1)} %get-tuple-element.37), channel_id=1, source_target_pairs={{128,256},{256,128},{129,257},{257,129},{130,258},{258,130},{131,2... | collective-permute-start | bytes 208904 | tf_op jit(solution)/shard_map/ppermute | solution.py:479

commit v12 on v9

--- a/solution.py
+++ b/solution.py
@@ -420,25 +420,42 @@
 
 def middle(sums_ref, top_ref, out_ref):
     lane = lanes((8, 128))
+    row = lax.broadcasted_iota(jnp.int32, (8, 128), 0)
     part = jnp.sum(sums_ref[...], axis=0, keepdims=True)
-    base = jnp.broadcast_to(part, (8, 128))
+    flat = []
+    for i in range(2):
+        found = top_ref[i]
+        for k in range(1, 8):
+            found = jnp.where(
+                lane // 16 == lax.rem(row + k, 8), rolled(rolled(top_ref[i], -k, 0), 16 * k), found
+            )
+        flat.append(found)
     for j in range(out_ref.shape[0]):
-        piece = jnp.where(lane < 16, rolled(top_ref[0], -16 * j), base)
-        out_ref[j] = jnp.where(lane // 16 == 1, rolled(top_ref[1], 16 - 16 * j), piece)
+        out_ref[j, 0:1, :] = flat[0][j : j + 1]
+        out_ref[j, 1:2, :] = flat[1][j : j + 1]
+        out_ref[j, 2:3, :] = part
+        out_ref[j, 3:4, :] = part
 
 
 def finish(parts_ref, planes_ref, image_ref, height_ref, velocity_hbm, surface_hbm, velocity_ref, surface_ref, sems):
     count = parts_ref.shape[0]
     lane = lanes((1, 128))
-    top = parts_ref[count - 1]
-    top = jnp.where(lanes((16, 128)) < 16, jnp.concatenate([top, rolled(top, -16)], axis=0), 0.0)
+    row = lax.broadcasted_iota(jnp.int32, (8, 128), 0)
+    found = []
+    for i in range(2):
+        flat = jnp.broadcast_to(parts_ref[count - 1, i : i + 1, :], (8, 128))
+        cells = flat
+        for r in range(1, 8):
+            cells = jnp.where(row == r, rolled(flat, -16 * r), cells)
+        found.append(cells)
+    top = jnp.where(lanes((16, 128)) < 16, jnp.concatenate(found, axis=0), 0.0)
     spread = (
         lax.broadcasted_iota(jnp.int32, (128, 128), 1) // 8 == lax.broadcasted_iota(jnp.int32, (128, 128), 0)
     ).astype(f32)
     wide = jnp.dot(top, spread, precision=lax.Precision.HIGHEST, preferred_element_type=f32)
-    total = parts_ref[0, 0:1, :]
+    total = parts_ref[0, 2:3, :]
     for j in range(1, count):
-        total = total + parts_ref[j, 0:1, :]
+        total = total + parts_ref[j, 2:3, :]
 
     def moment(k):
         return jnp.sum(jnp.where(lane // 16 == 2 + k, total, 0.0), axis=1, keepdims=True)
@@ -524,7 +541,7 @@
         (planes, low, high, columns, odd, even, height, conduct, inner),
     )
     sums = lax.all_to_all(sums.reshape(group, 1, 128), ("gx", "gy"), 0, 0)
-    (parts,) = call(middle, [(lax.axis_size("gz"), 8, 128)], (sums.reshape(group, 128), top))
+    (parts,) = call(middle, [(lax.axis_size("gz"), 4, 128)], (sums.reshape(group, 128), top))
     parts = lax.all_to_all(parts, "gz", 0, 0)
     shapes = ((3, 8, 8, 128), (64, 128))
     velocity, surface = pl.pallas_call(

time: 65.9 us -> 65.7 us (level)
  no operation moved by 1% of the time
where the time goes in v12:
time: 65.7 us; the launch traced here: 65.3 us
  blocking collectives  35.5 us (54%)
  starting transfers between devices  22 us (33%)
  Pallas kernels  5.76 us (9%)
  waiting for transfers between devices  1.23 us (2%)
  between operations  0.76 us (1%)
    all_to_all x1, blocking collectives, local(): sums = lax.all_to_all(sums.reshape(group, 1, 128), ('gx', 'gy'), 0, 0)  22.9 us
    ppermute x3, starting transfers between devices, swap(): lax.ppermute(even, axis, pairs(0))  14.1 us
    all_to_all x1, blocking collectives, local(): parts = lax.all_to_all(parts, 'gz', 0, 0)  12.7 us
    ppermute x3, starting transfers between devices, swap(): lax.ppermute(odd, axis, pairs(1))  7.98 us
    pallas_call x6, Pallas kernels, call(): pl.pallas_call(body, out_shape=[jax.ShapeDtypeStruct(s, f32) for s in out...  2.6 us
    pallas_call x1, Pallas kernels, local(): pl.pallas_call(own_block, out_shape=[jax.ShapeDtypeStruct(shape, f32) for...  1.46 us
  transfers between devices with their start and end apart: 6, of which 2 were waited for; matrix products, arithmetic and copies ran while one was open for 0% of the time, Pallas kernels for 4%

profile of v12, /device:TPU:1, one launch (start us, length us, event | category | flops | bytes accessed | tf_op | source)
XLA Modules:
  0.0 65.3 jit_solution(7154185496287072888)
XLA Ops:
  0.6 0.8 %shard_map.60 = (f32[4,2,8,128]{3,2,1,0:T(8,128)S(1)}, f32[4,2,8,128]{3,2,1,0:T(8,128)S(1)}) custom-call(f32[3,8,8,128]{3,2,1,0:T(8,128)} %force_ref.1, f32[8,8,128]{2,1,0:T(8,128)} %visc_ref.1), custom_call_target="tpu_custom_call" | custom-call | tf_op jit(solution)/shard_map/pallas_call | solution.py:501
  1.5 0.7 %collective-permute-start = (f32[4,2,8,128]{3,2,1,0:T(8,128)S(1)}, f32[4,2,8,128]{3,2,1,0:T(8,128)S(1)}, u32[]{:S(2)}, u32[]{:S(2)}) collective-permute-start(f32[4,2,8,128]{3,2,1,0:T(8,128)S(1)} %get-tuple-element.24), channel_id=1, source_target_pairs={{1,2},{2,1},{3,4},{4,3},{5,6},{6,5},{9,10},{10,9},{11,12},{12,11},... | collective-permute-start | bytes 98312 | tf_op jit(solution)/shard_map/ppermute | solution.py:494
  2.1 6.6 %collective-permute-start.1 = (f32[4,2,8,128]{3,2,1,0:T(8,128)S(1)}, f32[4,2,8,128]{3,2,1,0:T(8,128)S(1)}, u32[]{:S(2)}, u32[]{:S(2)}) collective-permute-start(f32[4,2,8,128]{3,2,1,0:T(8,128)S(1)} %get-tuple-element.25), channel_id=1, source_target_pairs={{0,1},{1,0},{2,3},{3,2},{4,5},{5,4},{6,7},{7,6},{8,9},{9,8},{10,11... | collective-permute-start | bytes 98312 | tf_op jit(solution)/shard_map/ppermute | solution.py:494
  8.7 1.5 %shard_map.59 = (f32[4,8,8,128]{3,2,1,0:T(8,128)S(1)}, f32[2,8,128]{2,1,0:T(8,128)S(1)}, f32[2,8,128]{2,1,0:T(8,128)S(1)}, f32[64,256]{1,0:T(8,128)S(1)}, f32[64,256]{1,0:T(8,128)S(1)}) custom-call(f32[3,8,8,128]{3,2,1,0:T(8,128)} %force_ref.1, f32[8,8,128]{2,1,0:T(8,128)} %visc_ref.1, f32[64,1024]{1,0:T(8,128)} %topo_hbm.1, bf16[64,1024]{1,0:T(8,128)(2,1)} %kappa_hbm.1), custom_call_target="tpu_custom_call" | custom-call | flops 20480000 | bytes 262144 | tf_op jit(solution)/shard_map/pallas_call | solution.py:510
  10.2 0.0 collective-permute-done.odd_ref
  10.2 0.0 collective-permute-done.1.even_ref
  10.2 0.1 shard_map.61
  10.3 0.7 %collective-permute-start.2 = (f32[2,8,128]{2,1,0:T(8,128)S(1)}, f32[2,8,128]{2,1,0:T(8,128)S(1)}, u32[]{:S(2)}, u32[]{:S(2)}) collective-permute-start(f32[2,8,128]{2,1,0:T(8,128)S(1)} %get-tuple-element.31.own_odd), channel_id=1, source_target_pairs={{8,16},{16,8},{24,32},{32,24},{40,48},{48,40},{56,64},{64,56},{72,... | collective-permute-start | bytes 24584 | tf_op jit(solution)/shard_map/ppermute | solution.py:494
  11.0 5.6 %collective-permute-start.3 = (f32[2,8,128]{2,1,0:T(8,128)S(1)}, f32[2,8,128]{2,1,0:T(8,128)S(1)}, u32[]{:S(2)}, u32[]{:S(2)}) collective-permute-start(f32[2,8,128]{2,1,0:T(8,128)S(1)} %get-tuple-element.32.own_even), channel_id=1, source_target_pairs={{0,8},{8,0},{16,24},{24,16},{32,40},{40,32},{48,56},{56,48},{64,72... | collective-permute-start | bytes 24584 | tf_op jit(solution)/shard_map/ppermute | solution.py:494
  16.6 0.1 shard_map.62
  16.6 0.0 collective-permute-done.2.odd_ref
  16.6 0.9 %collective-permute-done.3.even_ref = f32[2,8,128]{2,1,0:T(8,128)S(1)} collective-permute-done((f32[2,8,128]{2,1,0:T(8,128)S(1)}, f32[2,8,128]{2,1,0:T(8,128)S(1)}, u32[]{:S(2)}, u32[]{:S(2)}) %collective-permute-start.3) | collective-permute-done | bytes 8224 | tf_op jit(solution)/shard_map/ppermute | solution.py:494
  17.6 0.1 shard_map.63
  17.7 6.7 %collective-permute-start.4 = (f32[136,128]{1,0:T(8,128)S(1)}, f32[136,128]{1,0:T(8,128)S(1)}, u32[]{:S(2)}, u32[]{:S(2)}) collective-permute-start(f32[136,128]{1,0:T(8,128)S(1)} %get-tuple-element.36), channel_id=1, source_target_pairs={{128,256},{256,128},{129,257},{257,129},{130,258},{258,130},{131,2... | collective-permute-start | bytes 208904 | tf_op jit(solution)/shard_map/ppermute | solution.py:494
  24.4 1.9 %collective-permute-start.5 = (f32[136,128]{1,0:T(8,128)S(1)}, f32[136,128]{1,0:T(8,128)S(1)}, u32[]{:S(2)}, u32[]{:S(2)}) collective-permute-start(f32[136,128]{1,0:T(8,128)S(1)} %get-tuple-element.37), channel_id=1, source_target_pairs={{0,128},{128,0},{256,384},{384,256},{1,129},{129,1},{257,385},{385... | collective-permute-start | bytes 208904 | tf_op jit(solution)/shard_map/ppermute | solution.py:494
  26.3 0.9 %shard_map.64.inner_ref = f32[48,128]{1,0:T(8,128)S(1)} custom-call(f32[64,256]{1,0:T(8,128)S(1)} %get-tuple-element.38.height_ref, f32[64,256]{1,0:T(8,128)S(1)} %get-tuple-element.39.conduct_ref), custom_call_target="tpu_custom_call" | custom-call | flops 20480000 | bytes 262144 | tf_op jit(solution)/shard_map/pallas_call | solution.py:29
  27.2 0.0 collective-permute-done.4.odd_ref
  27.2 0.3 collective-permute-done.5.even_ref
  27.5 1.3 %shard_map.65 = (f32[3,8,8,128]{3,2,1,0:T(8,128)S(1)}, f32[64,128]{1,0:T(8,128)S(1)}, f32[2,8,128]{2,1,0:T(8,128)S(1)}, f32[64,128]{1,0:T(8,128)S(1)}) custom-call(f32[48,8,128]{2,1,0:T(8,128)S(1)} %get-tuple-element.28.planes_ref, f32[96,128]{1,0:T(8,128)S(1)} %get-tuple-element.29.low_ref, f32[96,128]{1,0:T(8,128)S(1)} %get-tuple-element.30.high_ref, ...), custom_call_target="tpu_custom_call" | custom-call | flops 20480000 | bytes 262144 | tf_op jit(solution)/shard_map/pallas_call | solution.py:29
  28.8 22.9 %all_to_all.10 = f32[64,1,128]{2,1,0:T(1,128)S(1)} all-to-all(f32[64,1,128]{2,1,0:T(1,128)S(1)} %bitcast.4), channel_id=1, replica_groups=mesh['gx'=4,'gy'=16,'gz'=8] {'gx','gy'}, dimensions={0} | all-to-all | bytes 65536 | tf_op jit(solution)/shard_map/all_to_all | solution.py:543
  51.7 0.1 shard_map.66
  51.8 12.7 %all_to_all.11.parts_ref = f32[8,4,128]{2,1,0:T(4,128)S(1)} all-to-all(f32[8,4,128]{2,1,0:T(4,128)S(1)} %shard_map.66), channel_id=1, replica_groups=mesh['gx'=4,'gy'=16,'gz'=8] {'gz'}, dimensions={0} | all-to-all | bytes 32768 | tf_op jit(solution)/shard_map/all_to_all | solution.py:545
  64.4 0.9 %shard_map.67 = (f32[3,8,8,128]{3,2,1,0:T(8,128)}, f32[64,128]{1,0:T(8,128)}) custom-call(f32[8,4,128]{2,1,0:T(4,128)S(1)} %all_to_all.11.parts_ref, f32[48,8,128]{2,1,0:T(8,128)S(1)} %get-tuple-element.28.planes_ref, f32[3,8,8,128]{3,2,1,0:T(8,128)S(1)} %get-tuple-element.42.image_ref, f32[64,128]{1,0:T(8,128)S(1)} %get-tuple-element.43.height_ref), custom_call_target="tpu_custom_call" | custom-call | tf_op jit(solution)/shard_map/pallas_call | solution.py:547
Async XLA Ops:
  1.5 8.7 %collective-permute-start = (f32[4,2,8,128]{3,2,1,0:T(8,128)S(1)}, f32[4,2,8,128]{3,2,1,0:T(8,128)S(1)}, u32[]{:S(2)}, u32[]{:S(2)}) collective-permute-start(f32[4,2,8,128]{3,2,1,0:T(8,128)S(1)} %get-tuple-element.24), channel_id=1, source_target_pairs={{1,2},{2,1},{3,4},{4,3},{5,6},{6,5},{9,10},{10,9},{11,12},{12,11},... | collective-permute-start | bytes 98312 | tf_op jit(solution)/shard_map/ppermute | solution.py:494
  2.1 8.1 %collective-permute-start.1 = (f32[4,2,8,128]{3,2,1,0:T(8,128)S(1)}, f32[4,2,8,128]{3,2,1,0:T(8,128)S(1)}, u32[]{:S(2)}, u32[]{:S(2)}) collective-permute-start(f32[4,2,8,128]{3,2,1,0:T(8,128)S(1)} %get-tuple-element.25), channel_id=1, source_target_pairs={{0,1},{1,0},{2,3},{3,2},{4,5},{5,4},{6,7},{7,6},{8,9},{9,8},{10,11... | collective-permute-start | bytes 98312 | tf_op jit(solution)/shard_map/ppermute | solution.py:494
  10.3 6.3 %collective-permute-start.2 = (f32[2,8,128]{2,1,0:T(8,128)S(1)}, f32[2,8,128]{2,1,0:T(8,128)S(1)}, u32[]{:S(2)}, u32[]{:S(2)}) collective-permute-start(f32[2,8,128]{2,1,0:T(8,128)S(1)} %get-tuple-element.31.own_odd), channel_id=1, source_target_pairs={{8,16},{16,8},{24,32},{32,24},{40,48},{48,40},{56,64},{64,56},{72,... | collective-permute-start | bytes 24584 | tf_op jit(solution)/shard_map/ppermute | solution.py:494
  11.0 6.6 %collective-permute-start.3 = (f32[2,8,128]{2,1,0:T(8,128)S(1)}, f32[2,8,128]{2,1,0:T(8,128)S(1)}, u32[]{:S(2)}, u32[]{:S(2)}) collective-permute-start(f32[2,8,128]{2,1,0:T(8,128)S(1)} %get-tuple-element.32.own_even), channel_id=1, source_target_pairs={{0,8},{8,0},{16,24},{24,16},{32,40},{40,32},{48,56},{56,48},{64,72... | collective-permute-start | bytes 24584 | tf_op jit(solution)/shard_map/ppermute | solution.py:494
  17.7 9.5 %collective-permute-start.4 = (f32[136,128]{1,0:T(8,128)S(1)}, f32[136,128]{1,0:T(8,128)S(1)}, u32[]{:S(2)}, u32[]{:S(2)}) collective-permute-start(f32[136,128]{1,0:T(8,128)S(1)} %get-tuple-element.36), channel_id=1, source_target_pairs={{128,256},{256,128},{129,257},{257,129},{130,258},{258,130},{131,2... | collective-permute-start | bytes 208904 | tf_op jit(solution)/shard_map/ppermute | solution.py:494
  24.4 3.2 %collective-permute-start.5 = (f32[136,128]{1,0:T(8,128)S(1)}, f32[136,128]{1,0:T(8,128)S(1)}, u32[]{:S(2)}, u32[]{:S(2)}) collective-permute-start(f32[136,128]{1,0:T(8,128)S(1)} %get-tuple-element.37), channel_id=1, source_target_pairs={{0,128},{128,0},{256,384},{384,256},{1,129},{129,1},{257,385},{385... | collective-permute-start | bytes 208904 | tf_op jit(solution)/shard_map/ppermute | solution.py:494

commit v13 on v12

--- a/solution.py
+++ b/solution.py
@@ -16,7 +16,7 @@
 PLANES = 4 * DEPTHS
 COLUMN_ROW = 8 * DEPTHS
 SURFACE_ROW = COLUMN_ROW + 8
-GX_ROWS = SURFACE_ROW + 32
+GX_ROWS = SURFACE_ROW + 16
 
 f32 = jnp.float32
 
@@ -198,17 +198,12 @@
     for depth in range(DEPTHS):
         rows = slice(8 * depth, 8 * depth + 8)
         send(rows, low_ref[rows, :], high_ref[rows, :])
-    pad = [jnp.zeros((2, 128), f32)]
-    send(
-        slice(COLUMN_ROW, SURFACE_ROW),
-        jnp.concatenate([x[0:2] for x in levels] + pad, axis=0),
-        jnp.concatenate([x[6:8] for x in levels] + pad, axis=0),
-    )
     for i in range(3):
         column_ref[i] = levels[i]
     slot = 0
+    low_sides, high_sides = [], []
     for index, (source, target) in enumerate(((height_ref, height_out), (conduct_ref, conduct_out))):
-        base = SURFACE_ROW + 16 * index
+        base = SURFACE_ROW + 8 * index
         for r in range(8):
             rows = slice(8 * r, 8 * r + 8)
             main = source[rows, 0:128]
@@ -218,11 +213,20 @@
             target[rows, 0:128] = main
             target[rows, 128:256] = side
             if r == 0:
-                first = (main, side)
+                first = main
+                low_sides.append(side)
             if r == 7:
-                send(slice(base, base + 8), first[0], main)
-                send(slice(base + 8, base + 16), first[1], side)
+                send(slice(base, base + 8), first, main)
+                high_sides.append(side)
             slot += 1
+    pad = [jnp.zeros((2, 128), f32)]
+    shared = []
+    for sides, rows in ((low_sides, slice(0, 2)), (high_sides, slice(6, 8))):
+        found = rolled(jnp.concatenate([x[rows] for x in levels] + pad, axis=0), 16)
+        found = jnp.where((lane < 8) | (lane >= 120), sides[0], found)
+        found = jnp.where(lane // 8 == 1, rolled(sides[1], 8), found)
+        shared.append(jnp.where(lane // 8 == 14, rolled(sides[1], -8), found))
+    send(slice(COLUMN_ROW, SURFACE_ROW), *shared)
 
 
 def weighted(before, here, after):
@@ -324,20 +328,31 @@
     wide = lanes((16, 128))
     before, after = sided(odd_ref, even_ref, "gx")
 
-    def banded(source, base):
-        def joined(side):
-            return jnp.concatenate([side(slice(base, base + 8)), side(slice(base + 8, base + 16))], axis=1)
-
-        return jnp.concatenate([source[48:64, :], joined(after), joined(before), source[0:16, :]], axis=0)
-
-    band = steps(banded(height_ref, SURFACE_ROW), banded(conduct_ref, SURFACE_ROW + 16))
+    def parted(shared):
+        edge = (lane < 8) | (lane >= 120)
+        conduct = jnp.where(lane < 8, rolled(shared, -8), jnp.where(lane >= 120, rolled(shared, 8), 0.0))
+        return jnp.where(edge, shared, 0.0), conduct, jnp.where(lane < 96, rolled(shared, -16), 0.0)
+
+    shared_before = parted(before(slice(COLUMN_ROW, SURFACE_ROW)))
+    shared_after = parted(after(slice(COLUMN_ROW, SURFACE_ROW)))
+
+    def banded(source, index):
+        rows = slice(SURFACE_ROW + 8 * index, SURFACE_ROW + 8 * index + 8)
+        outer = [
+            jnp.concatenate([side(rows), shared[index]], axis=1)
+            for side, shared in ((after, shared_after), (before, shared_before))
+        ]
+        return jnp.concatenate([source[48:64, :], *outer, source[0:16, :]], axis=0)
+
+    band = steps(banded(height_ref, 0), banded(conduct_ref, 1))
     out_ref[0:8, :] = band[32:40, 0:128]
     out_ref[8:56, :] = inner_ref[...]
     out_ref[56:64, :] = band[8:16, 0:128]
     columns = []
     for i in range(3):
-        rows = slice(COLUMN_ROW + 2 * i, COLUMN_ROW + 2 * i + 2)
-        columns.append(jnp.concatenate([column_ref[i], after(rows), jnp.zeros((4, 128), f32), before(rows)], axis=0))
+        rows = slice(2 * i, 2 * i + 2)
+        halo = [shared_after[2][rows], jnp.zeros((4, 128), f32), shared_before[2][rows]]
+        columns.append(jnp.concatenate([column_ref[i], *halo], axis=0))
     column_eta = [spread_columns(x, wide) for x in columns]
     column_sum, beside = column_sums(columns)
     column_sum_eta, beside_eta = column_sums([x * y for x, y in zip(columns, column_eta)])

time: 65.7 us -> 65.8 us (level)
  no operation moved by 1% of the time
where the time goes in v13:
time: 65.8 us; the launch traced here: 65.4 us
  blocking collectives  35.5 us (54%)
  starting transfers between devices  22 us (33%)
  Pallas kernels  5.81 us (9%)
  waiting for transfers between devices  1.22 us (2%)
  between operations  0.75 us (1%)
    all_to_all x1, blocking collectives, local(): sums = lax.all_to_all(sums.reshape(group, 1, 128), ('gx', 'gy'), 0, 0)  22.9 us
    ppermute x3, starting transfers between devices, swap(): lax.ppermute(even, axis, pairs(0))  14.1 us
    all_to_all x1, blocking collectives, local(): parts = lax.all_to_all(parts, 'gz', 0, 0)  12.7 us
    ppermute x3, starting transfers between devices, swap(): lax.ppermute(odd, axis, pairs(1))  7.98 us
    pallas_call x6, Pallas kernels, call(): pl.pallas_call(body, out_shape=[jax.ShapeDtypeStruct(s, f32) for s in out...  2.66 us
    pallas_call x1, Pallas kernels, local(): pl.pallas_call(own_block, out_shape=[jax.ShapeDtypeStruct(shape, f32) for...  1.46 us
  transfers between devices with their start and end apart: 6, of which 2 were waited for; matrix products, arithmetic and copies ran while one was open for 0% of the time, Pallas kernels for 4%

profile of v13, /device:TPU:1, one launch (start us, length us, event | category | flops | bytes accessed | tf_op | source)
XLA Modules:
  0.0 65.4 jit_solution(2332404078258765784)
XLA Ops:
  0.6 0.8 %shard_map.60 = (f32[4,2,8,128]{3,2,1,0:T(8,128)S(1)}, f32[4,2,8,128]{3,2,1,0:T(8,128)S(1)}) custom-call(f32[3,8,8,128]{3,2,1,0:T(8,128)} %force_ref.1, f32[8,8,128]{2,1,0:T(8,128)} %visc_ref.1), custom_call_target="tpu_custom_call" | custom-call | tf_op jit(solution)/shard_map/pallas_call | solution.py:516
  1.5 0.7 %collective-permute-start = (f32[4,2,8,128]{3,2,1,0:T(8,128)S(1)}, f32[4,2,8,128]{3,2,1,0:T(8,128)S(1)}, u32[]{:S(2)}, u32[]{:S(2)}) collective-permute-start(f32[4,2,8,128]{3,2,1,0:T(8,128)S(1)} %get-tuple-element.24), channel_id=1, source_target_pairs={{1,2},{2,1},{3,4},{4,3},{5,6},{6,5},{9,10},{10,9},{11,12},{12,11},... | collective-permute-start | bytes 98312 | tf_op jit(solution)/shard_map/ppermute | solution.py:509
  2.1 6.6 %collective-permute-start.1 = (f32[4,2,8,128]{3,2,1,0:T(8,128)S(1)}, f32[4,2,8,128]{3,2,1,0:T(8,128)S(1)}, u32[]{:S(2)}, u32[]{:S(2)}) collective-permute-start(f32[4,2,8,128]{3,2,1,0:T(8,128)S(1)} %get-tuple-element.25), channel_id=1, source_target_pairs={{0,1},{1,0},{2,3},{3,2},{4,5},{5,4},{6,7},{7,6},{8,9},{9,8},{10,11... | collective-permute-start | bytes 98312 | tf_op jit(solution)/shard_map/ppermute | solution.py:509
  8.7 1.5 %shard_map.59 = (f32[4,8,8,128]{3,2,1,0:T(8,128)S(1)}, f32[2,8,128]{2,1,0:T(8,128)S(1)}, f32[2,8,128]{2,1,0:T(8,128)S(1)}, f32[64,256]{1,0:T(8,128)S(1)}, f32[64,256]{1,0:T(8,128)S(1)}) custom-call(f32[3,8,8,128]{3,2,1,0:T(8,128)} %force_ref.1, f32[8,8,128]{2,1,0:T(8,128)} %visc_ref.1, f32[64,1024]{1,0:T(8,128)} %topo_hbm.1, bf16[64,1024]{1,0:T(8,128)(2,1)} %kappa_hbm.1), custom_call_target="tpu_custom_call" | custom-call | flops 20480000 | bytes 262144 | tf_op jit(solution)/shard_map/pallas_call | solution.py:525
  10.2 0.0 collective-permute-done.odd_ref
  10.2 0.0 collective-permute-done.1.even_ref
  10.2 0.1 shard_map.61
  10.3 0.7 %collective-permute-start.2 = (f32[2,8,128]{2,1,0:T(8,128)S(1)}, f32[2,8,128]{2,1,0:T(8,128)S(1)}, u32[]{:S(2)}, u32[]{:S(2)}) collective-permute-start(f32[2,8,128]{2,1,0:T(8,128)S(1)} %get-tuple-element.31.own_odd), channel_id=1, source_target_pairs={{8,16},{16,8},{24,32},{32,24},{40,48},{48,40},{56,64},{64,56},{72,... | collective-permute-start | bytes 24584 | tf_op jit(solution)/shard_map/ppermute | solution.py:509
  11.0 5.6 %collective-permute-start.3 = (f32[2,8,128]{2,1,0:T(8,128)S(1)}, f32[2,8,128]{2,1,0:T(8,128)S(1)}, u32[]{:S(2)}, u32[]{:S(2)}) collective-permute-start(f32[2,8,128]{2,1,0:T(8,128)S(1)} %get-tuple-element.32.own_even), channel_id=1, source_target_pairs={{0,8},{8,0},{16,24},{24,16},{32,40},{40,32},{48,56},{56,48},{64,72... | collective-permute-start | bytes 24584 | tf_op jit(solution)/shard_map/ppermute | solution.py:509
  16.6 0.1 shard_map.62
  16.6 0.0 collective-permute-done.2.odd_ref
  16.6 0.9 %collective-permute-done.3.even_ref = f32[2,8,128]{2,1,0:T(8,128)S(1)} collective-permute-done((f32[2,8,128]{2,1,0:T(8,128)S(1)}, f32[2,8,128]{2,1,0:T(8,128)S(1)}, u32[]{:S(2)}, u32[]{:S(2)}) %collective-permute-start.3) | collective-permute-done | bytes 8224 | tf_op jit(solution)/shard_map/ppermute | solution.py:509
  17.6 0.1 shard_map.63
  17.7 6.7 %collective-permute-start.4 = (f32[120,128]{1,0:T(8,128)S(1)}, f32[120,128]{1,0:T(8,128)S(1)}, u32[]{:S(2)}, u32[]{:S(2)}) collective-permute-start(f32[120,128]{1,0:T(8,128)S(1)} %get-tuple-element.36), channel_id=1, source_target_pairs={{128,256},{256,128},{129,257},{257,129},{130,258},{258,130},{131,2... | collective-permute-start | bytes 184328 | tf_op jit(solution)/shard_map/ppermute | solution.py:509
  24.4 1.9 %collective-permute-start.5 = (f32[120,128]{1,0:T(8,128)S(1)}, f32[120,128]{1,0:T(8,128)S(1)}, u32[]{:S(2)}, u32[]{:S(2)}) collective-permute-start(f32[120,128]{1,0:T(8,128)S(1)} %get-tuple-element.37), channel_id=1, source_target_pairs={{0,128},{128,0},{256,384},{384,256},{1,129},{129,1},{257,385},{385... | collective-permute-start | bytes 184328 | tf_op jit(solution)/shard_map/ppermute | solution.py:509
  26.3 0.9 %shard_map.64.inner_ref = f32[48,128]{1,0:T(8,128)S(1)} custom-call(f32[64,256]{1,0:T(8,128)S(1)} %get-tuple-element.38.height_ref, f32[64,256]{1,0:T(8,128)S(1)} %get-tuple-element.39.conduct_ref), custom_call_target="tpu_custom_call" | custom-call | flops 20480000 | bytes 262144 | tf_op jit(solution)/shard_map/pallas_call | solution.py:29
  27.3 0.0 collective-permute-done.4.odd_ref
  27.3 0.3 collective-permute-done.5.even_ref
  27.5 1.3 %shard_map.65 = (f32[3,8,8,128]{3,2,1,0:T(8,128)S(1)}, f32[64,128]{1,0:T(8,128)S(1)}, f32[2,8,128]{2,1,0:T(8,128)S(1)}, f32[64,128]{1,0:T(8,128)S(1)}) custom-call(f32[48,8,128]{2,1,0:T(8,128)S(1)} %get-tuple-element.28.planes_ref, f32[96,128]{1,0:T(8,128)S(1)} %get-tuple-element.29.low_ref, f32[96,128]{1,0:T(8,128)S(1)} %get-tuple-element.30.high_ref, ...), custom_call_target="tpu_custom_call" | custom-call | flops 20480000 | bytes 262144 | tf_op jit(solution)/shard_map/pallas_call | solution.py:29
  28.9 22.9 %all_to_all.10 = f32[64,1,128]{2,1,0:T(1,128)S(1)} all-to-all(f32[64,1,128]{2,1,0:T(1,128)S(1)} %bitcast.4), channel_id=1, replica_groups=mesh['gx'=4,'gy'=16,'gz'=8] {'gx','gy'}, dimensions={0} | all-to-all | bytes 65536 | tf_op jit(solution)/shard_map/all_to_all | solution.py:558
  51.7 0.1 shard_map.66
  51.8 12.7 %all_to_all.11.parts_ref = f32[8,4,128]{2,1,0:T(4,128)S(1)} all-to-all(f32[8,4,128]{2,1,0:T(4,128)S(1)} %shard_map.66), channel_id=1, replica_groups=mesh['gx'=4,'gy'=16,'gz'=8] {'gz'}, dimensions={0} | all-to-all | bytes 32768 | tf_op jit(solution)/shard_map/all_to_all | solution.py:560
  64.5 0.9 %shard_map.67 = (f32[3,8,8,128]{3,2,1,0:T(8,128)}, f32[64,128]{1,0:T(8,128)}) custom-call(f32[8,4,128]{2,1,0:T(4,128)S(1)} %all_to_all.11.parts_ref, f32[48,8,128]{2,1,0:T(8,128)S(1)} %get-tuple-element.28.planes_ref, f32[3,8,8,128]{3,2,1,0:T(8,128)S(1)} %get-tuple-element.42.image_ref, f32[64,128]{1,0:T(8,128)S(1)} %get-tuple-element.43.height_ref), custom_call_target="tpu_custom_call" | custom-call | tf_op jit(solution)/shard_map/pallas_call | solution.py:562
Async XLA Ops:
  1.5 8.7 %collective-permute-start = (f32[4,2,8,128]{3,2,1,0:T(8,128)S(1)}, f32[4,2,8,128]{3,2,1,0:T(8,128)S(1)}, u32[]{:S(2)}, u32[]{:S(2)}) collective-permute-start(f32[4,2,8,128]{3,2,1,0:T(8,128)S(1)} %get-tuple-element.24), channel_id=1, source_target_pairs={{1,2},{2,1},{3,4},{4,3},{5,6},{6,5},{9,10},{10,9},{11,12},{12,11},... | collective-permute-start | bytes 98312 | tf_op jit(solution)/shard_map/ppermute | solution.py:509
  2.1 8.1 %collective-permute-start.1 = (f32[4,2,8,128]{3,2,1,0:T(8,128)S(1)}, f32[4,2,8,128]{3,2,1,0:T(8,128)S(1)}, u32[]{:S(2)}, u32[]{:S(2)}) collective-permute-start(f32[4,2,8,128]{3,2,1,0:T(8,128)S(1)} %get-tuple-element.25), channel_id=1, source_target_pairs={{0,1},{1,0},{2,3},{3,2},{4,5},{5,4},{6,7},{7,6},{8,9},{9,8},{10,11... | collective-permute-start | bytes 98312 | tf_op jit(solution)/shard_map/ppermute | solution.py:509
  10.3 6.3 %collective-permute-start.2 = (f32[2,8,128]{2,1,0:T(8,128)S(1)}, f32[2,8,128]{2,1,0:T(8,128)S(1)}, u32[]{:S(2)}, u32[]{:S(2)}) collective-permute-start(f32[2,8,128]{2,1,0:T(8,128)S(1)} %get-tuple-element.31.own_odd), channel_id=1, source_target_pairs={{8,16},{16,8},{24,32},{32,24},{40,48},{48,40},{56,64},{64,56},{72,... | collective-permute-start | bytes 24584 | tf_op jit(solution)/shard_map/ppermute | solution.py:509
  11.0 6.6 %collective-permute-start.3 = (f32[2,8,128]{2,1,0:T(8,128)S(1)}, f32[2,8,128]{2,1,0:T(8,128)S(1)}, u32[]{:S(2)}, u32[]{:S(2)}) collective-permute-start(f32[2,8,128]{2,1,0:T(8,128)S(1)} %get-tuple-element.32.own_even), channel_id=1, source_target_pairs={{0,8},{8,0},{16,24},{24,16},{32,40},{40,32},{48,56},{56,48},{64,72... | collective-permute-start | bytes 24584 | tf_op jit(solution)/shard_map/ppermute | solution.py:509
  17.7 9.5 %collective-permute-start.4 = (f32[120,128]{1,0:T(8,128)S(1)}, f32[120,128]{1,0:T(8,128)S(1)}, u32[]{:S(2)}, u32[]{:S(2)}) collective-permute-start(f32[120,128]{1,0:T(8,128)S(1)} %get-tuple-element.36), channel_id=1, source_target_pairs={{128,256},{256,128},{129,257},{257,129},{130,258},{258,130},{131,2... | collective-permute-start | bytes 184328 | tf_op jit(solution)/shard_map/ppermute | solution.py:509
  24.4 3.1 %collective-permute-start.5 = (f32[120,128]{1,0:T(8,128)S(1)}, f32[120,128]{1,0:T(8,128)S(1)}, u32[]{:S(2)}, u32[]{:S(2)}) collective-permute-start(f32[120,128]{1,0:T(8,128)S(1)} %get-tuple-element.37), channel_id=1, source_target_pairs={{0,128},{128,0},{256,384},{384,256},{1,129},{129,1},{257,385},{385... | collective-permute-start | bytes 184328 | tf_op jit(solution)/shard_map/ppermute | solution.py:509

commit v14 on v12

--- a/solution.py
+++ b/solution.py
@@ -113,7 +113,7 @@
     return lax.rem(lax.axis_index(axis), 2) == 0
 
 
-def fetch(force_ref, visc_ref, odd_ref, even_ref, sems):
+def fetch(force_ref, visc_ref, even_ref, odd_ref, sems):
     depth = visc_ref.shape[0]
     start = jnp.where(is_even("gz"), 0, depth - 2)
     moves = []
@@ -134,7 +134,7 @@
     return left, jnp.where(mask, rolled(plane, first - 126), right)
 
 
-def assemble(own_ref, odd_ref, even_ref, left_ref, right_ref, planes_ref, odd_out, even_out):
+def assemble(own_ref, even_ref, odd_ref, left_ref, right_ref, planes_ref, odd_out, even_out):
     upward = is_even("gz")
     lane = lanes((8, 128))
     left, right = left_ref[0], right_ref[0]
@@ -482,7 +482,7 @@
     surface_copy.wait()
 
 
-def swap(odd, even, axis):
+def swap(odd, even, axis, even_first=False):
     count = lax.axis_size(axis)
 
     def pairs(start):
@@ -491,6 +491,9 @@
             found += [(i, i + 1), (i + 1, i)]
         return found
 
+    if even_first:
+        even = lax.ppermute(even, axis, pairs(0))
+        return lax.ppermute(odd, axis, pairs(1)), even
     return lax.ppermute(odd, axis, pairs(1)), lax.ppermute(even, axis, pairs(0))
 
 
@@ -498,7 +501,7 @@
     inputs = [
         pltpu.with_memory_space_constraint(x, pltpu.HBM) for x in (body_force, viscosity, topography, kappa)
     ]
-    odd, even = pl.pallas_call(
+    even, odd = pl.pallas_call(
         fetch,
         out_shape=[jax.ShapeDtypeStruct((4, 2, 8, 128), f32)] * 2,
         in_specs=[pl.BlockSpec(memory_space=pltpu.HBM)] * 2,
@@ -506,7 +509,7 @@
         scratch_shapes=[pltpu.SemaphoreType.DMA((4,))],
         compiler_params=pltpu.CompilerParams(vmem_limit_bytes=1 << 20),
     )(*inputs[:2])
-    odd, even = swap(odd, even, "gz")
+    odd, even = swap(odd, even, "gz", even_first=True)
     planes, left, right, height, conduct = pl.pallas_call(
         own_block,
         out_shape=[
@@ -522,7 +525,7 @@
     planes, odd, even = call(
         assemble,
         [(PLANES, 8, 128), (2, 8, 128), (2, 8, 128)],
-        (planes, odd, even, left, right),
+        (planes, even, odd, left, right),
     )
     own = (odd, even)
     odd, even = swap(odd, even, "gy")

time: 65.7 us -> 67 us (1.020)
  blocking collectives: 35.5 us -> 39.9 us
  starting transfers between devices: 22 us -> 19 us
    ppermute x3 -> x2, starting transfers between devices: 14.1 us -> 7.5 us  [swap(): lax.ppermute(even, axis, pairs(0))]
    ppermute x0 -> x2, starting transfers between devices: none -> 4.69 us  [the longest x1 4.02 us: swap(): even = lax.ppermute(even, axis, pairs(0))]
    all_to_all x1, blocking collectives: 12.7 us -> 17 us  [local(): parts = lax.all_to_all(parts, 'gz', 0, 0)]
    ppermute x3 -> x2, starting transfers between devices: 7.98 us -> 6.81 us  [swap(): lax.ppermute(odd, axis, pairs(1))]
where the time goes in v14:
time: 67 us; the launch traced here: 66.6 us
  blocking collectives  39.9 us (60%)
  starting transfers between devices  19 us (28%)
  Pallas kernels  5.76 us (9%)
  waiting for transfers between devices  1.23 us (2%)
  between operations  0.76 us (1%)
    all_to_all x1, blocking collectives, local(): sums = lax.all_to_all(sums.reshape(group, 1, 128), ('gx', 'gy'), 0, 0)  22.9 us
    all_to_all x1, blocking collectives, local(): parts = lax.all_to_all(parts, 'gz', 0, 0)  17 us
    ppermute x2, starting transfers between devices, swap(): lax.ppermute(even, axis, pairs(0))  7.5 us
    ppermute x2, starting transfers between devices, swap(): lax.ppermute(odd, axis, pairs(1))  6.81 us
    ppermute x1, starting transfers between devices, swap(): even = lax.ppermute(even, axis, pairs(0))  4.02 us
    pallas_call x6, Pallas kernels, call(): pl.pallas_call(body, out_shape=[jax.ShapeDtypeStruct(s, f32) for s in out...  2.6 us
    pallas_call x1, Pallas kernels, local(): pl.pallas_call(own_block, out_shape=[jax.ShapeDtypeStruct(shape, f32) for...  1.46 us
  transfers between devices with their start and end apart: 6, of which 2 were waited for; matrix products, arithmetic and copies ran while one was open for 0% of the time, Pallas kernels for 4%

profile of v14, /device:TPU:1, one launch (start us, length us, event | category | flops | bytes accessed | tf_op | source)
XLA Modules:
  0.0 66.6 jit_solution(12189517946574894152)
XLA Ops:
  0.6 0.8 %shard_map.60 = (f32[4,2,8,128]{3,2,1,0:T(8,128)S(1)}, f32[4,2,8,128]{3,2,1,0:T(8,128)S(1)}) custom-call(f32[3,8,8,128]{3,2,1,0:T(8,128)} %force_ref.1, f32[8,8,128]{2,1,0:T(8,128)} %visc_ref.1), custom_call_target="tpu_custom_call" | custom-call | tf_op jit(solution)/shard_map/pallas_call | solution.py:504
  1.5 4.0 %collective-permute-start = (f32[4,2,8,128]{3,2,1,0:T(8,128)S(1)}, f32[4,2,8,128]{3,2,1,0:T(8,128)S(1)}, u32[]{:S(2)}, u32[]{:S(2)}) collective-permute-start(f32[4,2,8,128]{3,2,1,0:T(8,128)S(1)} %get-tuple-element.24), channel_id=1, source_target_pairs={{0,1},{1,0},{2,3},{3,2},{4,5},{5,4},{6,7},{7,6},{8,9},{9,8},{10,11... | collective-permute-start | bytes 98312 | tf_op jit(solution)/shard_map/ppermute | solution.py:495
  5.5 0.7 collective-permute-start.1
  6.2 1.5 %shard_map.59 = (f32[4,8,8,128]{3,2,1,0:T(8,128)S(1)}, f32[2,8,128]{2,1,0:T(8,128)S(1)}, f32[2,8,128]{2,1,0:T(8,128)S(1)}, f32[64,256]{1,0:T(8,128)S(1)}, f32[64,256]{1,0:T(8,128)S(1)}) custom-call(f32[3,8,8,128]{3,2,1,0:T(8,128)} %force_ref.1, f32[8,8,128]{2,1,0:T(8,128)} %visc_ref.1, f32[64,1024]{1,0:T(8,128)} %topo_hbm.1, bf16[64,1024]{1,0:T(8,128)(2,1)} %kappa_hbm.1), custom_call_target="tpu_custom_call" | custom-call | flops 20480000 | bytes 262144 | tf_op jit(solution)/shard_map/pallas_call | solution.py:513
  7.6 0.0 collective-permute-done.even_ref
  7.6 0.0 collective-permute-done.1.odd_ref
  7.7 0.1 shard_map.61
  7.8 0.7 collective-permute-start.2
  8.4 5.6 %collective-permute-start.3 = (f32[2,8,128]{2,1,0:T(8,128)S(1)}, f32[2,8,128]{2,1,0:T(8,128)S(1)}, u32[]{:S(2)}, u32[]{:S(2)}) collective-permute-start(f32[2,8,128]{2,1,0:T(8,128)S(1)} %get-tuple-element.32.own_even), channel_id=1, source_target_pairs={{0,8},{8,0},{16,24},{24,16},{32,40},{40,32},{48,56},{56,48},{64,72... | collective-permute-start | bytes 24584 | tf_op jit(solution)/shard_map/ppermute | solution.py:497
  14.0 0.1 shard_map.62
  14.1 0.0 collective-permute-done.2.odd_ref
  14.1 0.9 %collective-permute-done.3.even_ref = f32[2,8,128]{2,1,0:T(8,128)S(1)} collective-permute-done((f32[2,8,128]{2,1,0:T(8,128)S(1)}, f32[2,8,128]{2,1,0:T(8,128)S(1)}, u32[]{:S(2)}, u32[]{:S(2)}) %collective-permute-start.3) | collective-permute-done | bytes 8224 | tf_op jit(solution)/shard_map/ppermute | solution.py:497
  15.0 0.1 shard_map.63
  15.2 6.1 %collective-permute-start.4 = (f32[136,128]{1,0:T(8,128)S(1)}, f32[136,128]{1,0:T(8,128)S(1)}, u32[]{:S(2)}, u32[]{:S(2)}) collective-permute-start(f32[136,128]{1,0:T(8,128)S(1)} %get-tuple-element.36), channel_id=1, source_target_pairs={{128,256},{256,128},{129,257},{257,129},{130,258},{258,130},{131,2... | collective-permute-start | bytes 208904 | tf_op jit(solution)/shard_map/ppermute | solution.py:497
  21.3 1.9 %collective-permute-start.5 = (f32[136,128]{1,0:T(8,128)S(1)}, f32[136,128]{1,0:T(8,128)S(1)}, u32[]{:S(2)}, u32[]{:S(2)}) collective-permute-start(f32[136,128]{1,0:T(8,128)S(1)} %get-tuple-element.37), channel_id=1, source_target_pairs={{0,128},{128,0},{256,384},{384,256},{1,129},{129,1},{257,385},{385... | collective-permute-start | bytes 208904 | tf_op jit(solution)/shard_map/ppermute | solution.py:497
  23.2 0.9 %shard_map.64.inner_ref = f32[48,128]{1,0:T(8,128)S(1)} custom-call(f32[64,256]{1,0:T(8,128)S(1)} %get-tuple-element.38.height_ref, f32[64,256]{1,0:T(8,128)S(1)} %get-tuple-element.39.conduct_ref), custom_call_target="tpu_custom_call" | custom-call | flops 20480000 | bytes 262144 | tf_op jit(solution)/shard_map/pallas_call | solution.py:29
  24.2 0.0 collective-permute-done.4.odd_ref
  24.2 0.3 collective-permute-done.5.even_ref
  24.5 1.3 %shard_map.65 = (f32[3,8,8,128]{3,2,1,0:T(8,128)S(1)}, f32[64,128]{1,0:T(8,128)S(1)}, f32[2,8,128]{2,1,0:T(8,128)S(1)}, f32[64,128]{1,0:T(8,128)S(1)}) custom-call(f32[48,8,128]{2,1,0:T(8,128)S(1)} %get-tuple-element.28.planes_ref, f32[96,128]{1,0:T(8,128)S(1)} %get-tuple-element.29.low_ref, f32[96,128]{1,0:T(8,128)S(1)} %get-tuple-element.30.high_ref, ...), custom_call_target="tpu_custom_call" | custom-call | flops 20480000 | bytes 262144 | tf_op jit(solution)/shard_map/pallas_call | solution.py:29
  25.8 22.9 %all_to_all.10 = f32[64,1,128]{2,1,0:T(1,128)S(1)} all-to-all(f32[64,1,128]{2,1,0:T(1,128)S(1)} %bitcast.4), channel_id=1, replica_groups=mesh['gx'=4,'gy'=16,'gz'=8] {'gx','gy'}, dimensions={0} | all-to-all | bytes 65536 | tf_op jit(solution)/shard_map/all_to_all | solution.py:546
  48.6 0.1 shard_map.66
  48.7 17.0 %all_to_all.11.parts_ref = f32[8,4,128]{2,1,0:T(4,128)S(1)} all-to-all(f32[8,4,128]{2,1,0:T(4,128)S(1)} %shard_map.66), channel_id=1, replica_groups=mesh['gx'=4,'gy'=16,'gz'=8] {'gz'}, dimensions={0} | all-to-all | bytes 32768 | tf_op jit(solution)/shard_map/all_to_all | solution.py:548
  65.8 0.9 %shard_map.67 = (f32[3,8,8,128]{3,2,1,0:T(8,128)}, f32[64,128]{1,0:T(8,128)}) custom-call(f32[8,4,128]{2,1,0:T(4,128)S(1)} %all_to_all.11.parts_ref, f32[48,8,128]{2,1,0:T(8,128)S(1)} %get-tuple-element.28.planes_ref, f32[3,8,8,128]{3,2,1,0:T(8,128)S(1)} %get-tuple-element.42.image_ref, f32[64,128]{1,0:T(8,128)S(1)} %get-tuple-element.43.height_ref), custom_call_target="tpu_custom_call" | custom-call | tf_op jit(solution)/shard_map/pallas_call | solution.py:550
Async XLA Ops:
  1.5 6.2 %collective-permute-start = (f32[4,2,8,128]{3,2,1,0:T(8,128)S(1)}, f32[4,2,8,128]{3,2,1,0:T(8,128)S(1)}, u32[]{:S(2)}, u32[]{:S(2)}) collective-permute-start(f32[4,2,8,128]{3,2,1,0:T(8,128)S(1)} %get-tuple-element.24), channel_id=1, source_target_pairs={{0,1},{1,0},{2,3},{3,2},{4,5},{5,4},{6,7},{7,6},{8,9},{9,8},{10,11... | collective-permute-start | bytes 98312 | tf_op jit(solution)/shard_map/ppermute | solution.py:495
  5.5 2.2 %collective-permute-start.1 = (f32[4,2,8,128]{3,2,1,0:T(8,128)S(1)}, f32[4,2,8,128]{3,2,1,0:T(8,128)S(1)}, u32[]{:S(2)}, u32[]{:S(2)}) collective-permute-start(f32[4,2,8,128]{3,2,1,0:T(8,128)S(1)} %get-tuple-element.25), channel_id=1, source_target_pairs={{1,2},{2,1},{3,4},{4,3},{5,6},{6,5},{9,10},{10,9},{11,12},{12,11},... | collective-permute-start | bytes 98312 | tf_op jit(solution)/shard_map/ppermute | solution.py:496
  7.8 6.3 %collective-permute-start.2 = (f32[2,8,128]{2,1,0:T(8,128)S(1)}, f32[2,8,128]{2,1,0:T(8,128)S(1)}, u32[]{:S(2)}, u32[]{:S(2)}) collective-permute-start(f32[2,8,128]{2,1,0:T(8,128)S(1)} %get-tuple-element.31.own_odd), channel_id=1, source_target_pairs={{8,16},{16,8},{24,32},{32,24},{40,48},{48,40},{56,64},{64,56},{72,... | collective-permute-start | bytes 24584 | tf_op jit(solution)/shard_map/ppermute | solution.py:497
  8.4 6.6 %collective-permute-start.3 = (f32[2,8,128]{2,1,0:T(8,128)S(1)}, f32[2,8,128]{2,1,0:T(8,128)S(1)}, u32[]{:S(2)}, u32[]{:S(2)}) collective-permute-start(f32[2,8,128]{2,1,0:T(8,128)S(1)} %get-tuple-element.32.own_even), channel_id=1, source_target_pairs={{0,8},{8,0},{16,24},{24,16},{32,40},{40,32},{48,56},{56,48},{64,72... | collective-permute-start | bytes 24584 | tf_op jit(solution)/shard_map/ppermute | solution.py:497
  15.2 9.0 %collective-permute-start.4 = (f32[136,128]{1,0:T(8,128)S(1)}, f32[136,128]{1,0:T(8,128)S(1)}, u32[]{:S(2)}, u32[]{:S(2)}) collective-permute-start(f32[136,128]{1,0:T(8,128)S(1)} %get-tuple-element.36), channel_id=1, source_target_pairs={{128,256},{256,128},{129,257},{257,129},{130,258},{258,130},{131,2... | collective-permute-start | bytes 208904 | tf_op jit(solution)/shard_map/ppermute | solution.py:497
  21.3 3.2 %collective-permute-start.5 = (f32[136,128]{1,0:T(8,128)S(1)}, f32[136,128]{1,0:T(8,128)S(1)}, u32[]{:S(2)}, u32[]{:S(2)}) collective-permute-start(f32[136,128]{1,0:T(8,128)S(1)} %get-tuple-element.37), channel_id=1, source_target_pairs={{0,128},{128,0},{256,384},{384,256},{1,129},{129,1},{257,385},{385... | collective-permute-start | bytes 208904 | tf_op jit(solution)/shard_map/ppermute | solution.py:497

commit v15 on v12

--- a/solution.py
+++ b/solution.py
@@ -134,7 +134,7 @@
     return left, jnp.where(mask, rolled(plane, first - 126), right)
 
 
-def assemble(own_ref, odd_ref, even_ref, left_ref, right_ref, planes_ref, odd_out, even_out):
+def assemble(own_ref, odd_ref, even_ref, left_ref, right_ref, planes_ref, even_out, odd_out):
     upward = is_even("gz")
     lane = lanes((8, 128))
     left, right = left_ref[0], right_ref[0]
@@ -170,7 +170,7 @@
 
 
 def prepare_rows(
-    low_ref, high_ref, own_odd, own_even, odd_ref, even_ref, height_ref, conduct_ref,
+    low_ref, high_ref, own_odd, own_even, even_ref, odd_ref, height_ref, conduct_ref,
     odd_out, even_out, column_ref, height_out, conduct_out,
 ):
     g = lax.axis_index("gz")
@@ -482,7 +482,7 @@
     surface_copy.wait()
 
 
-def swap(odd, even, axis):
+def swap(odd, even, axis, even_first=False):
     count = lax.axis_size(axis)
 
     def pairs(start):
@@ -491,6 +491,9 @@
             found += [(i, i + 1), (i + 1, i)]
         return found
 
+    if even_first:
+        even = lax.ppermute(even, axis, pairs(0))
+        return lax.ppermute(odd, axis, pairs(1)), even
     return lax.ppermute(odd, axis, pairs(1)), lax.ppermute(even, axis, pairs(0))
 
 
@@ -519,18 +522,18 @@
         compiler_params=pltpu.CompilerParams(vmem_limit_bytes=8 << 20),
         cost_estimate=pl.CostEstimate(flops=20000 * 1024, bytes_accessed=1 << 18, transcendentals=0),
     )(*inputs)
-    planes, odd, even = call(
+    planes, even, odd = call(
         assemble,
         [(PLANES, 8, 128), (2, 8, 128), (2, 8, 128)],
         (planes, odd, even, left, right),
     )
     own = (odd, even)
-    odd, even = swap(odd, even, "gy")
+    odd, even = swap(odd, even, "gy", even_first=True)
     low, high = call(edge_rows, [(COLUMN_ROW, 128)] * 2, (planes,))
     odd, even, columns, height, conduct = call(
         prepare_rows,
         [(GX_ROWS, 128), (GX_ROWS, 128), (3, 8, 128), (64, 256), (64, 256)],
-        (low, high, *own, odd, even, height, conduct),
+        (low, high, *own, even, odd, height, conduct),
     )
     odd, even = swap(odd, even, "gx")
     (inner,) = call(inner_rows, [(48, 128)], (height, conduct))

time: 65.7 us -> 65.7 us (level)
    ppermute x0 -> x2, starting transfers between devices: none -> 6.24 us  [the longest x1 5.58 us: swap(): even = lax.ppermute(even, axis, pairs(0))]
    ppermute x3 -> x2, starting transfers between devices: 14.1 us -> 8.48 us  [swap(): lax.ppermute(even, axis, pairs(0))]
    ppermute x0 -> x2, waiting for transfers between devices: none -> 0.94 us  [the longest x1 0.94 us: swap(): even = lax.ppermute(even, axis, pairs(0))]
    ppermute x3 -> x2, waiting for transfers between devices: 1.22 us -> 0.29 us  [swap(): lax.ppermute(even, axis, pairs(0))]
    ppermute x3 -> x2, starting transfers between devices: 7.98 us -> 7.32 us  [swap(): lax.ppermute(odd, axis, pairs(1))]
where the time goes in v15:
time: 65.7 us; the launch traced here: 65.3 us
  blocking collectives  35.5 us (54%)
  starting transfers between devices  22 us (33%)
  Pallas kernels  5.76 us (9%)
  waiting for transfers between devices  1.23 us (2%)
  between operations  0.76 us (1%)
    all_to_all x1, blocking collectives, local(): sums = lax.all_to_all(sums.reshape(group, 1, 128), ('gx', 'gy'), 0, 0)  22.9 us
    all_to_all x1, blocking collectives, local(): parts = lax.all_to_all(parts, 'gz', 0, 0)  12.7 us
    ppermute x2, starting transfers between devices, swap(): lax.ppermute(even, axis, pairs(0))  8.48 us
    ppermute x2, starting transfers between devices, swap(): lax.ppermute(odd, axis, pairs(1))  7.32 us
    ppermute x1, starting transfers between devices, swap(): even = lax.ppermute(even, axis, pairs(0))  5.58 us
    pallas_call x6, Pallas kernels, call(): pl.pallas_call(body, out_shape=[jax.ShapeDtypeStruct(s, f32) for s in out...  2.6 us
    pallas_call x1, Pallas kernels, local(): pl.pallas_call(own_block, out_shape=[jax.ShapeDtypeStruct(shape, f32) for...  1.46 us
  transfers between devices with their start and end apart: 6, of which 2 were waited for; matrix products, arithmetic and copies ran while one was open for 0% of the time, Pallas kernels for 4%

profile of v15, /device:TPU:1, one launch (start us, length us, event | category | flops | bytes accessed | tf_op | source)
XLA Modules:
  0.0 65.3 jit_solution(1688276599543535927)
XLA Ops:
  0.6 0.8 %shard_map.60 = (f32[4,2,8,128]{3,2,1,0:T(8,128)S(1)}, f32[4,2,8,128]{3,2,1,0:T(8,128)S(1)}) custom-call(f32[3,8,8,128]{3,2,1,0:T(8,128)} %force_ref.1, f32[8,8,128]{2,1,0:T(8,128)} %visc_ref.1), custom_call_target="tpu_custom_call" | custom-call | tf_op jit(solution)/shard_map/pallas_call | solution.py:504
  1.5 0.7 %collective-permute-start = (f32[4,2,8,128]{3,2,1,0:T(8,128)S(1)}, f32[4,2,8,128]{3,2,1,0:T(8,128)S(1)}, u32[]{:S(2)}, u32[]{:S(2)}) collective-permute-start(f32[4,2,8,128]{3,2,1,0:T(8,128)S(1)} %get-tuple-element.24), channel_id=1, source_target_pairs={{1,2},{2,1},{3,4},{4,3},{5,6},{6,5},{9,10},{10,9},{11,12},{12,11},... | collective-permute-start | bytes 98312 | tf_op jit(solution)/shard_map/ppermute | solution.py:497
  2.1 6.6 %collective-permute-start.1 = (f32[4,2,8,128]{3,2,1,0:T(8,128)S(1)}, f32[4,2,8,128]{3,2,1,0:T(8,128)S(1)}, u32[]{:S(2)}, u32[]{:S(2)}) collective-permute-start(f32[4,2,8,128]{3,2,1,0:T(8,128)S(1)} %get-tuple-element.25), channel_id=1, source_target_pairs={{0,1},{1,0},{2,3},{3,2},{4,5},{5,4},{6,7},{7,6},{8,9},{9,8},{10,11... | collective-permute-start | bytes 98312 | tf_op jit(solution)/shard_map/ppermute | solution.py:497
  8.7 1.5 %shard_map.59 = (f32[4,8,8,128]{3,2,1,0:T(8,128)S(1)}, f32[2,8,128]{2,1,0:T(8,128)S(1)}, f32[2,8,128]{2,1,0:T(8,128)S(1)}, f32[64,256]{1,0:T(8,128)S(1)}, f32[64,256]{1,0:T(8,128)S(1)}) custom-call(f32[3,8,8,128]{3,2,1,0:T(8,128)} %force_ref.1, f32[8,8,128]{2,1,0:T(8,128)} %visc_ref.1, f32[64,1024]{1,0:T(8,128)} %topo_hbm.1, bf16[64,1024]{1,0:T(8,128)(2,1)} %kappa_hbm.1), custom_call_target="tpu_custom_call" | custom-call | flops 20480000 | bytes 262144 | tf_op jit(solution)/shard_map/pallas_call | solution.py:513
  10.2 0.0 collective-permute-done.odd_ref
  10.2 0.0 collective-permute-done.1.even_ref
  10.2 0.1 shard_map.61
  10.3 0.7 %collective-permute-start.3 = (f32[2,8,128]{2,1,0:T(8,128)S(1)}, f32[2,8,128]{2,1,0:T(8,128)S(1)}, u32[]{:S(2)}, u32[]{:S(2)}) collective-permute-start(f32[2,8,128]{2,1,0:T(8,128)S(1)} %get-tuple-element.31.own_odd), channel_id=1, source_target_pairs={{8,16},{16,8},{24,32},{32,24},{40,48},{48,40},{56,64},{64,56},{72,... | collective-permute-start | bytes 24584 | tf_op jit(solution)/shard_map/ppermute | solution.py:496
  11.0 5.6 %collective-permute-start.2 = (f32[2,8,128]{2,1,0:T(8,128)S(1)}, f32[2,8,128]{2,1,0:T(8,128)S(1)}, u32[]{:S(2)}, u32[]{:S(2)}) collective-permute-start(f32[2,8,128]{2,1,0:T(8,128)S(1)} %get-tuple-element.32.own_even), channel_id=1, source_target_pairs={{0,8},{8,0},{16,24},{24,16},{32,40},{40,32},{48,56},{56,48},{64,72... | collective-permute-start | bytes 24584 | tf_op jit(solution)/shard_map/ppermute | solution.py:495
  16.6 0.1 shard_map.62
  16.6 0.0 collective-permute-done.3.odd_ref
  16.6 0.9 %collective-permute-done.2.even_ref = f32[2,8,128]{2,1,0:T(8,128)S(1)} collective-permute-done((f32[2,8,128]{2,1,0:T(8,128)S(1)}, f32[2,8,128]{2,1,0:T(8,128)S(1)}, u32[]{:S(2)}, u32[]{:S(2)}) %collective-permute-start.2) | collective-permute-done | bytes 8224 | tf_op jit(solution)/shard_map/ppermute | solution.py:495
  17.6 0.1 shard_map.63
  17.7 6.7 %collective-permute-start.4 = (f32[136,128]{1,0:T(8,128)S(1)}, f32[136,128]{1,0:T(8,128)S(1)}, u32[]{:S(2)}, u32[]{:S(2)}) collective-permute-start(f32[136,128]{1,0:T(8,128)S(1)} %get-tuple-element.36), channel_id=1, source_target_pairs={{128,256},{256,128},{129,257},{257,129},{130,258},{258,130},{131,2... | collective-permute-start | bytes 208904 | tf_op jit(solution)/shard_map/ppermute | solution.py:497
  24.4 1.9 %collective-permute-start.5 = (f32[136,128]{1,0:T(8,128)S(1)}, f32[136,128]{1,0:T(8,128)S(1)}, u32[]{:S(2)}, u32[]{:S(2)}) collective-permute-start(f32[136,128]{1,0:T(8,128)S(1)} %get-tuple-element.37), channel_id=1, source_target_pairs={{0,128},{128,0},{256,384},{384,256},{1,129},{129,1},{257,385},{385... | collective-permute-start | bytes 208904 | tf_op jit(solution)/shard_map/ppermute | solution.py:497
  26.3 0.9 %shard_map.64.inner_ref = f32[48,128]{1,0:T(8,128)S(1)} custom-call(f32[64,256]{1,0:T(8,128)S(1)} %get-tuple-element.38.height_ref, f32[64,256]{1,0:T(8,128)S(1)} %get-tuple-element.39.conduct_ref), custom_call_target="tpu_custom_call" | custom-call | flops 20480000 | bytes 262144 | tf_op jit(solution)/shard_map/pallas_call | solution.py:29
  27.2 0.0 collective-permute-done.4.odd_ref
  27.2 0.3 collective-permute-done.5.even_ref
  27.5 1.3 %shard_map.65 = (f32[3,8,8,128]{3,2,1,0:T(8,128)S(1)}, f32[64,128]{1,0:T(8,128)S(1)}, f32[2,8,128]{2,1,0:T(8,128)S(1)}, f32[64,128]{1,0:T(8,128)S(1)}) custom-call(f32[48,8,128]{2,1,0:T(8,128)S(1)} %get-tuple-element.28.planes_ref, f32[96,128]{1,0:T(8,128)S(1)} %get-tuple-element.29.low_ref, f32[96,128]{1,0:T(8,128)S(1)} %get-tuple-element.30.high_ref, ...), custom_call_target="tpu_custom_call" | custom-call | flops 20480000 | bytes 262144 | tf_op jit(solution)/shard_map/pallas_call | solution.py:29
  28.8 22.9 %all_to_all.10 = f32[64,1,128]{2,1,0:T(1,128)S(1)} all-to-all(f32[64,1,128]{2,1,0:T(1,128)S(1)} %bitcast.4), channel_id=1, replica_groups=mesh['gx'=4,'gy'=16,'gz'=8] {'gx','gy'}, dimensions={0} | all-to-all | bytes 65536 | tf_op jit(solution)/shard_map/all_to_all | solution.py:546
  51.7 0.1 shard_map.66
  51.8 12.7 %all_to_all.11.parts_ref = f32[8,4,128]{2,1,0:T(4,128)S(1)} all-to-all(f32[8,4,128]{2,1,0:T(4,128)S(1)} %shard_map.66), channel_id=1, replica_groups=mesh['gx'=4,'gy'=16,'gz'=8] {'gz'}, dimensions={0} | all-to-all | bytes 32768 | tf_op jit(solution)/shard_map/all_to_all | solution.py:548
  64.4 0.9 %shard_map.67 = (f32[3,8,8,128]{3,2,1,0:T(8,128)}, f32[64,128]{1,0:T(8,128)}) custom-call(f32[8,4,128]{2,1,0:T(4,128)S(1)} %all_to_all.11.parts_ref, f32[48,8,128]{2,1,0:T(8,128)S(1)} %get-tuple-element.28.planes_ref, f32[3,8,8,128]{3,2,1,0:T(8,128)S(1)} %get-tuple-element.42.image_ref, f32[64,128]{1,0:T(8,128)S(1)} %get-tuple-element.43.height_ref), custom_call_target="tpu_custom_call" | custom-call | tf_op jit(solution)/shard_map/pallas_call | solution.py:550
Async XLA Ops:
  1.5 8.7 %collective-permute-start = (f32[4,2,8,128]{3,2,1,0:T(8,128)S(1)}, f32[4,2,8,128]{3,2,1,0:T(8,128)S(1)}, u32[]{:S(2)}, u32[]{:S(2)}) collective-permute-start(f32[4,2,8,128]{3,2,1,0:T(8,128)S(1)} %get-tuple-element.24), channel_id=1, source_target_pairs={{1,2},{2,1},{3,4},{4,3},{5,6},{6,5},{9,10},{10,9},{11,12},{12,11},... | collective-permute-start | bytes 98312 | tf_op jit(solution)/shard_map/ppermute | solution.py:497
  2.1 8.1 %collective-permute-start.1 = (f32[4,2,8,128]{3,2,1,0:T(8,128)S(1)}, f32[4,2,8,128]{3,2,1,0:T(8,128)S(1)}, u32[]{:S(2)}, u32[]{:S(2)}) collective-permute-start(f32[4,2,8,128]{3,2,1,0:T(8,128)S(1)} %get-tuple-element.25), channel_id=1, source_target_pairs={{0,1},{1,0},{2,3},{3,2},{4,5},{5,4},{6,7},{7,6},{8,9},{9,8},{10,11... | collective-permute-start | bytes 98312 | tf_op jit(solution)/shard_map/ppermute | solution.py:497
  10.3 6.3 %collective-permute-start.3 = (f32[2,8,128]{2,1,0:T(8,128)S(1)}, f32[2,8,128]{2,1,0:T(8,128)S(1)}, u32[]{:S(2)}, u32[]{:S(2)}) collective-permute-start(f32[2,8,128]{2,1,0:T(8,128)S(1)} %get-tuple-element.31.own_odd), channel_id=1, source_target_pairs={{8,16},{16,8},{24,32},{32,24},{40,48},{48,40},{56,64},{64,56},{72,... | collective-permute-start | bytes 24584 | tf_op jit(solution)/shard_map/ppermute | solution.py:496
  11.0 6.6 %collective-permute-start.2 = (f32[2,8,128]{2,1,0:T(8,128)S(1)}, f32[2,8,128]{2,1,0:T(8,128)S(1)}, u32[]{:S(2)}, u32[]{:S(2)}) collective-permute-start(f32[2,8,128]{2,1,0:T(8,128)S(1)} %get-tuple-element.32.own_even), channel_id=1, source_target_pairs={{0,8},{8,0},{16,24},{24,16},{32,40},{40,32},{48,56},{56,48},{64,72... | collective-permute-start | bytes 24584 | tf_op jit(solution)/shard_map/ppermute | solution.py:495
  17.7 9.5 %collective-permute-start.4 = (f32[136,128]{1,0:T(8,128)S(1)}, f32[136,128]{1,0:T(8,128)S(1)}, u32[]{:S(2)}, u32[]{:S(2)}) collective-permute-start(f32[136,128]{1,0:T(8,128)S(1)} %get-tuple-element.36), channel_id=1, source_target_pairs={{128,256},{256,128},{129,257},{257,129},{130,258},{258,130},{131,2... | collective-permute-start | bytes 208904 | tf_op jit(solution)/shard_map/ppermute | solution.py:497
  24.4 3.2 %collective-permute-start.5 = (f32[136,128]{1,0:T(8,128)S(1)}, f32[136,128]{1,0:T(8,128)S(1)}, u32[]{:S(2)}, u32[]{:S(2)}) collective-permute-start(f32[136,128]{1,0:T(8,128)S(1)} %get-tuple-element.37), channel_id=1, source_target_pairs={{0,128},{128,0},{256,384},{384,256},{1,129},{129,1},{257,385},{385... | collective-permute-start | bytes 208904 | tf_op jit(solution)/shard_map/ppermute | solution.py:497

commit v16 on v15

--- a/solution.py
+++ b/solution.py
@@ -170,7 +170,7 @@
 
 
 def prepare_rows(
-    low_ref, high_ref, own_odd, own_even, even_ref, odd_ref, height_ref, conduct_ref,
+    low_ref, high_ref, own_even, own_odd, even_ref, odd_ref, height_ref, conduct_ref,
     odd_out, even_out, column_ref, height_out, conduct_out,
 ):
     g = lax.axis_index("gz")
@@ -527,7 +527,7 @@
         [(PLANES, 8, 128), (2, 8, 128), (2, 8, 128)],
         (planes, odd, even, left, right),
     )
-    own = (odd, even)
+    own = (even, odd)
     odd, even = swap(odd, even, "gy", even_first=True)
     low, high = call(edge_rows, [(COLUMN_ROW, 128)] * 2, (planes,))
     odd, even, columns, height, conduct = call(

time: 65.7 us -> 67.2 us (1.023)
  blocking collectives: 35.5 us -> 39.9 us
  starting transfers between devices: 22 us -> 19.6 us
    all_to_all x1, blocking collectives: 22.9 us -> 27.3 us  [local(): sums = lax.all_to_all(sums.reshape(group, 1, 128), ('gx', 'gy'), 0, 0)]
    ppermute x1, starting transfers between devices: 5.58 us -> 3.12 us  [swap(): even = lax.ppermute(even, axis, pairs(0))]
where the time goes in v16:
time: 67.2 us; the launch traced here: 66.8 us
  blocking collectives  39.9 us (59%)
  starting transfers between devices  19.6 us (29%)
  Pallas kernels  5.76 us (9%)
  waiting for transfers between devices  0.81 us (1%)
  between operations  0.75 us (1%)
    all_to_all x1, blocking collectives, local(): sums = lax.all_to_all(sums.reshape(group, 1, 128), ('gx', 'gy'), 0, 0)  27.3 us
    all_to_all x1, blocking collectives, local(): parts = lax.all_to_all(parts, 'gz', 0, 0)  12.7 us
    ppermute x2, starting transfers between devices, swap(): lax.ppermute(even, axis, pairs(0))  8.48 us
    ppermute x2, starting transfers between devices, swap(): lax.ppermute(odd, axis, pairs(1))  7.32 us
    ppermute x1, starting transfers between devices, swap(): even = lax.ppermute(even, axis, pairs(0))  3.12 us
    pallas_call x6, Pallas kernels, call(): pl.pallas_call(body, out_shape=[jax.ShapeDtypeStruct(s, f32) for s in out...  2.6 us
    pallas_call x1, Pallas kernels, local(): pl.pallas_call(own_block, out_shape=[jax.ShapeDtypeStruct(shape, f32) for...  1.46 us
  transfers between devices with their start and end apart: 6, of which 2 were waited for; matrix products, arithmetic and copies ran while one was open for 0% of the time, Pallas kernels for 4%

profile of v16, /device:TPU:1, one launch (start us, length us, event | category | flops | bytes accessed | tf_op | source)
XLA Modules:
  0.0 66.8 jit_solution(10871845593435510580)
XLA Ops:
  0.6 0.8 %shard_map.60 = (f32[4,2,8,128]{3,2,1,0:T(8,128)S(1)}, f32[4,2,8,128]{3,2,1,0:T(8,128)S(1)}) custom-call(f32[3,8,8,128]{3,2,1,0:T(8,128)} %force_ref.1, f32[8,8,128]{2,1,0:T(8,128)} %visc_ref.1), custom_call_target="tpu_custom_call" | custom-call | tf_op jit(solution)/shard_map/pallas_call | solution.py:504
  1.5 0.7 collective-permute-start
  2.1 6.6 %collective-permute-start.1 = (f32[4,2,8,128]{3,2,1,0:T(8,128)S(1)}, f32[4,2,8,128]{3,2,1,0:T(8,128)S(1)}, u32[]{:S(2)}, u32[]{:S(2)}) collective-permute-start(f32[4,2,8,128]{3,2,1,0:T(8,128)S(1)} %get-tuple-element.25), channel_id=1, source_target_pairs={{0,1},{1,0},{2,3},{3,2},{4,5},{5,4},{6,7},{7,6},{8,9},{9,8},{10,11... | collective-permute-start | bytes 98312 | tf_op jit(solution)/shard_map/ppermute | solution.py:497
  8.7 1.5 %shard_map.59 = (f32[4,8,8,128]{3,2,1,0:T(8,128)S(1)}, f32[2,8,128]{2,1,0:T(8,128)S(1)}, f32[2,8,128]{2,1,0:T(8,128)S(1)}, f32[64,256]{1,0:T(8,128)S(1)}, f32[64,256]{1,0:T(8,128)S(1)}) custom-call(f32[3,8,8,128]{3,2,1,0:T(8,128)} %force_ref.1, f32[8,8,128]{2,1,0:T(8,128)} %visc_ref.1, f32[64,1024]{1,0:T(8,128)} %topo_hbm.1, bf16[64,1024]{1,0:T(8,128)(2,1)} %kappa_hbm.1), custom_call_target="tpu_custom_call" | custom-call | flops 20480000 | bytes 262144 | tf_op jit(solution)/shard_map/pallas_call | solution.py:513
  10.2 0.0 collective-permute-done.odd_ref
  10.2 0.0 collective-permute-done.1.even_ref
  10.2 0.1 shard_map.61
  10.3 3.1 %collective-permute-start.2 = (f32[2,8,128]{2,1,0:T(8,128)S(1)}, f32[2,8,128]{2,1,0:T(8,128)S(1)}, u32[]{:S(2)}, u32[]{:S(2)}) collective-permute-start(f32[2,8,128]{2,1,0:T(8,128)S(1)} %get-tuple-element.31.own_even), channel_id=1, source_target_pairs={{0,8},{8,0},{16,24},{24,16},{32,40},{40,32},{48,56},{56,48},{64,72... | collective-permute-start | bytes 24584 | tf_op jit(solution)/shard_map/ppermute | solution.py:495
  13.4 0.7 collective-permute-start.3
  14.1 0.1 shard_map.62
  14.2 0.5 collective-permute-done.2.even_ref
  14.7 0.0 collective-permute-done.3.odd_ref
  14.7 0.1 shard_map.63
  14.8 6.7 %collective-permute-start.4 = (f32[136,128]{1,0:T(8,128)S(1)}, f32[136,128]{1,0:T(8,128)S(1)}, u32[]{:S(2)}, u32[]{:S(2)}) collective-permute-start(f32[136,128]{1,0:T(8,128)S(1)} %get-tuple-element.36), channel_id=1, source_target_pairs={{128,256},{256,128},{129,257},{257,129},{130,258},{258,130},{131,2... | collective-permute-start | bytes 208904 | tf_op jit(solution)/shard_map/ppermute | solution.py:497
  21.5 1.9 %collective-permute-start.5 = (f32[136,128]{1,0:T(8,128)S(1)}, f32[136,128]{1,0:T(8,128)S(1)}, u32[]{:S(2)}, u32[]{:S(2)}) collective-permute-start(f32[136,128]{1,0:T(8,128)S(1)} %get-tuple-element.37), channel_id=1, source_target_pairs={{0,128},{128,0},{256,384},{384,256},{1,129},{129,1},{257,385},{385... | collective-permute-start | bytes 208904 | tf_op jit(solution)/shard_map/ppermute | solution.py:497
  23.4 0.9 %shard_map.64.inner_ref = f32[48,128]{1,0:T(8,128)S(1)} custom-call(f32[64,256]{1,0:T(8,128)S(1)} %get-tuple-element.38.height_ref, f32[64,256]{1,0:T(8,128)S(1)} %get-tuple-element.39.conduct_ref), custom_call_target="tpu_custom_call" | custom-call | flops 20480000 | bytes 262144 | tf_op jit(solution)/shard_map/pallas_call | solution.py:29
  24.3 0.0 collective-permute-done.4.odd_ref
  24.4 0.3 collective-permute-done.5.even_ref
  24.6 1.3 %shard_map.65 = (f32[3,8,8,128]{3,2,1,0:T(8,128)S(1)}, f32[64,128]{1,0:T(8,128)S(1)}, f32[2,8,128]{2,1,0:T(8,128)S(1)}, f32[64,128]{1,0:T(8,128)S(1)}) custom-call(f32[48,8,128]{2,1,0:T(8,128)S(1)} %get-tuple-element.28.planes_ref, f32[96,128]{1,0:T(8,128)S(1)} %get-tuple-element.29.low_ref, f32[96,128]{1,0:T(8,128)S(1)} %get-tuple-element.30.high_ref, ...), custom_call_target="tpu_custom_call" | custom-call | flops 20480000 | bytes 262144 | tf_op jit(solution)/shard_map/pallas_call | solution.py:29
  25.9 27.3 %all_to_all.10 = f32[64,1,128]{2,1,0:T(1,128)S(1)} all-to-all(f32[64,1,128]{2,1,0:T(1,128)S(1)} %bitcast.4), channel_id=1, replica_groups=mesh['gx'=4,'gy'=16,'gz'=8] {'gx','gy'}, dimensions={0} | all-to-all | bytes 65536 | tf_op jit(solution)/shard_map/all_to_all | solution.py:546
  53.2 0.1 shard_map.66
  53.3 12.7 %all_to_all.11.parts_ref = f32[8,4,128]{2,1,0:T(4,128)S(1)} all-to-all(f32[8,4,128]{2,1,0:T(4,128)S(1)} %shard_map.66), channel_id=1, replica_groups=mesh['gx'=4,'gy'=16,'gz'=8] {'gz'}, dimensions={0} | all-to-all | bytes 32768 | tf_op jit(solution)/shard_map/all_to_all | solution.py:548
  66.0 0.9 %shard_map.67 = (f32[3,8,8,128]{3,2,1,0:T(8,128)}, f32[64,128]{1,0:T(8,128)}) custom-call(f32[8,4,128]{2,1,0:T(4,128)S(1)} %all_to_all.11.parts_ref, f32[48,8,128]{2,1,0:T(8,128)S(1)} %get-tuple-element.28.planes_ref, f32[3,8,8,128]{3,2,1,0:T(8,128)S(1)} %get-tuple-element.42.image_ref, f32[64,128]{1,0:T(8,128)S(1)} %get-tuple-element.43.height_ref), custom_call_target="tpu_custom_call" | custom-call | tf_op jit(solution)/shard_map/pallas_call | solution.py:550
Async XLA Ops:
  1.5 8.7 %collective-permute-start = (f32[4,2,8,128]{3,2,1,0:T(8,128)S(1)}, f32[4,2,8,128]{3,2,1,0:T(8,128)S(1)}, u32[]{:S(2)}, u32[]{:S(2)}) collective-permute-start(f32[4,2,8,128]{3,2,1,0:T(8,128)S(1)} %get-tuple-element.24), channel_id=1, source_target_pairs={{1,2},{2,1},{3,4},{4,3},{5,6},{6,5},{9,10},{10,9},{11,12},{12,11},... | collective-permute-start | bytes 98312 | tf_op jit(solution)/shard_map/ppermute | solution.py:497
  2.1 8.1 %collective-permute-start.1 = (f32[4,2,8,128]{3,2,1,0:T(8,128)S(1)}, f32[4,2,8,128]{3,2,1,0:T(8,128)S(1)}, u32[]{:S(2)}, u32[]{:S(2)}) collective-permute-start(f32[4,2,8,128]{3,2,1,0:T(8,128)S(1)} %get-tuple-element.25), channel_id=1, source_target_pairs={{0,1},{1,0},{2,3},{3,2},{4,5},{5,4},{6,7},{7,6},{8,9},{9,8},{10,11... | collective-permute-start | bytes 98312 | tf_op jit(solution)/shard_map/ppermute | solution.py:497
  10.3 4.4 %collective-permute-start.2 = (f32[2,8,128]{2,1,0:T(8,128)S(1)}, f32[2,8,128]{2,1,0:T(8,128)S(1)}, u32[]{:S(2)}, u32[]{:S(2)}) collective-permute-start(f32[2,8,128]{2,1,0:T(8,128)S(1)} %get-tuple-element.31.own_even), channel_id=1, source_target_pairs={{0,8},{8,0},{16,24},{24,16},{32,40},{40,32},{48,56},{56,48},{64,72... | collective-permute-start | bytes 24584 | tf_op jit(solution)/shard_map/ppermute | solution.py:495
  13.4 1.3 %collective-permute-start.3 = (f32[2,8,128]{2,1,0:T(8,128)S(1)}, f32[2,8,128]{2,1,0:T(8,128)S(1)}, u32[]{:S(2)}, u32[]{:S(2)}) collective-permute-start(f32[2,8,128]{2,1,0:T(8,128)S(1)} %get-tuple-element.32.own_odd), channel_id=1, source_target_pairs={{8,16},{16,8},{24,32},{32,24},{40,48},{48,40},{56,64},{64,56},{72,... | collective-permute-start | bytes 24584 | tf_op jit(solution)/shard_map/ppermute | solution.py:496
  14.8 9.5 %collective-permute-start.4 = (f32[136,128]{1,0:T(8,128)S(1)}, f32[136,128]{1,0:T(8,128)S(1)}, u32[]{:S(2)}, u32[]{:S(2)}) collective-permute-start(f32[136,128]{1,0:T(8,128)S(1)} %get-tuple-element.36), channel_id=1, source_target_pairs={{128,256},{256,128},{129,257},{257,129},{130,258},{258,130},{131,2... | collective-permute-start | bytes 208904 | tf_op jit(solution)/shard_map/ppermute | solution.py:497
  21.5 3.2 %collective-permute-start.5 = (f32[136,128]{1,0:T(8,128)S(1)}, f32[136,128]{1,0:T(8,128)S(1)}, u32[]{:S(2)}, u32[]{:S(2)}) collective-permute-start(f32[136,128]{1,0:T(8,128)S(1)} %get-tuple-element.37), channel_id=1, source_target_pairs={{0,128},{128,0},{256,384},{384,256},{1,129},{129,1},{257,385},{385... | collective-permute-start | bytes 208904 | tf_op jit(solution)/shard_map/ppermute | solution.py:497
